TPU v7x, 32 devices: a whole 2x2x4 slice. The times are simulated.
32 devices in a mesh: ctx: 16 (over z, y, core), wsh: 2 (over x).
Axes of the slice: x: 2, y: 2, z: 4, core: 2. Of those that a mesh axis runs over, the one named last changes fastest.
Arguments:
- tokens: bfloat16 [2, 2, 1024, 1024], P('wsh', None, 'ctx'), may hold values from -6 to 6
- w_query: bfloat16 [1024, 1024], P('wsh'), may hold values from -0.75 to 0.75
- w_key: bfloat16 [1024, 512], P('wsh'), may hold values from -0.75 to 0.75
- w_value: bfloat16 [1024, 512], P('wsh'), may hold values from -0.375 to 0.375
- w_output: bfloat16 [1024, 1024], P('wsh'), may hold values from -1.5 to 1.5
- attn_gain: bfloat16 [1024], P('wsh'), may hold values from 0.099609375 to 1.8984375
- w_router: bfloat16 [1024, 16], P('wsh'), may hold values from -0.09375 to 0.09375
- expert_in: bfloat16 [16, 1024, 2, 512], P(None, None, None, 'wsh'), may hold values from -0.375 to 0.375
- expert_out: bfloat16 [16, 1024, 512], P(None, None, 'wsh'), may hold values from -0.5 to 0.5
- moe_gain: bfloat16 [1024], P('wsh'), may hold values from 0.099609375 to 1.8984375
- segments: int32 [2, 2048], P('wsh'), may hold values from 0 to 2, as said below
- routes: int32 [2, 2, 1024, 8], P('wsh', None, 'ctx'), may hold values from 0 to 15, all different within a row
- priority: int32 [2, 2, 1024, 8], P('wsh', None, 'ctx'), may hold values from 0 to 65535
- cotangent: bfloat16 [2, 2, 1024, 1024], P('wsh', None, 'ctx'), may hold values from -6 to 6
Outputs:
- output: bfloat16 [2, 2, 1024, 1024], P('wsh', None, 'ctx')
- grad_tokens: float32 [2, 2, 1024, 1024], P('wsh', None, 'ctx')
- grad_w_query: float32 [1024, 1024], P(('ctx', 'wsh'))
- grad_w_key: float32 [1024, 512], P(('ctx', 'wsh'))
- grad_w_value: float32 [1024, 512], P(('ctx', 'wsh'))
- grad_w_output: float32 [1024, 1024], P(('ctx', 'wsh'))
- grad_attn_gain: float32 [1024], P(('ctx', 'wsh'))
- grad_w_router: float32 [1024, 16], P(('ctx', 'wsh'))
- grad_expert_in: float32 [16, 1024, 2, 512], P(None, ('ctx', 'wsh'))
- grad_expert_out: float32 [16, 1024, 512], P(None, ('ctx', 'wsh'))
- grad_moe_gain: float32 [1024], P(('ctx', 'wsh'))
Inputs may be any that keep to these rules, and one draw needn't show every extreme that they name: `segments`: each row numbers one sequence's 3 documents: ids start at 0 and rise by one at each new document; every document holds 102 to 1024 tokens, and one or more hold exactly 1024. `routes`: each token names 8 different experts.
All inputs are finite; a program needn't handle non-finite values.
Results may differ from a plain program's by a relative error of at most 0.02.
Values may be sent and summed in bfloat16 or wider, within the bound.
A program may use at most 320 MiB of HBM per device.

v0:
```python
import math

import jax
import jax.numpy as jnp
from jax import lax
from jax.sharding import PartitionSpec as P

D = 1024
HEADS = 16
KV_HEADS = 8
HEAD_DIM = 64
TOPK = 8
EXPERTS = 16
CAP = 80


RES_MULT = 0.22
ATT_MULT = 0.015625
EPS = 1e-06
THETA = 10000.0


def rms_scale(values):
    return lax.rsqrt(jnp.mean(values * values, axis=-1, keepdims=True) + EPS)


def rotate(values, position, sign):
    half_dim = values.shape[-1] // 2
    frequency = jnp.exp(
        -jnp.log(jnp.float32(THETA))
        * jnp.arange(half_dim, dtype=jnp.float32)
        * (2.0 / values.shape[-1])
    )
    angles = position.astype(jnp.float32)[:, None] * frequency[None, :]
    cosine = jnp.cos(angles)[:, None, :]
    sine_part = sign * jnp.sin(angles)[:, None, :]
    lower_part = values[..., :half_dim]
    upper_part = values[..., half_dim:]
    return jnp.concatenate(
        [
            lower_part * cosine - upper_part * sine_part,
            upper_part * cosine + lower_part * sine_part,
        ],
        axis=-1,
    )


def seq_position(row_ids, block_rows, ctx_count, half_ids):
    return jnp.where(
        half_ids == 0,
        row_ids,
        (2 * ctx_count - 1 - row_ids // block_rows) * block_rows + row_ids % block_rows,
    )


def span_for(row_count):
    return math.gcd(row_count, 1024)


def keep_state(state):
    return state


def body(
    tokens,
    w_query,
    w_key,
    w_value,
    w_output,
    attn_gain,
    w_router,
    expert_in,
    expert_out,
    moe_gain,
    segments,
    routes,
    priority,
    cotangent,
):
    ctx_count = lax.axis_size("ctx")
    ctx_index = lax.axis_index("ctx")
    block_rows = tokens.shape[2]
    half_rows = block_rows * ctx_count
    tok_count = 2 * block_rows
    group_size = HEADS // KV_HEADS
    kv_width = KV_HEADS * HEAD_DIM
    slot_count = EXPERTS * CAP
    f32 = jnp.float32
    bf16 = jnp.bfloat16
    query_w, key_w, value_w, output_w, gain_one, router_w, gain_two = (
        lax.all_gather(w_query, "wsh", axis=0, tiled=True),
        lax.all_gather(w_key, "wsh", axis=0, tiled=True),
        lax.all_gather(w_value, "wsh", axis=0, tiled=True),
        lax.all_gather(w_output, "wsh", axis=0, tiled=True),
        lax.all_gather(attn_gain, "wsh", axis=0, tiled=True),
        lax.all_gather(w_router, "wsh", axis=0, tiled=True),
        lax.all_gather(moe_gain, "wsh", axis=0, tiled=True),
    )
    token_rows = tokens.reshape(tok_count, D).astype(f32)
    scale_one = rms_scale(token_rows)
    normed_one = token_rows * scale_one
    gain_one_f = gain_one.astype(f32)
    hidden_one = (normed_one * gain_one_f).astype(bf16)
    query_lin = jnp.dot(hidden_one, query_w, preferred_element_type=f32)
    key_lin = jnp.dot(hidden_one, key_w, preferred_element_type=f32)
    value_lin = jnp.dot(hidden_one, value_w, preferred_element_type=f32)
    half_ids = jnp.arange(2, dtype=jnp.int32)[:, None]
    local_rows = ctx_index * block_rows + jnp.arange(block_rows, dtype=jnp.int32)
    query_pos = seq_position(local_rows[None, :], block_rows, ctx_count, half_ids)
    segment_ids = segments[0]
    query_seg = segment_ids[query_pos]
    flat_pos = query_pos.reshape(tok_count)
    rot_query = rotate(query_lin.reshape(tok_count, HEADS, HEAD_DIM), flat_pos, 1.0).astype(bf16)
    rot_key = rotate(key_lin.reshape(tok_count, KV_HEADS, HEAD_DIM), flat_pos, 1.0).astype(bf16)
    queries = rot_query.reshape(2, block_rows, KV_HEADS, group_size, HEAD_DIM).transpose(
        0, 2, 3, 1, 4
    )
    key_shard = rot_key.reshape(2, block_rows, kv_width)
    value_shard = value_lin.astype(bf16).reshape(2, block_rows, kv_width)

    def score_mask(half_side, key_pos, key_seg):
        return (key_seg[None, :] == query_seg[half_side][:, None]) & (
            key_pos[None, :] <= query_pos[half_side][:, None]
        )

    def needed(half_side, key_pos):
        return jnp.min(key_pos) <= jnp.max(query_pos[half_side])

    def forward_step(state_pair, block_in):
        numerator, totals = state_pair
        key_blk, value_blk, key_pos, key_seg = block_in
        new_numer = []
        new_totals = []
        for half_side in range(2):
            allowed = score_mask(half_side, key_pos, key_seg)

            def forward_compute(state):
                part_numer, part_total = state
                scores = jnp.einsum(
                    "grqd,kgd->grqk", queries[half_side], key_blk, preferred_element_type=f32
                )
                exp_values = jnp.where(allowed[None, None], jnp.exp(ATT_MULT * scores), 0.0)
                part_total = part_total + jnp.sum(exp_values, axis=-1)
                part_numer = part_numer + jnp.einsum(
                    "grqk,kgd->grqd", exp_values.astype(bf16), value_blk, preferred_element_type=f32
                )
                return (part_numer, part_total)

            part_numer, part_total = lax.cond(
                needed(half_side, key_pos),
                forward_compute,
                keep_state,
                (numerator[half_side], totals[half_side]),
            )
            new_numer.append(part_numer)
            new_totals.append(part_total)
        return ((jnp.stack(new_numer), jnp.stack(new_totals)), None)

    start_state = (
        jnp.zeros((2, KV_HEADS, group_size, block_rows, HEAD_DIM), f32),
        jnp.zeros((2, KV_HEADS, group_size, block_rows), f32),
    )
    state_pair = start_state
    key_part = lax.all_gather(key_shard, "ctx", axis=1, tiled=True)
    value_part = lax.all_gather(value_shard, "ctx", axis=1, tiled=True)
    row_count = key_part.shape[1]
    key_span = span_for(row_count)
    block_count = 2 * row_count // key_span
    row_ids = jnp.arange(row_count, dtype=jnp.int32)
    key_pos = seq_position(row_ids[None, :], block_rows, ctx_count, half_ids)
    key_seg = segment_ids[key_pos]
    blocks_in = (
        key_part.reshape(block_count, key_span, KV_HEADS, HEAD_DIM),
        value_part.reshape(block_count, key_span, KV_HEADS, HEAD_DIM),
        key_pos.reshape(block_count, key_span),
        key_seg.reshape(block_count, key_span),
    )
    state_pair, unused = lax.scan(forward_step, state_pair, blocks_in)
    numerator, totals = state_pair
    attn_raw = numerator / totals[..., None]
    mixed = attn_raw.transpose(0, 3, 1, 2, 4).reshape(tok_count, HEADS * HEAD_DIM).astype(bf16)
    attn_out = jnp.dot(mixed, output_w, preferred_element_type=f32)
    first_sum = token_rows + RES_MULT * attn_out
    scale_two = rms_scale(first_sum)
    normed_two = first_sum * scale_two
    gain_two_f = gain_two.astype(f32)
    hidden_two = (normed_two * gain_two_f).astype(bf16)
    logits = jnp.dot(hidden_two, router_w, preferred_element_type=f32)
    route_rows = routes.reshape(tok_count, TOPK)
    onehot = (route_rows[:, :, None] == jnp.arange(EXPERTS, dtype=jnp.int32)[None, None, :]).astype(
        f32
    )
    picked = jnp.sum(onehot * logits[:, None, :], axis=-1)
    gate_prob = jax.nn.softmax(picked, axis=-1)
    expert_ids = route_rows.reshape(-1)
    prio_flat = priority.reshape(-1)
    order_ids = jnp.arange(expert_ids.shape[0], dtype=jnp.int32)
    same_expert = expert_ids[None, :] == expert_ids[:, None]
    earlier = (prio_flat[None, :] < prio_flat[:, None]) | (
        prio_flat[None, :] == prio_flat[:, None]
    ) & (order_ids[None, :] < order_ids[:, None])
    rank_in = jnp.sum((same_expert & earlier).astype(jnp.int32), axis=1)
    kept_flat = rank_in < CAP
    slot_ids = expert_ids * CAP + rank_in
    target = jnp.where(kept_flat, slot_ids, slot_count)
    slot_token = jnp.zeros((slot_count,), jnp.int32).at[target].set(order_ids // TOPK, mode="drop")
    slot_filled = jnp.zeros((slot_count,), jnp.int32).at[target].set(1, mode="drop")
    kept_mask = kept_flat.reshape(tok_count, TOPK).astype(f32)
    slot_pick = jnp.where(kept_flat, slot_ids, 0).reshape(tok_count, TOPK)
    weight_kept = gate_prob * kept_mask
    filled_rows = slot_filled[:, None] > 0
    expert_rows = jnp.where(filled_rows, hidden_two[slot_token], jnp.zeros((), bf16)).reshape(
        EXPERTS, CAP, D
    )
    inner_w, outer_w = (
        lax.all_gather(expert_in, "wsh", axis=3, tiled=True),
        lax.all_gather(expert_out, "wsh", axis=2, tiled=True),
    )
    rows_all = expert_rows[None]
    gate_up = jnp.einsum("pecd,edhf->pechf", rows_all, inner_w, preferred_element_type=f32)
    gate_val = gate_up[:, :, :, 0]
    up_val = gate_up[:, :, :, 1]
    sigmoid_val = jax.nn.sigmoid(gate_val)
    silu_val = gate_val * sigmoid_val
    activation = (silu_val * up_val).astype(bf16)
    expert_rows_out = jnp.einsum(
        "ecf,edf->ecd", activation[0], outer_w, preferred_element_type=f32
    ).reshape(slot_count, D)
    chosen_rows = expert_rows_out[slot_pick]
    expert_sum = jnp.sum(weight_kept[:, :, None] * chosen_rows, axis=1)
    result = first_sum + RES_MULT * expert_sum
    output = result.astype(bf16).reshape(tokens.shape)
    cot_rows = cotangent.reshape(tok_count, D).astype(f32)
    expert_grad = RES_MULT * cot_rows
    gate_grad = kept_mask * jnp.sum(expert_grad[:, None, :] * chosen_rows, axis=-1)
    picked_grad = gate_prob * (gate_grad - jnp.sum(gate_prob * gate_grad, axis=-1, keepdims=True))
    logit_grad = jnp.sum(onehot * picked_grad[:, :, None], axis=1).astype(bf16)
    slot_weight = jnp.zeros((slot_count,), f32).at[target].set(weight_kept.reshape(-1), mode="drop")
    rows_grad = (
        (slot_weight[:, None] * expert_grad[slot_token]).astype(bf16).reshape(EXPERTS, CAP, D)
    )
    grad_all = rows_grad[None]
    act_grad = jnp.einsum("pecd,edf->pecf", grad_all, outer_w, preferred_element_type=f32)
    silu_grad = sigmoid_val * (1.0 + gate_val * (1.0 - sigmoid_val))
    gate_up_grad = jnp.stack([act_grad * up_val * silu_grad, act_grad * silu_val], axis=3).astype(
        bf16
    )
    outer_grad = jnp.einsum("pecd,pecf->edf", grad_all, activation, preferred_element_type=f32)
    inner_grad = jnp.einsum("pecd,pechf->edhf", rows_all, gate_up_grad, preferred_element_type=f32)
    input_grad = jnp.einsum(
        "echf,edhf->ecd", gate_up_grad[0], inner_w, preferred_element_type=f32
    ).reshape(slot_count, D)
    inner_sum, outer_sum = (
        lax.psum_scatter(inner_grad, ("ctx", "wsh"), scatter_dimension=1, tiled=True),
        lax.psum_scatter(outer_grad, ("ctx", "wsh"), scatter_dimension=1, tiled=True),
    )
    hidden_grad = (
        jnp.zeros((tok_count, D), f32).at[slot_token].add(jnp.where(filled_rows, input_grad, 0.0))
    )
    hidden_grad = hidden_grad + jnp.einsum(
        "te,de->td", logit_grad, router_w, preferred_element_type=f32
    )
    router_grad = jnp.einsum("td,te->de", hidden_two, logit_grad, preferred_element_type=f32)
    gain_two_grad = jnp.sum(hidden_grad * normed_two, axis=0)
    normed_grad = hidden_grad * gain_two_f
    first_grad = cot_rows + scale_two * (
        normed_grad - normed_two * jnp.mean(normed_grad * normed_two, axis=-1, keepdims=True)
    )
    attn_grad = (RES_MULT * first_grad).astype(bf16)
    output_w_grad = jnp.einsum("tm,td->md", mixed, attn_grad, preferred_element_type=f32)
    mixed_grad = jnp.einsum("td,md->tm", attn_grad, output_w, preferred_element_type=f32).astype(
        bf16
    )
    mixed_grad_f = (
        mixed_grad.reshape(2, block_rows, KV_HEADS, group_size, HEAD_DIM)
        .transpose(0, 2, 3, 1, 4)
        .astype(f32)
    )
    numer_grad = (mixed_grad_f / totals[..., None]).astype(bf16)
    total_grad = -jnp.sum(mixed_grad_f * attn_raw, axis=-1) / totals
    key_all, value_all = (
        lax.all_gather(key_shard, "ctx", axis=1, tiled=True),
        lax.all_gather(value_shard, "ctx", axis=1, tiled=True),
    )

    def backward_step(grad_query, block_in):
        key_blk, value_blk, key_pos, key_seg = block_in
        span_rows = key_blk.shape[0]
        key_acc = jnp.zeros((span_rows, KV_HEADS, HEAD_DIM), f32)
        value_acc = jnp.zeros((span_rows, KV_HEADS, HEAD_DIM), f32)
        new_query = []
        for half_side in range(2):
            allowed = score_mask(half_side, key_pos, key_seg)

            def backward_compute(state):
                part_query, part_key, part_value = state
                scores = jnp.einsum(
                    "grqd,kgd->grqk", queries[half_side], key_blk, preferred_element_type=f32
                )
                exp_values = jnp.where(allowed[None, None], jnp.exp(ATT_MULT * scores), 0.0)
                weights_low = exp_values.astype(bf16)
                through = jnp.einsum(
                    "grqd,kgd->grqk", numer_grad[half_side], value_blk, preferred_element_type=f32
                )
                score_grad = (
                    ATT_MULT * exp_values * (through + total_grad[half_side][..., None])
                ).astype(bf16)
                part_query = part_query + jnp.einsum(
                    "grqk,kgd->grqd", score_grad, key_blk, preferred_element_type=f32
                )
                part_key = part_key + jnp.einsum(
                    "grqk,grqd->kgd", score_grad, queries[half_side], preferred_element_type=f32
                )
                part_value = part_value + jnp.einsum(
                    "grqk,grqd->kgd", weights_low, numer_grad[half_side], preferred_element_type=f32
                )
                return (part_query, part_key, part_value)

            part_query, key_acc, value_acc = lax.cond(
                needed(half_side, key_pos),
                backward_compute,
                keep_state,
                (grad_query[half_side], key_acc, value_acc),
            )
            new_query.append(part_query)
        joined = jnp.concatenate(
            [key_acc.reshape(span_rows, kv_width), value_acc.reshape(span_rows, kv_width)], axis=1
        )
        return (jnp.stack(new_query), joined)

    span_all = span_for(half_rows)
    block_total = 2 * half_rows // span_all
    all_rows = jnp.arange(half_rows, dtype=jnp.int32)
    key_pos_all = seq_position(all_rows[None, :], block_rows, ctx_count, half_ids)
    blocks_all = (
        key_all.reshape(block_total, span_all, KV_HEADS, HEAD_DIM),
        value_all.reshape(block_total, span_all, KV_HEADS, HEAD_DIM),
        key_pos_all.reshape(block_total, span_all),
        segment_ids[key_pos_all].reshape(block_total, span_all),
    )
    query_grad, kv_terms = lax.scan(backward_step, jnp.zeros_like(numerator), blocks_all)
    kv_terms = kv_terms.reshape(2, half_rows, 2 * kv_width)
    kv_mine = lax.psum_scatter(kv_terms, "ctx", scatter_dimension=1, tiled=True)
    key_grad = (
        rotate(kv_mine[:, :, :kv_width].reshape(tok_count, KV_HEADS, HEAD_DIM), flat_pos, -1.0)
        .astype(bf16)
        .reshape(tok_count, kv_width)
    )
    value_grad = kv_mine[:, :, kv_width:].reshape(tok_count, kv_width).astype(bf16)
    query_rows_grad = query_grad.transpose(0, 3, 1, 2, 4).reshape(tok_count, HEADS, HEAD_DIM)
    query_lin_grad = (
        rotate(query_rows_grad, flat_pos, -1.0).astype(bf16).reshape(tok_count, HEADS * HEAD_DIM)
    )
    query_w_grad = jnp.einsum("td,tm->dm", hidden_one, query_lin_grad, preferred_element_type=f32)
    key_w_grad = jnp.einsum("td,tm->dm", hidden_one, key_grad, preferred_element_type=f32)
    value_w_grad = jnp.einsum("td,tm->dm", hidden_one, value_grad, preferred_element_type=f32)
    hidden_one_grad = jnp.einsum("tm,dm->td", query_lin_grad, query_w, preferred_element_type=f32)
    hidden_one_grad = hidden_one_grad + jnp.einsum(
        "tm,dm->td", key_grad, key_w, preferred_element_type=f32
    )
    hidden_one_grad = hidden_one_grad + jnp.einsum(
        "tm,dm->td", value_grad, value_w, preferred_element_type=f32
    )
    gain_one_grad = jnp.sum(hidden_one_grad * normed_one, axis=0)
    normed_one_grad = hidden_one_grad * gain_one_f
    token_grad = first_grad + scale_one * (
        normed_one_grad
        - normed_one * jnp.mean(normed_one_grad * normed_one, axis=-1, keepdims=True)
    )
    attn_sums = (
        lax.psum_scatter(query_w_grad, ("ctx", "wsh"), scatter_dimension=0, tiled=True),
        lax.psum_scatter(key_w_grad, ("ctx", "wsh"), scatter_dimension=0, tiled=True),
        lax.psum_scatter(value_w_grad, ("ctx", "wsh"), scatter_dimension=0, tiled=True),
        lax.psum_scatter(output_w_grad, ("ctx", "wsh"), scatter_dimension=0, tiled=True),
        lax.psum_scatter(gain_one_grad, ("ctx", "wsh"), scatter_dimension=0, tiled=True),
        lax.psum_scatter(router_grad, ("ctx", "wsh"), scatter_dimension=0, tiled=True),
        lax.psum_scatter(gain_two_grad, ("ctx", "wsh"), scatter_dimension=0, tiled=True),
    )
    return (
        output,
        token_grad.reshape(tokens.shape),
        attn_sums[0],
        attn_sums[1],
        attn_sums[2],
        attn_sums[3],
        attn_sums[4],
        attn_sums[5],
        inner_sum,
        outer_sum,
        attn_sums[6],
    )


def solution(mesh):
    placed = (
        P("wsh", None, "ctx", None),
        P("wsh", None),
        P("wsh", None),
        P("wsh", None),
        P("wsh", None),
        P("wsh"),
        P("wsh", None),
        P(None, None, None, "wsh"),
        P(None, None, "wsh"),
        P("wsh"),
        P("wsh", None),
        P("wsh", None, "ctx", None),
        P("wsh", None, "ctx", None),
        P("wsh", None, "ctx", None),
    )
    return jax.shard_map(
        body,
        mesh=mesh,
        in_specs=placed,
        out_specs=(
            P("wsh", None, "ctx", None),
            P("wsh", None, "ctx", None),
            P(("ctx", "wsh"), None),
            P(("ctx", "wsh"), None),
            P(("ctx", "wsh"), None),
            P(("ctx", "wsh"), None),
            P(("ctx", "wsh")),
            P(("ctx", "wsh"), None),
            P(None, ("ctx", "wsh"), None, None),
            P(None, ("ctx", "wsh"), None),
            P(("ctx", "wsh")),
        ),
        check_vma=False,
    )
```

profile of v0, /device:TPU:0, one launch (start us, length us, event | category | flops | bytes accessed | tf_op | source)
XLA Modules:
  0.0 3889.5 jit_solution(5827979884737225349)
XLA Ops:
  10.2 5.2 all-gather
  18.6 15.1 all-gather.11.cloned.1.call-done
  36.9 19.6 all-gather.15.cloned.1.call-done
  59.4 15.5 copy.185
  76.0 11.8 gather_fusion
  89.2 4.3 all-gather.1
  96.3 4.3 scatter_custom_fusion.1
  100.6 4.3 scatter_custom_fusion
  105.6 5.2 gather_fusion.4
  110.8 4.7 all_gather.43
  116.3 2.9 copy.175
  121.1 14.1 all-gather.13.cloned.1.call-done
  135.3 3.0 copy.173
  138.3 39.9 %all-gather.17.cloned.1.call-done = bf16[2,1024,512]{2,1,0:T(8,128)(2,1)} async-done(((bf16[2,64,512]{2,1,0:T(8,128)(2,1)}), bf16[2,1024,512]{2,1,0:T(8,128)(2,1)}) %all-gather.17.cloned.1.call-update) | async-done | bytes 2097168 | tf_op jit(solution)/shard_map/all_gather | solution.py:165
  178.1 3.9 copy.174
  183.1 43.7 %while.28 = (s32[]{:T(128)}, f32[2,8,2,64,64]{4,3,2,1,0:T(8,128)}, f32[2,8,2,64]{3,2,1,0:T(2,128)S(1)}, s32[2,1024]{1,0:T(2,128)S(1)}, s32[]{:T(128)}, /*index=5...) while((s32[]{:T(128)}, f32[2,8,2,64,64]{4,3,2,1,0:T(8,128)}, ...), condition=%wide.region_11.12_spmd.clone, body=%wide.region_3.11_spmd.clone.sunk | while | flops 550112384 | bytes 32993732 | solution.py:178
  188.4 2.9 dynamic-slice_bitcast_fusion.6
  191.2 6.6 conditional.12
  194.8 3.0 fusion.34
  199.1 6.6 conditional.13
  213.0 2.9 dynamic-slice_bitcast_fusion.6
  215.9 6.9 conditional.12
  219.5 3.3 fusion.34
  232.5 3.1 multiply_reduce_fusion.4
  236.5 5.1 gather_fusion.2
  242.4 5.0 scatter_custom_fusion.2
  247.5 354.1 %all-gather.23.cloned.1.call-done = bf16[16,1024,2,512]{3,1,2,0:T(8,128)(2,1)} async-done(((bf16[16,1024,2,256]{3,1,2,0:T(8,128)(2,1)}), bf16[16,1024,2,512]{3,1,2,0:T(8,128)(2,1)}) %all-gather.23.cloned.1.call-update) | async-done | bytes 33554448 | tf_op jit(solution)/shard_map/all_gather | solution.py:216
  601.6 23.2 fusion.116
  624.8 3.5 fusion.115
  628.3 173.7 %all-gather.25.cloned.1.call-done = bf16[16,1024,512]{2,1,0:T(8,128)(2,1)} async-done(((bf16[16,1024,256]{2,1,0:T(8,128)(2,1)}), bf16[16,1024,512]{2,1,0:T(8,128)(2,1)}) %all-gather.25.cloned.1.call-update) | async-done | bytes 16777232 | tf_op jit(solution)/shard_map/all_gather | solution.py:217
  802.0 13.2 fusion.168
  815.2 9.0 gather_fusion.3
  824.2 4.7 fusion.92
  829.4 13.3 fusion.122
  842.7 18.4 fusion.90
  861.1 5.2 bitcast_select_fusion
  866.3 15.2 scatter_fusion
  889.9 82.1 %while.29 = (s32[]{:T(128)}, f32[2,8,2,64,64]{4,3,2,1,0:T(8,128)S(1)}, f32[2,1024,1024]{2,1,0:T(8,128)}, s32[2,1024]{1,0:T(2,128)S(1)}, s32[]{:T(128)}, /*index=...) while((s32[]{:T(128)}, ...), condition=%wide.region_33.34_spmd.clone, body=%wide.region_27.33_spmd.clone.sunk | while | flops 1363805312 | bytes 107934520 | solution.py:341
  894.4 3.0 dynamic-slice_bitcast_fusion.7
  897.4 8.4 conditional.14
  906.6 10.7 conditional.15
  913.3 4.0 bitcast_add_fusion
  919.6 4.3 maximum_bitcast_fusion.3
  923.9 5.4 copy.249
  929.3 4.9 constant_dynamic-update-slice_fusion.2
  938.8 3.0 dynamic-slice_bitcast_fusion.7
  944.4 10.7 conditional.15
  951.1 4.0 bitcast_add_fusion
  957.4 4.3 maximum_bitcast_fusion.3
  961.7 5.4 copy.249
  967.1 4.9 constant_dynamic-update-slice_fusion.2
  975.1 30.4 fusion.110
  1013.8 63.9 %reduce-scatter.11.cloned.1.call-done = f32[2,64,1024]{2,1,0:T(8,128)} async-done(((f32[2,1024,1024]{2,1,0:T(8,128)}), f32[2,64,1024]{2,1,0:T(8,128)}) %reduce-scatter.11.cloned.1.call-update) | async-done | bytes 524304 | tf_op jit(solution)/shard_map/reduce_scatter | solution.py:343
  1084.3 16.0 fusion.127
  1100.4 3.4 fusion.169
  1103.8 110.5 %reduce-scatter.25.cloned.1.call-done = f32[32,16]{1,0:T(8,128)} async-done(((f32[1024,16]{1,0:T(8,128)}), f32[32,16]{1,0:T(8,128)}) %reduce-scatter.25.cloned.1.call-update) | async-done | bytes 2064
  1217.9 44.0 %all-reduce.2 = (f32[1024]{0:T(1024)S(1)}, f32[1024]{0:T(1024)S(1)}) all-reduce(f32[1024]{0:T(1024)S(1)} %get-tuple-element.652, f32[1024]{0:T(1024)S(1)} %copy-done.58), channel_id=7, replica_groups=mesh['ctx'=16,'wsh'=2] {'ctx','wsh'}, use_global_device_ids=true, to_apply=%region_41.42.clone | all-reduce | flops 2048 | bytes 16384
  1264.0 1352.6 %reduce-scatter.21.cloned.1.call-done = f32[16,32,2,512]{3,1,2,0:T(8,128)} async-done(((f32[16,1024,2,512]{3,1,2,0:T(8,128)}), f32[16,32,2,512]{3,1,2,0:T(8,128)}) %reduce-scatter.21.cloned.1.call-update) | async-done | bytes 2097168 | tf_op jit(solution)/shard_map/reduce_scatter | solution.py:254
  2616.6 4.5 copy.199
  2621.2 142.4 %reduce-scatter.13.cloned.1.call-done = f32[32,1024]{1,0:T(8,128)} async-done(((f32[1024,1024]{1,0:T(8,128)}), f32[32,1024]{1,0:T(8,128)}) %reduce-scatter.13.cloned.1.call-update) | async-done | bytes 131088 | tf_op jit(solution)/shard_map/reduce_scatter | solution.py:371
  2763.5 142.1 %reduce-scatter.19.cloned.1.call-done = f32[32,1024]{1,0:T(8,128)} async-done(((f32[1024,1024]{1,0:T(8,128)}), f32[32,1024]{1,0:T(8,128)}) %reduce-scatter.19.cloned.1.call-update) | async-done | bytes 131088 | tf_op jit(solution)/shard_map/reduce_scatter | solution.py:374
  2905.7 136.5 %reduce-scatter.15.cloned.1.call-done = f32[32,512]{1,0:T(8,128)} async-done(((f32[1024,512]{1,0:T(8,128)}), f32[32,512]{1,0:T(8,128)}) %reduce-scatter.15.cloned.1.call-update) | async-done | bytes 65552 | tf_op jit(solution)/shard_map/reduce_scatter | solution.py:372
  3042.2 135.9 %reduce-scatter.17.cloned.1.call-done = f32[32,512]{1,0:T(8,128)} async-done(((f32[1024,512]{1,0:T(8,128)}), f32[32,512]{1,0:T(8,128)}) %reduce-scatter.17.cloned.1.call-update) | async-done | bytes 65552 | tf_op jit(solution)/shard_map/reduce_scatter | solution.py:373
  3178.1 704.7 %reduce-scatter.23.cloned.1.call-done = f32[16,32,512]{2,1,0:T(8,128)} async-done(((f32[16,1024,512]{2,1,0:T(8,128)}), f32[16,32,512]{2,1,0:T(8,128)}) %reduce-scatter.23.cloned.1.call-update) | async-done | bytes 1048592 | tf_op jit(solution)/shard_map/reduce_scatter | solution.py:255
  (379 shorter events, 122.5 us)
Async XLA Ops:
  7.2 68.7 %copy-start = (s32[1,2048]{1,0:T(1,128)S(1)}, s32[1,2048]{1,0:T(1,128)}, u32[]{:S(2)}) copy-start(s32[1,2048]{1,0:T(1,128)} %param.36) | copy-start | bytes 24580
  7.2 29.5 copy-start.26
  7.2 26.4 all-gather.11.cloned.1.call-start
  7.9 48.6 %all-gather.15.cloned.1.call-start = ((), (), s32[]{:S(2)}) async-start(), calls=%async_computation.10 | async-start | bytes 1572864 | tf_op jit(solution)/shard_map/all_gather | solution.py:93
  8.7 107.6 %all-gather.19.cloned.1.call-start = ((), (), s32[]{:S(2)}) async-start(), calls=%async_computation.12 | async-start | bytes 3145728 | tf_op jit(solution)/shard_map/all_gather | solution.py:91
  9.4 125.9 %all-gather.13.cloned.1.call-start = ((), (), s32[]{:S(2)}) async-start(), calls=%async_computation.9 | async-start | bytes 2228224 | tf_op jit(solution)/shard_map/all_gather | solution.py:164
  15.4 43.9 %copy-start.47 = (f32[2,1,512]{2,1,0:T(1,128)}, f32[2,1,512]{2,1,0:T(1,128)S(1)}, u32[]{:S(2)}) copy-start(f32[2,1,512]{2,1,0:T(1,128)S(1)} %convert_element_type.232) | copy-start | bytes 12292
  17.4 102.4 %copy-start.44 = (f32[128,32]{0,1:T(8,128)}, f32[128,32]{0,1:T(8,128)S(1)}, u32[]{:S(2)}) copy-start(f32[128,32]{0,1:T(8,128)S(1)} %get-tuple-element.768) | copy-start | bytes 49156
  18.6 100.6 %copy-start.28 = (bf16[1,2,64,1024]{3,2,1,0:T(8,128)(2,1)}, bf16[1,2,64,1024]{3,2,1,0:T(8,128)(2,1)S(1)}, u32[]{:S(2)}) copy-start(bf16[1,2,64,1024]{3,2,1,0:T(8,128)(2,1)S(1)} %multiply_convert_fusion.8) | copy-start | bytes 786436
  36.6 141.5 %all-gather.17.cloned.1.call-start = ((), (), s32[]{:S(2)}) async-start(), calls=%async_computation.11 | async-start | bytes 2228224 | tf_op jit(solution)/shard_map/all_gather | solution.py:165
  36.7 38.1 copy-start.63
  58.7 173.8 %all-gather.21.cloned.1.call-start = ((), (), s32[]{:S(2)}) async-start(), calls=%async_computation.13 | async-start | bytes 3145728 | tf_op jit(solution)/shard_map/all_gather | solution.py:94
  59.3 542.3 %all-gather.23.cloned.1.call-start = ((), (), s32[]{:S(2)}) async-start(), calls=%async_computation.14 | async-start | bytes 50331648 | tf_op jit(solution)/shard_map/all_gather | solution.py:216
  74.9 727.1 %all-gather.25.cloned.1.call-start = ((), (), s32[]{:S(2)}) async-start(), calls=%async_computation.15 | async-start | bytes 25165824 | tf_op jit(solution)/shard_map/all_gather | solution.py:217
  75.6 1002.1 %reduce-scatter.11.cloned.1.call-start = ((), (), s32[]{:S(2)}) async-start(), calls=%async_computation.16 | async-start | bytes 8912896 | tf_op jit(solution)/shard_map/reduce_scatter | solution.py:343
  75.9 13.2 copy-start.66
  75.9 17.7 copy-start.60
  75.9 29.6 copy-start.42
  96.3 4.3 copy-start.65
  105.0 496.5 %copy-start.49 = (pred[16,80]{1,0:T(8,128)(4,1)}, pred[16,80]{1,0:T(8,128)(4,1)S(1)}, u32[]{:S(2)}) copy-start(pred[16,80]{1,0:T(8,128)(4,1)S(1)} %broadcast_in_dim.238) | copy-start | bytes 3844
  105.6 5.2 copy-start.59
  199.1 3.7 copy-start.16
  226.9 8.8 copy-start.8
  232.5 9.1 copy-start.37
  235.6 6.0 copy-start.61
  236.5 5.1 copy-start.2
  247.5 581.9 %copy-start.54 = (f32[16,80]{1,0:T(8,128)}, f32[16,80]{1,0:T(8,128)S(1)}, u32[]{:S(2)}) copy-start(f32[16,80]{1,0:T(8,128)S(1)} %mul.550) | copy-start | bytes 15364
  628.3 186.9 %copy-start.24 = (bf16[16,80,512]{2,1,0:T(8,128)(2,1)}, bf16[16,80,512]{2,1,0:T(8,128)(2,1)S(1)}, u32[]{:S(2)}) copy-start(bf16[16,80,512]{2,1,0:T(8,128)(2,1)S(1)} %fusion.115) | copy-start | bytes 3932164
  829.1 13.6 copy-start.52
  842.7 18.4 copy-start.39
  842.7 18.4 copy-start.57
  866.3 15.2 copy-start.34
  866.3 15.2 copy-start.62
  866.3 16.0 copy-start.43
  881.5 5.6 copy-start.9
  884.5 5.4 copy-start.30
  889.9 4.5 copy-start.10
  894.3 3.1 copy-start.6
  912.1 5.2 copy-start.5
  929.3 4.9 copy-start.11
  929.3 4.9 copy-start.18
  934.2 4.5 copy-start.10
  938.6 3.1 copy-start.6
  949.9 5.2 copy-start.5
  967.1 4.9 copy-start.11
  967.1 4.9 copy-start.18
  973.0 241.3 %reduce-scatter.25.cloned.1.call-start = ((), (), s32[]{:S(2)}) async-start(), calls=%async_computation.23 | async-start | bytes 540672
  975.0 1641.6 %reduce-scatter.21.cloned.1.call-start = ((), (), s32[]{:S(2)}) async-start(), calls=%async_computation.21 | async-start | bytes 69206016 | tf_op jit(solution)/shard_map/reduce_scatter | solution.py:254
  1005.6 1758.0 %reduce-scatter.13.cloned.1.call-start = ((), (), s32[]{:S(2)}) async-start(), calls=%async_computation.17 | async-start | bytes 4325376 | tf_op jit(solution)/shard_map/reduce_scatter | solution.py:371
  1010.9 1894.8 %reduce-scatter.19.cloned.1.call-start = ((), (), s32[]{:S(2)}) async-start(), calls=%async_computation.20 | async-start | bytes 4325376 | tf_op jit(solution)/shard_map/reduce_scatter | solution.py:374
  1013.8 2028.4 %reduce-scatter.15.cloned.1.call-start = ((), (), s32[]{:S(2)}) async-start(), calls=%async_computation.18 | async-start | bytes 2162688 | tf_op jit(solution)/shard_map/reduce_scatter | solution.py:372
  1079.6 4.7 copy-start.25
  1079.6 4.7 copy-start.55
  1081.4 2096.7 %reduce-scatter.17.cloned.1.call-start = ((), (), s32[]{:S(2)}) async-start(), calls=%async_computation.19 | async-start | bytes 2162688 | tf_op jit(solution)/shard_map/reduce_scatter | solution.py:373
  1082.4 17.9 copy-start.40
  1084.2 2798.6 %reduce-scatter.23.cloned.1.call-start = ((), (), s32[]{:S(2)}) async-start(), calls=%async_computation.22 | async-start | bytes 34603008 | tf_op jit(solution)/shard_map/reduce_scatter | solution.py:255
  1100.3 115.4 %copy-start.35 = (bf16[1024,512]{1,0:T(8,128)(2,1)S(1)}, bf16[1024,512]{1,0:T(8,128)(2,1)}, u32[]{:S(2)}) copy-start(bf16[1024,512]{1,0:T(8,128)(2,1)} %all-gather.11.cloned.1.call-done) | copy-start | bytes 3145732
  1100.3 116.9 %copy-start.27 = (bf16[1,2,64,1024]{3,2,1,0:T(8,128)(2,1)S(1)}, bf16[1,2,64,1024]{3,2,1,0:T(8,128)(2,1)}, u32[]{:S(2)}) copy-start(bf16[1,2,64,1024]{3,2,1,0:T(8,128)(2,1)} %param.26) | copy-start | bytes 786436
  1100.4 116.9 %copy-start.36 = (bf16[1024,512]{1,0:T(8,128)(2,1)S(1)}, bf16[1024,512]{1,0:T(8,128)(2,1)}, u32[]{:S(2)}) copy-start(bf16[1024,512]{1,0:T(8,128)(2,1)} %all-gather.15.cloned.1.call-done) | copy-start | bytes 3145732
  1100.4 116.9 %copy-start.41 = (bf16[2,64,512]{2,1,0:T(8,128)(2,1)S(1)}, bf16[2,64,512]{2,1,0:T(8,128)(2,1)}, u32[]{:S(2)}) copy-start(bf16[2,64,512]{2,1,0:T(8,128)(2,1)} %copy-done.40) | copy-start | bytes 393220
  1100.4 116.9 %copy-start.48 = (f32[2,1,512]{2,1,0:T(1,128)S(1)}, f32[2,1,512]{2,1,0:T(1,128)}, u32[]{:S(2)}) copy-start(f32[2,1,512]{2,1,0:T(1,128)} %copy-done.47) | copy-start | bytes 12292
  1100.4 116.9 %copy-start.64 = (f32[128]{0:T(128)S(1)}, f32[128]{0:T(128)}, u32[]{:S(2)}) copy-start(f32[128]{0:T(128)} %copy-done.63) | copy-start | bytes 1540
  1100.4 117.5 %copy-start.58 = (f32[1024]{0:T(1024)S(1)}, f32[1024]{0:T(1024)}, u32[]{:S(2)}) copy-start(f32[1024]{0:T(1024)} %get-tuple-element.650) | copy-start | bytes 12292
  1215.7 2667.1 %copy-start.1 = (s32[1,2048]{1,0:T(1,128)S(1)}, s32[1,2048]{1,0:T(1,128)}, u32[]{:S(2)}) copy-start(s32[1,2048]{1,0:T(1,128)} %param.36) | copy-start | bytes 24580
  (31 other events, 57.2 us)
Sparse Core Ops, SparseCore 0:
  9.6 23.9 all-gather.10
  35.2 21.2 all-gather.14
  58.1 33.1 all-gather.18
  93.8 41.4 all-gather.12
  137.9 40.1 all-gather.16
  179.5 31.8 all-gather.20
  213.0 388.5 all-gather.22
  603.1 198.8 all-gather.24
  973.1 104.5 reduce-scatter.10
  1080.4 133.8 reduce-scatter.24
  1216.8 1399.8 reduce-scatter.20
  2619.4 144.0 reduce-scatter.12
  2766.5 139.1 reduce-scatter.18
  2908.5 133.6 reduce-scatter.14
  3044.9 133.1 reduce-scatter.16
  3180.9 701.8 reduce-scatter.22
where the time goes:
time: 3900 us; the launch traced here: 3890 us
  waiting for transfers between devices  3410 us (87%)
  matrix products  182 us (5%)
  local copies, waits for them, and re-layouts  144 us (4%)
  other arithmetic  69.8 us (2%)
  blocking collectives  58.2 us (1%)
    reduce_scatter x1, waiting for transfers between devices, body(): lax.psum_scatter(inner_grad, ('ctx', 'wsh'), scatter_dimension=1, tiled=T...  1350 us
    reduce_scatter x1, waiting for transfers between devices, body(): lax.psum_scatter(outer_grad, ('ctx', 'wsh'), scatter_dimension=1, tiled=T...  705 us
    all_gather x1, waiting for transfers between devices, body(): lax.all_gather(expert_in, 'wsh', axis=3, tiled=True)  354 us
    all_gather x1, waiting for transfers between devices, body(): lax.all_gather(expert_out, 'wsh', axis=2, tiled=True)  174 us
    reduce_scatter x1, waiting for transfers between devices, body(): lax.psum_scatter(query_w_grad, ('ctx', 'wsh'), scatter_dimension=0, tiled...  142 us
    reduce_scatter x1, waiting for transfers between devices, body(): lax.psum_scatter(output_w_grad, ('ctx', 'wsh'), scatter_dimension=0, tile...  142 us
    reduce_scatter x1, waiting for transfers between devices, body(): lax.psum_scatter(key_w_grad, ('ctx', 'wsh'), scatter_dimension=0, tiled=T...  137 us
    reduce_scatter x1, waiting for transfers between devices, body(): lax.psum_scatter(value_w_grad, ('ctx', 'wsh'), scatter_dimension=0, tiled...  136 us
  transfers between devices with their start and end apart: 16, of which 14 were waited for; matrix products, arithmetic and copies ran while one was open for 6% of the time, Pallas kernels for 0%

commit v1 on v0

v1 whole, which is shorter than its diff:
```python
import functools
import math

import jax
import jax.numpy as jnp
from jax import lax
from jax.experimental import pallas as pl
from jax.experimental.pallas import tpu as pltpu
from jax.sharding import PartitionSpec as P

D = 1024
HEADS = 16
KV_HEADS = 8
HEAD_DIM = 64
TOPK = 8
EXPERTS = 16
CAP = 80
PLANE = 8
INNER = 4
OWN = EXPERTS // INNER


RES_MULT = 0.22
ATT_MULT = 0.015625
EPS = 1e-06
THETA = 10000.0

MESH = pl.DeviceIdType.MESH
F32 = jnp.float32
BF16 = jnp.bfloat16
ANY = pl.BlockSpec(memory_space=pl.ANY)
VMEM = pl.BlockSpec(memory_space=pltpu.VMEM)


class Place:
    def __init__(self):
        self.c = lax.axis_index("ctx")
        self.w = lax.axis_index("wsh")
        self.core = self.c % 2
        self.y = (self.c // 2) % 2
        self.inner = self.c % INNER
        self.outer = self.c // INNER
        self.j = self.inner * 2 + self.w
        self.sib = self.c + 1 - 2 * self.core
        self.yn = self.c + 2 - 4 * self.y

    def relative(self, dy, dc, dw):
        y = self.y + dy * (1 - 2 * self.y)
        core = self.core + dc * (1 - 2 * self.core)
        w = self.w + dw * (1 - 2 * self.w)
        ctx = self.outer * INNER + y * 2 + core
        return (ctx, w), (y * 2 + core) * 2 + w


OTHERS = [(a, b, d) for a in range(2) for b in range(2) for d in range(2) if a + b + d]
XY = [(0, 0, 1), (1, 0, 0), (1, 0, 1)]


def meet(devices):
    barrier = pltpu.get_barrier_semaphore()
    for device in devices:
        pl.semaphore_signal(barrier, inc=1, device_id=device, device_id_type=MESH)
    pl.semaphore_wait(barrier, len(devices))


def remote(src, dst, send, recv, device):
    return pltpu.make_async_remote_copy(
        src_ref=src,
        dst_ref=dst,
        send_sem=send,
        recv_sem=recv,
        device_id=device,
        device_id_type=MESH,
    )


def comm_call(kernel, out_shape, in_specs, out_specs, scratch, ident, name, vmem=None):
    return pl.pallas_call(
        kernel,
        out_shape=out_shape,
        in_specs=in_specs,
        out_specs=out_specs,
        scratch_shapes=scratch,
        compiler_params=pltpu.CompilerParams(
            collective_id=ident, has_side_effects=True, vmem_limit_bytes=vmem
        ),
        name=name,
    )


DMA = pltpu.SemaphoreType.DMA


def gather_start(at, pairs, send, recv, local):
    copies = []
    for index, (src, dst) in enumerate(pairs):
        keep = pltpu.make_async_copy(src, dst.at[at.j], local.at[index])
        keep.start()
        sends = []
        for slot, bits in enumerate(XY + [(0, 1, 0)]):
            device, unused = at.relative(*bits)
            copy = remote(src, dst.at[at.j], send.at[index, slot], recv.at[index, slot], device)
            copy.start()
            sends.append(copy)
        copies.append((keep, sends))
    return copies


def gather_finish(at, pairs, copies, send, recv):
    sib, unused = at.relative(0, 1, 0)
    passed = []
    for slot, bits in enumerate(XY):
        unused, j_from = at.relative(*bits)
        for index, (src, dst) in enumerate(pairs):
            copies[index][1][slot].wait_recv()
            copy = remote(
                dst.at[j_from],
                dst.at[j_from],
                send.at[index, 4 + slot],
                recv.at[index, 4 + slot],
                sib,
            )
            copy.start()
            passed.append(copy)
    for keep, sends in copies:
        keep.wait()
        sends[3].wait_recv()
        for copy in sends:
            copy.wait_send()
    for copy in passed:
        copy.wait()


def plane_gather_kernel(count, *refs):
    ins, outs = refs[:count], refs[count : 2 * count]
    send, recv, local = refs[2 * count :]
    at = Place()
    meet([at.relative(*bits)[0] for bits in XY + [(0, 1, 0)]])
    pairs = list(zip(ins, outs))
    copies = gather_start(at, pairs, send, recv, local)
    gather_finish(at, pairs, copies, send, recv)


def plane_gather(arrays, ident, name):
    count = len(arrays)
    return comm_call(
        functools.partial(plane_gather_kernel, count),
        [jax.ShapeDtypeStruct((PLANE,) + a.shape, a.dtype) for a in arrays],
        [ANY] * count,
        [ANY] * count,
        [DMA((count, 7)), DMA((count, 7)), DMA((count,))],
        ident,
        name,
    )(*arrays)


def weights_kernel(
    wq, wk, wv, wo, small, cot, wqkv_o, wo_o, small_o, cot_o, xs, xr, fs, fr, ls, gs, gr, gl
):
    at = Place()
    meet([at.relative(*bits)[0] for bits in XY + [(0, 1, 0)]])
    partner, unused = at.relative(0, 0, 1)
    sib, unused = at.relative(0, 1, 0)
    pieces = [(wq, wqkv_o, 0), (wk, wqkv_o, 1024), (wv, wqkv_o, 1536), (wo, wo_o, 0)]
    locals_, sends, passed = [], [], []
    for index, (src, dst, col) in enumerate(pieces):
        depth, width = src.shape
        half = depth // 2
        row = at.w * depth + at.core * half
        copy = remote(
            src.at[pl.ds(at.core * half, half), :],
            dst.at[pl.ds(row, half), pl.ds(col, width)],
            xs.at[index],
            xr.at[index],
            partner,
        )
        copy.start()
        sends.append(copy)
        keep = pltpu.make_async_copy(
            src, dst.at[pl.ds(at.w * depth, depth), pl.ds(col, width)], ls.at[index]
        )
        keep.start()
        locals_.append(keep)
    last = len(pieces)
    copy = remote(small, small_o.at[at.w], xs.at[last], xr.at[last], partner)
    copy.start()
    sends.append(copy)
    keep = pltpu.make_async_copy(small, small_o.at[at.w], ls.at[last])
    keep.start()
    locals_.append(keep)
    pairs = [(cot, cot_o)]
    copies = gather_start(at, pairs, gs, gr, gl)
    for index, (src, dst, col) in enumerate(pieces):
        depth, width = src.shape
        half = depth // 2
        row = (1 - at.w) * depth + at.core * half
        sends[index].wait_recv()
        piece = dst.at[pl.ds(row, half), pl.ds(col, width)]
        copy = remote(piece, piece, fs.at[index], fr.at[index], sib)
        copy.start()
        passed.append(copy)
    sends[last].wait_recv()
    gather_finish(at, pairs, copies, gs, gr)
    for copy in sends:
        copy.wait_send()
    for copy in passed:
        copy.wait()
    for keep in locals_:
        keep.wait()


def gather_weights(wq, wk, wv, wo, small, cot):
    shape = jax.ShapeDtypeStruct
    return comm_call(
        weights_kernel,
        [
            shape((D, 2048), BF16),
            shape((D, D), BF16),
            shape((2,) + small.shape, BF16),
            shape((PLANE,) + cot.shape, BF16),
        ],
        [ANY] * 6,
        [ANY] * 4,
        [DMA((5,)), DMA((5,)), DMA((4,)), DMA((4,)), DMA((5,)), DMA((1, 7)), DMA((1, 7)), DMA((1,))],
        1,
        "gather_weights",
    )(wq, wk, wv, wo, small, cot)


def kv_gather_kernel(outers, own, full, zs, zr, ys, yr, cs, cr, local):
    at = Place()
    sib, unused = at.relative(0, 1, 0)
    side, unused = at.relative(1, 0, 0)
    other = [lax.rem(at.outer + r, outers) for r in range(outers)]
    back = [lax.rem(at.outer + outers - r, outers) for r in range(outers)]
    far = [(other[r] * INNER + at.inner, at.w) for r in range(1, outers)]
    meet([sib, side] + far)
    keep = pltpu.make_async_copy(own, full.at[:, at.c], local)
    keep.start()
    mine = full.at[:, at.c]
    waits = []
    zs_copies = []
    for r in range(1, outers):
        copy = remote(own, mine, zs.at[r], zr.at[r], far[r - 1])
        copy.start()
        zs_copies.append(copy)
        waits.append(copy)
    y_copies, c_copies = [], []
    for ref, sems, into, device in ((ys, yr, y_copies, side), (cs, cr, c_copies, sib)):
        copy = remote(own, mine, ref.at[0], sems.at[0], device)
        copy.start()
        into.append(copy)
    for r in range(1, outers):
        zs_copies[r - 1].wait_recv()
        block = full.at[:, back[r] * INNER + at.inner]
        for ref, sems, into, device in ((ys, yr, y_copies, side), (cs, cr, c_copies, sib)):
            copy = remote(block, block, ref.at[r], sems.at[r], device)
            copy.start()
            into.append(copy)
    inner_side = at.inner + 2 - 4 * at.y
    for r in range(outers):
        y_copies[r].wait_recv()
        block = full.at[:, back[r] * INNER + inner_side]
        copy = remote(block, block, cs.at[outers + r], cr.at[outers + r], sib)
        copy.start()
        c_copies.append(copy)
    for copy in zs_copies + y_copies:
        copy.wait_send()
    for copy in c_copies:
        copy.wait()
    keep.wait()


def kv_gather(own, ctx_count):
    outers = ctx_count // INNER
    return comm_call(
        functools.partial(kv_gather_kernel, outers),
        jax.ShapeDtypeStruct((2, ctx_count) + own.shape[1:], own.dtype),
        [ANY],
        ANY,
        [DMA((outers,))] * 4 + [DMA((2 * outers,))] * 2 + [DMA],
        2,
        "kv_gather",
    )(own)


def kv_reduce_kernel(outers, part, out, half_in, half_sum, y_in, y_sum, z_in, ss, sr, ys, yr, zs, zr):
    at = Place()
    sib, unused = at.relative(0, 1, 0)
    side, unused = at.relative(1, 0, 0)
    other = [lax.rem(at.outer + r, outers) for r in range(outers)]
    far = [(other[r] * INNER + at.inner, at.w) for r in range(1, outers)]
    meet([sib, side] + far)
    width = part.shape[-1] // 2
    first = []
    for k in range(2):
        cols = pl.ds(k * width, width)
        copy = remote(
            part.at[:, :, :, 1 - at.core, :, cols], half_in.at[:, :, :, :, cols], ss.at[k], sr.at[k], sib
        )
        copy.start()
        first.append(copy)
    second = []
    for k in range(2):
        cols = pl.ds(k * width, width)
        first[k].wait_recv()
        for o in range(outers):
            for y in range(2):
                for h in range(2):
                    total = part[h, o, y, at.core, :, cols].astype(F32) + half_in[
                        h, o, y, :, cols
                    ].astype(F32)
                    half_sum[y, h, o, :, cols] = total.astype(BF16)
        copy = remote(
            half_sum.at[1 - at.y, :, :, :, cols], y_in.at[:, :, :, cols], ys.at[k], yr.at[k], side
        )
        copy.start()
        second.append(copy)
    third = []
    for k in range(2):
        cols = pl.ds(k * width, width)
        second[k].wait_recv()
        for o in range(outers):
            for h in range(2):
                total = half_sum[at.y, h, o, :, cols].astype(F32) + y_in[h, o, :, cols].astype(F32)
                y_sum[o, h, :, cols] = total.astype(BF16)
        for r in range(1, outers):
            copy = remote(
                y_sum.at[other[r], :, :, cols],
                z_in.at[r, :, :, cols],
                zs.at[k, r],
                zr.at[k, r],
                far[r - 1],
            )
            copy.start()
            third.append(copy)
    for copy in third:
        copy.wait_recv()
    total = y_sum[at.outer].astype(F32)
    for r in range(1, outers):
        total = total + z_in[r].astype(F32)
    out[...] = total
    for copy in first + second + third:
        copy.wait_send()


def kv_reduce(part, ctx_count):
    outers = ctx_count // INNER
    rows, width = part.shape[-2:]
    return comm_call(
        functools.partial(kv_reduce_kernel, outers),
        jax.ShapeDtypeStruct((2, rows, width), F32),
        [VMEM],
        VMEM,
        [
            pltpu.VMEM((2, outers, 2, rows, width), BF16),
            pltpu.VMEM((2, 2, outers, rows, width), BF16),
            pltpu.VMEM((2, outers, rows, width), BF16),
            pltpu.VMEM((outers, 2, rows, width), BF16),
            pltpu.VMEM((outers, 2, rows, width), BF16),
            DMA((2,)),
            DMA((2,)),
            DMA((2,)),
            DMA((2,)),
            DMA((2, outers)),
            DMA((2, outers)),
        ],
        3,
        "kv_reduce",
        vmem=60 * 2**20,
    )(part.reshape(2, outers, 2, 2, rows, width))


def plane_reduce_kernel(count, *refs):
    parts, picks = refs[:count], refs[count]
    outs, picks_o = refs[count + 1 : 2 * count + 1], refs[2 * count + 1]
    near, summed, far, ss, sr, xs, xr, ps, pr, pl_sem = refs[2 * count + 2 :]
    at = Place()
    meet([at.relative(*bits)[0] for bits in OTHERS])
    sib, unused = at.relative(0, 1, 0)
    first = []
    for index in range(count):
        copy = remote(
            parts[index].at[:, 1 - at.core], near.at[index], ss.at[index], sr.at[index], sib
        )
        copy.start()
        first.append(copy)
    keep = pltpu.make_async_copy(picks.at[at.j], picks_o.at[at.j], pl_sem)
    keep.start()
    small = []
    for slot, bits in enumerate(OTHERS):
        device, j_to = at.relative(*bits)
        copy = remote(picks.at[j_to], picks_o.at[at.j], ps.at[slot], pr.at[slot], device)
        copy.start()
        small.append(copy)
    second = []
    for index in range(count):
        first[index].wait_recv()
        for y in range(2):
            for w in range(2):
                total = parts[index][y, at.core, w].astype(F32) + near[index, y, w].astype(F32)
                summed[index, y, w] = total.astype(BF16)
        for slot, (dy, dc, dw) in enumerate(XY):
            device, unused = at.relative(dy, dc, dw)
            y = at.y + dy * (1 - 2 * at.y)
            w = at.w + dw * (1 - 2 * at.w)
            copy = remote(
                summed.at[index, y, w], far.at[index, slot], xs.at[index, slot], xr.at[index, slot], device
            )
            copy.start()
            second.append(copy)
    for index in range(count):
        total = parts[index][at.y, at.core, at.w].astype(F32) + near[index, at.y, at.w].astype(F32)
        for slot in range(3):
            second[index * 3 + slot].wait_recv()
            total = total + far[index, slot].astype(F32)
        outs[index][...] = total
    keep.wait()
    for copy in small:
        copy.wait()
    for copy in first + second:
        copy.wait_send()


def plane_reduce(parts, picks, ident, name):
    count = len(parts)
    rows, width = parts[0].shape[-2:]
    shape = jax.ShapeDtypeStruct
    return comm_call(
        functools.partial(plane_reduce_kernel, count),
        [shape((rows, width), F32)] * count + [shape(picks.shape, picks.dtype)],
        [VMEM] * (count + 1),
        [VMEM] * (count + 1),
        [
            pltpu.VMEM((count, 2, 2, rows, width), BF16),
            pltpu.VMEM((count, 2, 2, rows, width), BF16),
            pltpu.VMEM((count, 3, rows, width), BF16),
            DMA((count,)),
            DMA((count,)),
            DMA((count, 3)),
            DMA((count, 3)),
            DMA((7,)),
            DMA((7,)),
            DMA,
        ],
        ident,
        name,
        vmem=60 * 2**20,
    )(*[p.reshape(2, 2, 2, rows, width) for p in parts], picks)


def plane_swap_kernel(src, gather_in, dst, gather_out, ss, sr, local, gs, gr, gl):
    at = Place()
    meet([at.relative(*bits)[0] for bits in OTHERS])
    keep = pltpu.make_async_copy(src.at[at.j], dst.at[at.j], local)
    keep.start()
    copies = []
    for slot, bits in enumerate(OTHERS):
        device, j_to = at.relative(*bits)
        copy = remote(src.at[j_to], dst.at[at.j], ss.at[slot], sr.at[slot], device)
        copy.start()
        copies.append(copy)
    pairs = [(gather_in, gather_out)]
    started = gather_start(at, pairs, gs, gr, gl)
    gather_finish(at, pairs, started, gs, gr)
    for copy in copies:
        copy.wait()
    keep.wait()


def plane_swap(src, gathered, ident, name):
    shape = jax.ShapeDtypeStruct
    return comm_call(
        plane_swap_kernel,
        [shape(src.shape, src.dtype), shape((PLANE,) + gathered.shape, gathered.dtype)],
        [ANY] * 2,
        [ANY] * 2,
        [DMA((7,)), DMA((7,)), DMA, DMA((1, 7)), DMA((1, 7)), DMA((1,))],
        ident,
        name,
    )(src, gathered)


def owners_kernel(devices, count, *refs):
    parts, outs = refs[:count], refs[count : 2 * count]
    send, recv, local = refs[2 * count :]
    at = Place()
    me = at.c * 2 + at.w
    rows = D // devices

    def device_of(r):
        index = lax.rem(me + r, devices)
        return index, (index // 2, lax.rem(index, 2))

    def rows_of(ref, index):
        block = pl.ds(pl.multiple_of(index * rows, rows), rows)
        return ref.at[:, block, :] if len(ref.shape) == 3 else ref.at[block, :]

    barrier = pltpu.get_barrier_semaphore()

    def greet(r, carry):
        unused, device = device_of(r)
        pl.semaphore_signal(barrier, inc=1, device_id=device, device_id_type=MESH)
        return carry

    lax.fori_loop(1, devices, greet, 0)
    pl.semaphore_wait(barrier, devices - 1)

    keeps = []
    for k in range(count):
        keep = pltpu.make_async_copy(rows_of(parts[k], me), outs[k].at[me], local.at[k])
        keep.start()
        keeps.append(keep)

    def copy_of(k, r):
        index, device = device_of(r)
        return remote(rows_of(parts[k], index), outs[k].at[me], send.at[k, r], recv.at[k, r], device)

    def start(r, carry):
        for k in range(count):
            copy_of(k, r).start()
        return carry

    lax.fori_loop(1, devices, start, 0)

    def finish(r, carry):
        for k in range(count):
            copy_of(k, r).wait()
        return carry

    lax.fori_loop(1, devices, finish, 0)
    for keep in keeps:
        keep.wait()


def owners(parts, devices, ident, name):
    count = len(parts)
    rows = D // devices
    shapes = []
    for part in parts:
        lead = part.shape[:-2]
        shapes.append(
            jax.ShapeDtypeStruct((devices,) + lead + (rows, part.shape[-1]), part.dtype)
        )
    return comm_call(
        functools.partial(owners_kernel, devices, count),
        shapes,
        [ANY] * count,
        [ANY] * count,
        [DMA((count, devices)), DMA((count, devices)), DMA((count,))],
        ident,
        name,
    )(*parts)


def rms_scale(values):
    return lax.rsqrt(jnp.mean(values * values, axis=-1, keepdims=True) + EPS)


def rotate(values, position, sign):
    half_dim = values.shape[-1] // 2
    frequency = jnp.exp(
        -jnp.log(jnp.float32(THETA))
        * jnp.arange(half_dim, dtype=jnp.float32)
        * (2.0 / values.shape[-1])
    )
    angles = position.astype(jnp.float32)[:, None] * frequency[None, :]
    cosine = jnp.cos(angles)[:, None, :]
    sine_part = sign * jnp.sin(angles)[:, None, :]
    lower_part = values[..., :half_dim]
    upper_part = values[..., half_dim:]
    return jnp.concatenate(
        [
            lower_part * cosine - upper_part * sine_part,
            upper_part * cosine + lower_part * sine_part,
        ],
        axis=-1,
    )


def seq_position(row_ids, block_rows, ctx_count, half_ids):
    return jnp.where(
        half_ids == 0,
        row_ids,
        (2 * ctx_count - 1 - row_ids // block_rows) * block_rows + row_ids % block_rows,
    )


def span_for(row_count):
    return math.gcd(row_count, 1024)


def keep_state(state):
    return state


def body(
    tokens,
    w_query,
    w_key,
    w_value,
    w_output,
    attn_gain,
    w_router,
    expert_in,
    expert_out,
    moe_gain,
    segments,
    routes,
    priority,
    cotangent,
):
    ctx_count = lax.axis_size("ctx")
    ctx_index = lax.axis_index("ctx")
    devices = ctx_count * 2
    outers = ctx_count // INNER
    owner_rows = D // devices
    block_rows = tokens.shape[2]
    half_rows = block_rows * ctx_count
    tok_count = 2 * block_rows
    plane_rows = PLANE * tok_count
    group_size = HEADS // KV_HEADS
    kv_width = KV_HEADS * HEAD_DIM
    f32 = jnp.float32
    bf16 = jnp.bfloat16
    first_expert = (ctx_index % INNER) * OWN

    small = jnp.concatenate(
        [w_router.T, attn_gain[None], moe_gain[None], jnp.zeros((14, w_router.shape[0]), bf16)]
    )
    cot_own = cotangent.reshape(tok_count, D)
    qkv_w, output_w, small_all, cot_all = gather_weights(
        w_query, w_key, w_value, w_output, small, cot_own
    )
    small_all = small_all.transpose(1, 0, 2).reshape(32, D)
    router_t = small_all[:EXPERTS]
    gain_one_f = small_all[EXPERTS].astype(f32)
    gain_two_f = small_all[EXPERTS + 1].astype(f32)

    token_rows = tokens.reshape(tok_count, D).astype(f32)
    scale_one = rms_scale(token_rows)
    normed_one = token_rows * scale_one
    hidden_one = (normed_one * gain_one_f).astype(bf16)
    qkv_lin = jnp.dot(hidden_one, qkv_w, preferred_element_type=f32)
    half_ids = jnp.arange(2, dtype=jnp.int32)[:, None]
    local_rows = ctx_index * block_rows + jnp.arange(block_rows, dtype=jnp.int32)
    query_pos = seq_position(local_rows[None, :], block_rows, ctx_count, half_ids)
    segment_ids = segments[0]
    query_seg = segment_ids[query_pos]
    flat_pos = query_pos.reshape(tok_count)
    rot_query = rotate(qkv_lin[:, :1024].reshape(tok_count, HEADS, HEAD_DIM), flat_pos, 1.0).astype(
        bf16
    )
    rot_key = rotate(
        qkv_lin[:, 1024:1536].reshape(tok_count, KV_HEADS, HEAD_DIM), flat_pos, 1.0
    ).astype(bf16)
    queries = rot_query.reshape(2, block_rows, KV_HEADS, group_size, HEAD_DIM).transpose(
        0, 2, 3, 1, 4
    )
    kv_own = jnp.concatenate(
        [rot_key.reshape(tok_count, kv_width), qkv_lin[:, 1536:].astype(bf16)], axis=1
    ).reshape(2, block_rows, 2 * kv_width)
    kv_all = kv_gather(kv_own, ctx_count).reshape(2, half_rows, 2 * kv_width)

    def score_mask(half_side, key_pos, key_seg):
        return (key_seg[None, :] == query_seg[half_side][:, None]) & (
            key_pos[None, :] <= query_pos[half_side][:, None]
        )

    def needed(half_side, key_pos):
        return jnp.min(key_pos) <= jnp.max(query_pos[half_side])

    def forward_step(state_pair, block_in):
        numerator, totals = state_pair
        key_blk, value_blk, key_pos, key_seg = block_in
        new_numer = []
        new_totals = []
        for half_side in range(2):
            allowed = score_mask(half_side, key_pos, key_seg)

            def forward_compute(state):
                part_numer, part_total = state
                scores = jnp.einsum(
                    "grqd,kgd->grqk", queries[half_side], key_blk, preferred_element_type=f32
                )
                exp_values = jnp.where(allowed[None, None], jnp.exp(ATT_MULT * scores), 0.0)
                part_total = part_total + jnp.sum(exp_values, axis=-1)
                part_numer = part_numer + jnp.einsum(
                    "grqk,kgd->grqd", exp_values.astype(bf16), value_blk, preferred_element_type=f32
                )
                return (part_numer, part_total)

            part_numer, part_total = lax.cond(
                needed(half_side, key_pos),
                forward_compute,
                keep_state,
                (numerator[half_side], totals[half_side]),
            )
            new_numer.append(part_numer)
            new_totals.append(part_total)
        return ((jnp.stack(new_numer), jnp.stack(new_totals)), None)

    start_state = (
        jnp.zeros((2, KV_HEADS, group_size, block_rows, HEAD_DIM), f32),
        jnp.zeros((2, KV_HEADS, group_size, block_rows), f32),
    )
    span_all = span_for(half_rows)
    block_total = 2 * half_rows // span_all
    all_rows = jnp.arange(half_rows, dtype=jnp.int32)
    key_pos_all = seq_position(all_rows[None, :], block_rows, ctx_count, half_ids)
    blocks_all = (
        kv_all[..., :kv_width].reshape(block_total, span_all, KV_HEADS, HEAD_DIM),
        kv_all[..., kv_width:].reshape(block_total, span_all, KV_HEADS, HEAD_DIM),
        key_pos_all.reshape(block_total, span_all),
        segment_ids[key_pos_all].reshape(block_total, span_all),
    )
    state_pair, unused = lax.scan(forward_step, start_state, blocks_all)
    numerator, totals = state_pair
    attn_raw = numerator / totals[..., None]
    mixed = attn_raw.transpose(0, 3, 1, 2, 4).reshape(tok_count, HEADS * HEAD_DIM).astype(bf16)
    attn_out = jnp.dot(mixed, output_w, preferred_element_type=f32)
    first_sum = token_rows + RES_MULT * attn_out
    scale_two = rms_scale(first_sum)
    normed_two = first_sum * scale_two
    hidden_two = (normed_two * gain_two_f).astype(bf16)
    logits = jnp.einsum("td,ed->te", hidden_two, router_t, preferred_element_type=f32)

    route_rows = routes.reshape(tok_count, TOPK)
    onehot = route_rows[:, :, None] == jnp.arange(EXPERTS, dtype=jnp.int32)[None, None, :]
    routed = jnp.any(onehot, axis=1)
    prio = jnp.sum(jnp.where(onehot, priority.reshape(tok_count, TOPK)[:, :, None], 0), axis=1)
    prio = jnp.where(routed, prio, 1 << 20)
    top = jnp.max(jnp.where(routed, logits, -jnp.inf), axis=-1, keepdims=True)
    weight = jnp.where(routed, jnp.exp(logits - top), 0.0)
    gate = weight / jnp.sum(weight, axis=-1, keepdims=True)
    order = jnp.arange(tok_count, dtype=jnp.int32)
    ahead = (prio[None, :, :] < prio[:, None, :]) | (
        (prio[None, :, :] == prio[:, None, :]) & (order[None, :, None] < order[:, None, None])
    )
    rank = jnp.sum(ahead.astype(jnp.int32), axis=1)
    kept = routed & (rank < CAP)
    kept_f = kept.astype(f32)
    gate_kept = gate * kept_f

    hidden_all, gates_all = plane_gather([hidden_two, gate_kept.T], 4, "gather_hidden")
    hidden_all = hidden_all.reshape(plane_rows, D)
    cot_rows_all = cot_all.reshape(plane_rows, D)
    own_gates = lax.dynamic_slice_in_dim(gates_all, first_expert, OWN, axis=1)
    own_gates = own_gates.transpose(1, 0, 2).reshape(OWN, plane_rows)

    inner_w = lax.dynamic_slice_in_dim(expert_in, first_expert, OWN, axis=0)
    outer_w = lax.dynamic_slice_in_dim(expert_out, first_expert, OWN, axis=0)
    hidden_units = outer_w.shape[-1]
    inner_w = inner_w.reshape(OWN, D, 2 * hidden_units)
    gate_up = jnp.einsum("td,edf->etf", hidden_all, inner_w, preferred_element_type=f32)
    gate_val = gate_up[:, :, :hidden_units]
    up_val = gate_up[:, :, hidden_units:]
    sigmoid_val = jax.nn.sigmoid(gate_val)
    silu_val = gate_val * sigmoid_val
    act = silu_val * up_val
    act_kept = (own_gates[:, :, None] * act).astype(bf16)
    moe_part = jnp.einsum("etf,edf->td", act_kept, outer_w, preferred_element_type=f32).astype(bf16)
    act_grad = RES_MULT * jnp.einsum("td,edf->etf", cot_rows_all, outer_w, preferred_element_type=f32)
    pick_part = jnp.sum(act * act_grad, axis=-1)
    act_grad = own_gates[:, :, None] * act_grad
    silu_grad = sigmoid_val * (1.0 + gate_val * (1.0 - sigmoid_val))
    gate_up_grad = jnp.concatenate(
        [act_grad * up_val * silu_grad, act_grad * silu_val], axis=-1
    ).astype(bf16)
    hidden_part = jnp.einsum("etf,edf->td", gate_up_grad, inner_w, preferred_element_type=f32).astype(
        bf16
    )
    inner_grad = jnp.einsum("td,etf->edf", hidden_all, gate_up_grad, preferred_element_type=f32).astype(
        bf16
    )
    outer_grad = (
        RES_MULT * jnp.einsum("td,etf->edf", cot_rows_all, act_kept, preferred_element_type=f32)
    ).astype(bf16)

    picks = jnp.pad(pick_part.reshape(OWN, PLANE, tok_count).transpose(1, 0, 2), ((0, 0), (0, 8 - OWN), (0, 0)))
    expert_sum, hidden_grad, picks_all = plane_reduce(
        [
            moe_part.reshape(PLANE, tok_count, D),
            hidden_part.reshape(PLANE, tok_count, D),
        ],
        picks,
        5,
        "reduce_hidden",
    )
    output = (first_sum + RES_MULT * expert_sum).astype(bf16).reshape(tokens.shape)
    gate_grad = (
        jnp.sum(picks_all[:, :OWN].reshape(INNER, 2, OWN, tok_count), axis=1)
        .reshape(EXPERTS, tok_count)
        .T
    )
    gate_grad = kept_f * gate_grad
    picked_grad = gate * (gate_grad - jnp.sum(gate * gate_grad, axis=-1, keepdims=True))
    logit_grad = picked_grad.astype(bf16)
    hidden_grad = hidden_grad + jnp.einsum(
        "te,ed->td", logit_grad, router_t, preferred_element_type=f32
    )
    router_grad = jnp.einsum("td,te->de", hidden_two, logit_grad, preferred_element_type=f32)
    gain_two_grad = jnp.sum(hidden_grad * normed_two, axis=0)
    normed_grad = hidden_grad * gain_two_f
    cot_rows = cot_own.astype(f32)
    first_grad = cot_rows + scale_two * (
        normed_grad - normed_two * jnp.mean(normed_grad * normed_two, axis=-1, keepdims=True)
    )
    attn_grad = (RES_MULT * first_grad).astype(bf16)
    mixed_grad = jnp.einsum("td,md->tm", attn_grad, output_w, preferred_element_type=f32).astype(
        bf16
    )
    mixed_grad_f = (
        mixed_grad.reshape(2, block_rows, KV_HEADS, group_size, HEAD_DIM)
        .transpose(0, 2, 3, 1, 4)
        .astype(f32)
    )
    numer_grad = (mixed_grad_f / totals[..., None]).astype(bf16)
    total_grad = -jnp.sum(mixed_grad_f * attn_raw, axis=-1) / totals

    def backward_step(grad_query, block_in):
        key_blk, value_blk, key_pos, key_seg = block_in
        span_rows = key_blk.shape[0]
        key_acc = jnp.zeros((span_rows, KV_HEADS, HEAD_DIM), f32)
        value_acc = jnp.zeros((span_rows, KV_HEADS, HEAD_DIM), f32)
        new_query = []
        for half_side in range(2):
            allowed = score_mask(half_side, key_pos, key_seg)

            def backward_compute(state):
                part_query, part_key, part_value = state
                scores = jnp.einsum(
                    "grqd,kgd->grqk", queries[half_side], key_blk, preferred_element_type=f32
                )
                exp_values = jnp.where(allowed[None, None], jnp.exp(ATT_MULT * scores), 0.0)
                weights_low = exp_values.astype(bf16)
                through = jnp.einsum(
                    "grqd,kgd->grqk", numer_grad[half_side], value_blk, preferred_element_type=f32
                )
                score_grad = (
                    ATT_MULT * exp_values * (through + total_grad[half_side][..., None])
                ).astype(bf16)
                part_query = part_query + jnp.einsum(
                    "grqk,kgd->grqd", score_grad, key_blk, preferred_element_type=f32
                )
                part_key = part_key + jnp.einsum(
                    "grqk,grqd->kgd", score_grad, queries[half_side], preferred_element_type=f32
                )
                part_value = part_value + jnp.einsum(
                    "grqk,grqd->kgd", weights_low, numer_grad[half_side], preferred_element_type=f32
                )
                return (part_query, part_key, part_value)

            part_query, key_acc, value_acc = lax.cond(
                needed(half_side, key_pos),
                backward_compute,
                keep_state,
                (grad_query[half_side], key_acc, value_acc),
            )
            new_query.append(part_query)
        joined = jnp.concatenate(
            [key_acc.reshape(span_rows, kv_width), value_acc.reshape(span_rows, kv_width)], axis=1
        )
        return (jnp.stack(new_query), joined)

    query_grad, kv_terms = lax.scan(backward_step, jnp.zeros_like(numerator), blocks_all)
    kv_terms = kv_terms.reshape(2, ctx_count, block_rows, 2 * kv_width).astype(bf16)
    kv_mine = kv_reduce(kv_terms, ctx_count)
    key_grad = (
        rotate(kv_mine[:, :, :kv_width].reshape(tok_count, KV_HEADS, HEAD_DIM), flat_pos, -1.0)
        .astype(bf16)
        .reshape(tok_count, kv_width)
    )
    value_grad = kv_mine[:, :, kv_width:].reshape(tok_count, kv_width).astype(bf16)
    query_rows_grad = query_grad.transpose(0, 3, 1, 2, 4).reshape(tok_count, HEADS, HEAD_DIM)
    query_lin_grad = (
        rotate(query_rows_grad, flat_pos, -1.0).astype(bf16).reshape(tok_count, HEADS * HEAD_DIM)
    )
    qkv_grad = jnp.concatenate([query_lin_grad, key_grad, value_grad], axis=1)
    hidden_one_grad = jnp.einsum("tm,dm->td", qkv_grad, qkv_w, preferred_element_type=f32)
    gain_one_grad = jnp.sum(hidden_one_grad * normed_one, axis=0)
    normed_one_grad = hidden_one_grad * gain_one_f
    token_grad = first_grad + scale_one * (
        normed_one_grad
        - normed_one * jnp.mean(normed_one_grad * normed_one, axis=-1, keepdims=True)
    )

    swap = jnp.concatenate(
        [
            qkv_grad.reshape(tok_count, PLANE, 2048 // PLANE),
            attn_grad.reshape(tok_count, PLANE, D // PLANE),
        ],
        axis=2,
    ).transpose(1, 0, 2)
    left_own = jnp.stack([hidden_one, mixed])
    grads_all, left_all = plane_swap(swap, left_own, 6, "swap_grads")
    left_one = left_all[:, 0].reshape(plane_rows, D)
    left_mixed = left_all[:, 1].reshape(plane_rows, D)
    grads_all = grads_all.reshape(plane_rows, 3 * D // PLANE)
    qkv_cols = 2048 // PLANE
    attn_part = jnp.concatenate(
        [
            jnp.einsum("td,tm->dm", left_one, grads_all[:, :qkv_cols], preferred_element_type=f32),
            jnp.einsum("td,tm->dm", left_mixed, grads_all[:, qkv_cols:], preferred_element_type=f32),
        ],
        axis=1,
    ).astype(bf16)
    small_part = jnp.concatenate(
        [router_grad, gain_one_grad[:, None], gain_two_grad[:, None], jnp.zeros((D, 110), f32)], axis=1
    )
    attn_in, inner_in, outer_in, small_in = owners(
        [attn_part, inner_grad, outer_grad, small_part], devices, 7, "owners"
    )
    attn_sum = jnp.sum(
        attn_in.astype(f32).reshape(outers, PLANE, owner_rows, 3 * D // PLANE), axis=0
    ).transpose(1, 0, 2)
    qkv_sum = attn_sum[:, :, :qkv_cols].reshape(owner_rows, 2048)
    output_sum = attn_sum[:, :, qkv_cols:].reshape(owner_rows, D)
    inner_sum = jnp.sum(
        inner_in.astype(f32).reshape(outers, INNER, 2, OWN, owner_rows, 2, hidden_units), axis=0
    )
    inner_sum = inner_sum.transpose(0, 2, 3, 4, 1, 5).reshape(EXPERTS, owner_rows, 2, 2 * hidden_units)
    outer_sum = jnp.sum(
        outer_in.astype(f32).reshape(outers, INNER, 2, OWN, owner_rows, hidden_units), axis=0
    )
    outer_sum = outer_sum.transpose(0, 2, 3, 1, 4).reshape(EXPERTS, owner_rows, 2 * hidden_units)
    small_sum = jnp.sum(small_in, axis=0)
    return (
        output,
        token_grad.reshape(tokens.shape),
        qkv_sum[:, :1024],
        qkv_sum[:, 1024:1536],
        qkv_sum[:, 1536:],
        output_sum,
        small_sum[:, EXPERTS],
        small_sum[:, :EXPERTS],
        inner_sum,
        outer_sum,
        small_sum[:, EXPERTS + 1],
    )


def solution(mesh):
    placed = (
        P("wsh", None, "ctx", None),
        P("wsh", None),
        P("wsh", None),
        P("wsh", None),
        P("wsh", None),
        P("wsh"),
        P("wsh", None),
        P(None, None, None, "wsh"),
        P(None, None, "wsh"),
        P("wsh"),
        P("wsh", None),
        P("wsh", None, "ctx", None),
        P("wsh", None, "ctx", None),
        P("wsh", None, "ctx", None),
    )
    return jax.shard_map(
        body,
        mesh=mesh,
        in_specs=placed,
        out_specs=(
            P("wsh", None, "ctx", None),
            P("wsh", None, "ctx", None),
            P(("ctx", "wsh"), None),
            P(("ctx", "wsh"), None),
            P(("ctx", "wsh"), None),
            P(("ctx", "wsh"), None),
            P(("ctx", "wsh")),
            P(("ctx", "wsh"), None),
            P(None, ("ctx", "wsh"), None, None),
            P(None, ("ctx", "wsh"), None),
            P(("ctx", "wsh")),
        ),
        check_vma=False,
    )
```

time: 3900 us -> 753 us (0.19)
  the two profiles are of different devices: /device:TPU:0 before, /device:TPU:31 now
where the time goes in v1:
time: 753 us; the launch traced here: 743 us
  Pallas kernels  472 us (63%)
  local copies, waits for them, and re-layouts  110 us (15%)
  matrix products  95.9 us (13%)
  other arithmetic  52.1 us (7%)
  loops' own time  11.2 us (1%)
    pallas_call x1, Pallas kernels, owners(): comm_call(functools.partial(owners_kernel, devices, count), shapes, [ANY]...  191 us
    pallas_call x1, Pallas kernels, gather_weights(): comm_call(weights_kernel, [shape((D, 2048), BF16), shape((D, D), BF16), s...  106 us
    pallas_call x1, Pallas kernels, kv_reduce(): comm_call(functools.partial(kv_reduce_kernel, outers), jax.ShapeDtypeStru...  46.2 us
    pallas_call x1, Pallas kernels, kv_gather(): comm_call(functools.partial(kv_gather_kernel, outers), jax.ShapeDtypeStru...  40.6 us
    pallas_call x1, Pallas kernels, plane_swap(): comm_call(plane_swap_kernel, [shape(src.shape, src.dtype), shape((PLANE,)...  37.7 us
    pallas_call x1, Pallas kernels, plane_reduce(): comm_call(functools.partial(plane_reduce_kernel, count), [shape((rows, wi...  32.3 us
    dynamic_slice x2, local copies, waits for them, and re-layouts, body(): inner_w = lax.dynamic_slice_in_dim(expert_in, first_expert, OWN, axis=0)  18.2 us
    pallas_call x1, Pallas kernels, plane_gather(): comm_call(functools.partial(plane_gather_kernel, count), [jax.ShapeDtypeS...  17.9 us

profile of v1, /device:TPU:31, one launch (start us, length us, event | category | flops | bytes accessed | tf_op | source)
XLA Modules:
  0.0 743.2 jit_solution(15401767043499531213)
XLA Ops:
  7.1 11.8 %gather_fusion = s32[2048]{0:T(1024)S(1)} fusion(s32[2048]{0:T(1024)S(1)} %bitcast.366, s32[2048]{0:T(1024)S(1)} %bitcast_clamp_fusion), kind=kCustom, calls=%fused_computation | custom fusion | bytes 24576 | tf_op jit(solution)/shard_map/gather | solution.py:715
  20.8 2.6 convert_reduce_fusion.2
  23.5 7.0 constant_dynamic-slice_fusion.4
  30.5 11.2 %copy.204 = bf16[4,1024,2,256]{1,3,2,0:T(8,128)(2,1)} copy(bf16[4,1024,2,256]{3,2,1,0:T(2,128)(2,1)} %constant_dynamic-slice_fusion.4) | data formatting | bytes 8388608 | tf_op jit(solution)/shard_map/dynamic_slice | solution.py:751
  41.7 106.4 %gather_weights.1 = (bf16[1024,2048]{1,0:T(8,128)(2,1)}, bf16[1024,1024]{1,0:T(8,128)(2,1)}, bf16[2,32,512]{2,1,0:T(8,128)(2,1)}, bf16[8,128,1024]{2,1,0:T(8,128)(2,1)}) custom-call(bf16[512,1024]{1,0:T(8,128)(2,1)} %wq.1, bf16[512,512]{1,0:T(8,128)(2,1)} %wk.1, bf16[512,512]{1,0:T(8,128)(2,1)} %wv.1, bf16[512,1024]{1,0:T(8,128)(2,1)} %wo.1, ...), custom_call_target="tpu_custom_call" | custom-call | tf_op jit(solution)/shard_map/gather_weights/pallas_call | solution.py:214
  150.0 2.9 fusion.137
  156.8 40.6 %kv_gather.1 = bf16[2,16,64,1024]{3,2,1,0:T(8,128)(2,1)} custom-call(bf16[2,64,1024]{2,1,0:T(8,128)(2,1)} %pad_maximum_fusion.13.own), custom_call_target="tpu_custom_call" | custom-call | tf_op jit(solution)/shard_map/kv_gather/pallas_call | solution.py:276
  197.3 3.9 fusion.134
  201.3 4.0 copy.195
  205.3 2.4 copy.194
  207.7 23.9 %while.28 = (s32[]{:T(128)}, f32[2,8,2,64,64]{4,3,2,1,0:T(8,128)S(1)}, f32[2,8,2,64]{3,2,1,0:T(2,128)S(1)}, s32[2,1024]{1,0:T(2,128)S(1)}, s32[]{:T(128)}, /*ind...) while((s32[]{:T(128)}, ...), condition=%wide.region_11.12_spmd.clone, body=%wide.region_3.11_spmd.clone.sunk | while | flops 550112384 | bytes 30896524 | solution.py:717
  211.4 2.8 dynamic-slice_bitcast_fusion.8
  214.2 3.6 conditional.13
  214.3 2.6 fusion.4
  217.8 3.7 conditional.12
  218.0 2.6 fusion.24
  225.1 2.8 dynamic-slice_bitcast_fusion.8
  227.9 3.6 conditional.12
  228.0 2.6 fusion.24
  234.1 2.2 multiply_reduce_fusion.4
  237.3 17.9 %gather_hidden.1 = (bf16[8,128,1024]{2,1,0:T(8,128)(2,1)}, f32[8,16,128]{2,1,0:T(8,128)}) custom-call(bf16[128,1024]{1,0:T(8,128)(2,1)} %copy-done.14, f32[16,128]{1,0:T(8,128)} %get-tuple-element.809.refs_1_), custom_call_target="tpu_custom_call" | custom-call | tf_op jit(solution)/shard_map/gather_hidden/pallas_call | solution.py:146
  255.9 7.4 convolution_bitcast_fusion.1
  263.4 5.9 fusion.93
  269.3 6.1 bitcast_convert_fusion
  275.4 3.9 fusion.101.refs_2_
  279.3 5.3 bitcast_convert_fusion.1
  285.2 32.3 %reduce_hidden.1 = (f32[128,1024]{1,0:T(8,128)}, f32[128,1024]{1,0:T(8,128)}, f32[8,8,128]{2,1,0:T(8,128)}) custom-call(bf16[2,2,2,128,1024]{4,3,2,1,0:T(8,128)(2,1)} %bitcast.384, bf16[2,2,2,128,1024]{4,3,2,1,0:T(8,128)(2,1)} %bitcast.383, f32[8,8,128]{2,1,0:T(8,128)} %pad.4.refs_2_), custom_call_target="tpu_custom_call" | custom-call | tf_op jit(solution)/shard_map/reduce_hidden/pallas_call | solution.py:429
  321.1 2.4 fusion.103
  328.8 67.5 %while.29 = (s32[]{:T(128)}, f32[2,8,2,64,64]{4,3,2,1,0:T(8,128)}, bf16[2,1024,1024]{1,2,0:T(8,128)(2,1)}, s32[2,1024]{1,0:T(2,128)S(1)}, s32[]{:T(128)}, /*inde...) while((s32[]{:T(128)}, f32[2,8,2,64,64]{4,3,2,1,0:T(8,128)}, ...), condition=%wide.region_29.30_spmd.clone, body=%wide.region_23.29_spmd.clone.sunk | while | flops 1366951040 | bytes 79622736 | solution.py:866
  333.1 2.1 slice_bitcast_fusion.25
  335.2 2.8 dynamic-slice_bitcast_fusion.9
  337.9 10.0 %conditional.14 = (f32[8,2,64,64]{3,2,1,0:T(8,128)S(1)}, f32[1024,8,64]{0,2,1:T(8,128)S(1)}, f32[1024,8,64]{0,2,1:T(8,128)}) conditional(s32[]{:T(128)} %convert_element_type.324, f32[8,2,64,64]{3,2,1,0:T(8,128)S(1)} %get-tuple-element.1097, (s32[2,64]{1,0:T(2,128)S(1)}, s32[64,1024]{1,0:T(8,128)}, s32[2,64]{1,0:T(2,128)S(1)}, ...), branch_computations={%region_25.25_spmd, %region_26.26_spmd} | conditional | flops 680787968 | bytes 28526104 | solution.py:854
  340.7 2.8 multiply_convert_fusion
  343.4 2.2 fusion.50
  348.7 12.4 %conditional.15 = (f32[1,8,2,64,64]{4,3,2,1,0:T(8,128)}, f32[1024,512]{0,1:T(8,128)S(1)}, f32[1024,512]{0,1:T(8,128)}) conditional(s32[]{:T(128)} %convert_element_type.323, (f32[8,2,64,64]{3,2,1,0:T(8,128)}, f32[1024,8,64]{0,2,1:T(8,128)S(1)}, f32[1024,8,64]{0,2,1:T(8,128)}) %tuple.246, (s32[2,64]{1,0:T(2,128)S(1)}, s32[64,1024]{1,0:T(8,128)}, ...), branch_computations={%region_27.27_spmd, %region_28.28_spmd} | conditional | flops 681836544 | bytes 35866220 | solution.py:854
  351.5 4.0 bitcast_add_fusion
  355.5 2.8 multiply_convert_fusion.1
  359.1 2.0 bitcast_add_fusion.1
  361.1 2.3 pad_maximum_fusion.23
  363.4 3.3 fusion.171
  370.8 2.1 slice_bitcast_fusion.25
  372.9 2.8 dynamic-slice_bitcast_fusion.9
  375.6 1.9 conditional.14
  378.3 12.4 %conditional.15 = (f32[1,8,2,64,64]{4,3,2,1,0:T(8,128)}, f32[1024,512]{0,1:T(8,128)S(1)}, f32[1024,512]{0,1:T(8,128)}) conditional(s32[]{:T(128)} %convert_element_type.323, (f32[8,2,64,64]{3,2,1,0:T(8,128)}, f32[1024,8,64]{0,2,1:T(8,128)S(1)}, f32[1024,8,64]{0,2,1:T(8,128)}) %tuple.246, (s32[2,64]{1,0:T(2,128)S(1)}, s32[64,1024]{1,0:T(8,128)}, ...), branch_computations={%region_27.27_spmd, %region_28.28_spmd} | conditional | flops 681836544 | bytes 35866220 | solution.py:854
  379.5 1.6 fusion.78
  381.2 4.0 bitcast_add_fusion
  385.1 2.8 multiply_convert_fusion.1
  388.7 2.0 bitcast_add_fusion.1
  390.8 2.3 pad_maximum_fusion.23
  393.1 3.3 fusion.171
  396.3 6.3 copy.213
  402.6 46.2 %kv_reduce.1 = f32[2,64,1024]{2,1,0:T(8,128)} custom-call(bf16[2,4,2,2,64,1024]{5,4,3,2,1,0:T(8,128)(2,1)} %bitcast.375), custom_call_target="tpu_custom_call" | custom-call | tf_op jit(solution)/shard_map/kv_reduce/pallas_call | solution.py:350
  448.8 1.9 copy.212
  452.5 4.6 multiply_reduce_fusion.1
  460.2 2.4 multiply_add_fusion
  464.0 9.4 %convert_bitcast_fusion.refs_1_ = bf16[4,1024,512]{2,1,0:T(8,128)(2,1)} fusion(bf16[1024,1024,1]{1,0,2:T(8,128)(2,1)} %bitcast.433, bf16[4,1024,256]{2,1,0:T(8,128)(2,1)} %copy-done.37, bf16[4,1024,256]{2,1,0:T(8,128)(2,1)} %copy-done.36), kind=kOutput, calls=%fused_computation.134 | convolution fusion | flops 4305453056 | bytes 10485760 | tf_op jit(solution)/shard_map/td,etf->edf/dot_general | solution.py:773
  473.4 37.7 %swap_grads.1 = (bf16[8,128,384]{2,1,0:T(8,128)(2,1)}, bf16[8,2,128,1024]{3,2,1,0:T(8,128)(2,1)}) custom-call(bf16[8,128,384]{2,1,0:T(8,128)(2,1)} %maximum_bitcast_fusion.1.src, bf16[2,128,1024]{2,1,0:T(8,128)(2,1)} %pad_maximum_fusion.12.gather_in), custom_call_target="tpu_custom_call" | custom-call | tf_op jit(solution)/shard_map/swap_grads/pallas_call | solution.py:473
  511.1 2.8 fusion.133
  516.4 190.6 %owners.1 = (bf16[32,32,384]{2,1,0:T(8,128)(2,1)}, bf16[32,4,32,512]{3,2,1,0:T(8,128)(2,1)}, bf16[32,4,32,256]{3,2,1,0:T(8,128)(2,1)}, f32[32,32,128]{2,1,0:T(8,128)}) custom-call(bf16[1024,384]{1,0:T(8,128)(2,1)} %pad_maximum_fusion.10.refs_0_, bf16[4,1024,512]{2,1,0:T(8,128)(2,1)} %convert_bitcast_fusion.refs_1_, bf16[4,1024,256]{2,1,0:T(8,128)(2,1)} %fusion.101.refs_2_, ...), custom_call_target="tpu_custom_call" | custom-call | tf_op jit(solution)/shard_map/owners/pallas_call | solution.py:545
  714.2 1.8 reshape.709
  716.0 9.6 %reshape.721 = f32[4,4,2,4,32,2,256]{6,5,4,3,2,1,0:T(2,128)} reshape(bf16[32,4,32,512]{3,2,1,0:T(8,128)(2,1)} %get-tuple-element.486) | data formatting | bytes 12582912 | tf_op jit(solution)/shard_map/reshape | solution.py:920
  725.6 10.5 %reduce_sum.186 = f32[4,2,4,32,2,256]{5,4,3,2,1,0:T(2,128)} reduce(f32[4,4,2,4,32,2,256]{6,5,4,3,2,1,0:T(2,128)} %reshape.721, f32[]{:T(128)} %constant.154.clone.1), dimensions={0}, to_apply=%region_35.36 | reduce | flops 1572864 | bytes 10485764 | tf_op jit(solution)/shard_map/reduce_sum | solution.py:919
  736.1 3.2 copy.264
  739.4 3.4 reshape.760
  (259 shorter events, 65.0 us)
Async XLA Ops:
  0.6 0.7 copy-start
  3.5 146.4 %copy-start.31 = (f32[128]{0:T(128)}, f32[128]{0:T(128)S(1)}, u32[]{:S(2)}) copy-start(f32[128]{0:T(128)S(1)} %rsqrt.20) | copy-start | bytes 1540
  7.1 11.8 %copy-start.29 = (s32[1,2,64,8]{2,3,1,0:T(8,128)S(1)}, s32[1,2,64,8]{2,3,1,0:T(8,128)}, u32[]{:S(2)}) copy-start(s32[1,2,64,8]{2,3,1,0:T(8,128)} %param.37) | copy-start | bytes 12292
  7.1 12.0 %copy-start.30 = (s32[1,2,64,8]{2,3,1,0:T(8,128)S(1)}, s32[1,2,64,8]{2,3,1,0:T(8,128)}, u32[]{:S(2)}) copy-start(s32[1,2,64,8]{2,3,1,0:T(8,128)} %param.38) | copy-start | bytes 12292
  7.1 12.1 %copy-start.28 = (bf16[512,16]{0,1:T(8,128)(2,1)S(1)}, bf16[512,16]{0,1:T(8,128)(2,1)}, u32[]{:S(2)}) copy-start(bf16[512,16]{0,1:T(8,128)(2,1)} %param.32) | copy-start | bytes 49156
  20.7 132.8 %copy-start.23 = (f32[128,32]{0,1:T(8,128)}, f32[128,32]{0,1:T(8,128)S(1)}, u32[]{:S(2)}) copy-start(f32[128,32]{0,1:T(8,128)S(1)} %get-tuple-element.865) | copy-start | bytes 49156
  30.5 119.2 %copy-start.9 = (bf16[1,2,64,1024]{3,2,1,0:T(8,128)(2,1)S(1)}, bf16[1,2,64,1024]{3,2,1,0:T(8,128)(2,1)}, u32[]{:S(2)}) copy-start(bf16[1,2,64,1024]{3,2,1,0:T(8,128)(2,1)} %param.26) | copy-start | bytes 786436
  148.9 4.1 copy-start.26
  236.3 84.6 %copy-start.7 = (f32[128,1024]{1,0:T(8,128)}, f32[128,1024]{1,0:T(8,128)S(1)}, u32[]{:S(2)}) copy-start(f32[128,1024]{1,0:T(8,128)S(1)} %get-tuple-element.867) | copy-start | bytes 1572868
  236.4 0.9 copy-start.14
  255.9 7.4 copy-start.34
  263.3 6.0 copy-start.13
  269.3 6.1 copy-start.36
  269.3 6.1 copy-start.37
  284.6 35.2 %copy-start.15 = (bf16[128,1024]{1,0:T(8,128)(2,1)S(1)}, bf16[128,1024]{1,0:T(8,128)(2,1)}, u32[]{:S(2)}) copy-start(bf16[128,1024]{1,0:T(8,128)(2,1)} %copy-done.14) | copy-start | bytes 786436
  284.6 36.3 %copy-start.16 = (bf16[1,2,64,1024]{3,2,1,0:T(8,128)(2,1)S(1)}, bf16[1,2,64,1024]{3,2,1,0:T(8,128)(2,1)}, u32[]{:S(2)}) copy-start(bf16[1,2,64,1024]{3,2,1,0:T(8,128)(2,1)} %param.39) | copy-start | bytes 786436
  319.7 1.1 copy-start.11
  332.3 5.6 copy-start.5
  347.9 0.8 copy-start.4
  348.7 2.8 copy-start.6
  355.5 2.8 copy-start.2
  359.1 2.1 copy-start.3
  370.0 5.6 copy-start.5
  377.5 0.8 copy-start.4
  378.3 2.8 copy-start.6
  385.1 2.8 copy-start.2
  388.7 2.1 copy-start.3
  402.6 48.7 %copy-start.24 = (f32[128,32]{0,1:T(8,128)S(1)}, f32[128,32]{0,1:T(8,128)}, u32[]{:S(2)}) copy-start(f32[128,32]{0,1:T(8,128)} %copy-done.23) | copy-start | bytes 49156
  402.6 48.7 %copy-start.25 = (f32[128,32]{0,1:T(8,128)S(1)}, f32[128,32]{0,1:T(8,128)}, u32[]{:S(2)}) copy-start(f32[128,32]{0,1:T(8,128)} %get-tuple-element.863) | copy-start | bytes 49156
  448.8 2.7 copy-start.21
  448.8 2.8 slice-start
  450.7 1.8 copy-start.10
  450.7 1.8 copy-start.27
  450.7 1.8 copy-start.32
  452.4 6.8 copy-start.22
  452.5 7.7 %copy-start.8 = (f32[128,1024]{1,0:T(8,128)S(1)}, f32[128,1024]{1,0:T(8,128)}, u32[]{:S(2)}) copy-start(f32[128,1024]{1,0:T(8,128)} %copy-done.7) | copy-start | bytes 1572868
  452.5 7.7 %copy-start.12 = (f32[128,1024]{1,0:T(8,128)S(1)}, f32[128,1024]{1,0:T(8,128)}, u32[]{:S(2)}) copy-start(f32[128,1024]{1,0:T(8,128)} %copy-done.11) | copy-start | bytes 1572868
  452.5 7.7 %copy-start.17 = (bf16[1,2,64,1024]{3,2,1,0:T(8,128)(2,1)S(1)}, bf16[1,2,64,1024]{3,2,1,0:T(8,128)(2,1)}, u32[]{:S(2)}) copy-start(bf16[1,2,64,1024]{3,2,1,0:T(8,128)(2,1)} %param.39) | copy-start | bytes 786436
  457.2 5.7 copy-start.18
  457.2 5.7 copy-start.19
  457.2 5.7 copy-start.33
  511.1 2.8 copy-start.35
  707.0 5.9 copy-start.20
  736.1 6.7 copy-start.1

commit v2 on v1

v2 whole, which is shorter than its diff:
```python
import functools

import jax
import jax.numpy as jnp
from jax import lax
from jax.experimental import pallas as pl
from jax.experimental.pallas import tpu as pltpu
from jax.sharding import PartitionSpec as P

D = 1024
HEADS = 16
KV_HEADS = 8
HEAD_DIM = 64
TOPK = 8
EXPERTS = 16
CAP = 80
PLANE = 8
INNER = 4
OWN = EXPERTS // INNER


RES_MULT = 0.22
ATT_MULT = 0.015625
EPS = 1e-06
THETA = 10000.0

MESH = pl.DeviceIdType.MESH
F32 = jnp.float32
BF16 = jnp.bfloat16
ANY = pl.BlockSpec(memory_space=pl.ANY)
VMEM = pl.BlockSpec(memory_space=pltpu.VMEM)


class Place:
    def __init__(self):
        self.c = lax.axis_index("ctx")
        self.w = lax.axis_index("wsh")
        self.core = self.c % 2
        self.y = (self.c // 2) % 2
        self.inner = self.c % INNER
        self.outer = self.c // INNER
        self.j = self.inner * 2 + self.w
        self.sib = self.c + 1 - 2 * self.core
        self.yn = self.c + 2 - 4 * self.y

    def relative(self, dy, dc, dw):
        y = self.y + dy * (1 - 2 * self.y)
        core = self.core + dc * (1 - 2 * self.core)
        w = self.w + dw * (1 - 2 * self.w)
        ctx = self.outer * INNER + y * 2 + core
        return (ctx, w), (y * 2 + core) * 2 + w


OTHERS = [(a, b, d) for a in range(2) for b in range(2) for d in range(2) if a + b + d]
XY = [(0, 0, 1), (1, 0, 0), (1, 0, 1)]


def meet(devices):
    barrier = pltpu.get_barrier_semaphore()
    for device in devices:
        pl.semaphore_signal(barrier, inc=1, device_id=device, device_id_type=MESH)
    pl.semaphore_wait(barrier, len(devices))


def remote(src, dst, send, recv, device):
    return pltpu.make_async_remote_copy(
        src_ref=src,
        dst_ref=dst,
        send_sem=send,
        recv_sem=recv,
        device_id=device,
        device_id_type=MESH,
    )


def comm_call(kernel, out_shape, in_specs, out_specs, scratch, ident, name, vmem=None):
    return pl.pallas_call(
        kernel,
        out_shape=out_shape,
        in_specs=in_specs,
        out_specs=out_specs,
        scratch_shapes=scratch,
        compiler_params=pltpu.CompilerParams(
            collective_id=ident, has_side_effects=True, vmem_limit_bytes=vmem
        ),
        name=name,
    )


DMA = pltpu.SemaphoreType.DMA


def gather_start(at, pairs, send, recv, local):
    copies = []
    for index, (src, dst) in enumerate(pairs):
        keep = pltpu.make_async_copy(src, dst.at[at.j], local.at[index])
        keep.start()
        sends = []
        for slot, bits in enumerate(XY + [(0, 1, 0)]):
            device, unused = at.relative(*bits)
            copy = remote(src, dst.at[at.j], send.at[index, slot], recv.at[index, slot], device)
            copy.start()
            sends.append(copy)
        copies.append((keep, sends))
    return copies


def gather_finish(at, pairs, copies, send, recv):
    sib, unused = at.relative(0, 1, 0)
    passed = []
    for slot, bits in enumerate(XY):
        unused, j_from = at.relative(*bits)
        for index, (src, dst) in enumerate(pairs):
            copies[index][1][slot].wait_recv()
            copy = remote(
                dst.at[j_from],
                dst.at[j_from],
                send.at[index, 4 + slot],
                recv.at[index, 4 + slot],
                sib,
            )
            copy.start()
            passed.append(copy)
    for keep, sends in copies:
        keep.wait()
        sends[3].wait_recv()
        for copy in sends:
            copy.wait_send()
    for copy in passed:
        copy.wait()


def plane_gather_kernel(count, *refs):
    ins, outs = refs[:count], refs[count : 2 * count]
    send, recv, local = refs[2 * count :]
    at = Place()
    meet([at.relative(*bits)[0] for bits in XY + [(0, 1, 0)]])
    pairs = list(zip(ins, outs))
    copies = gather_start(at, pairs, send, recv, local)
    gather_finish(at, pairs, copies, send, recv)


def plane_gather(arrays, ident, name):
    count = len(arrays)
    return comm_call(
        functools.partial(plane_gather_kernel, count),
        [jax.ShapeDtypeStruct((PLANE,) + a.shape, a.dtype) for a in arrays],
        [ANY] * count,
        [ANY] * count,
        [DMA((count, 7)), DMA((count, 7)), DMA((count,))],
        ident,
        name,
    )(*arrays)


def weights_kernel(wq, wk, wv, small, wqkv_o, small_o, xs, xr, fs, fr):
    at = Place()
    partner, unused = at.relative(0, 0, 1)
    sib, unused = at.relative(0, 1, 0)
    meet([partner, sib])
    pieces = [(wk, 1024), (wv, 1536), (wq, 0)]
    sends, passed = [], []
    for index, (src, col) in enumerate(pieces):
        depth, width = src.shape
        half = depth // 2
        row = at.w * depth + at.core * half
        copy = remote(
            src.at[pl.ds(at.core * half, half), :],
            wqkv_o.at[pl.ds(row, half), pl.ds(col, width)],
            xs.at[index],
            xr.at[index],
            partner,
        )
        copy.start()
        sends.append(copy)
    last = len(pieces)
    copy = remote(small, small_o.at[at.w], xs.at[last], xr.at[last], partner)
    copy.start()
    sends.append(copy)
    small_o[at.w] = small[...]
    for src, col in pieces:
        depth, width = src.shape
        wqkv_o[pl.ds(at.w * depth, depth), pl.ds(col, width)] = src[...]
    for index, (src, col) in enumerate(pieces):
        depth, width = src.shape
        half = depth // 2
        row = (1 - at.w) * depth + at.core * half
        sends[index].wait_recv()
        piece = wqkv_o.at[pl.ds(row, half), pl.ds(col, width)]
        copy = remote(piece, piece, fs.at[index], fr.at[index], sib)
        copy.start()
        passed.append(copy)
    sends[last].wait_recv()
    for copy in sends:
        copy.wait_send()
    for copy in passed:
        copy.wait()


def gather_weights(wq, wk, wv, small):
    shape = jax.ShapeDtypeStruct
    return comm_call(
        weights_kernel,
        [shape((D, 2048), BF16), shape((2,) + small.shape, BF16)],
        [VMEM] * 4,
        [VMEM] * 2,
        [DMA((4,)), DMA((4,)), DMA((3,)), DMA((3,))],
        1,
        "gather_weights",
        vmem=40 * 2**20,
    )(wq, wk, wv, small)


class Blocks:
    def __init__(self, count):
        self.count = count

    def __call__(self, ref, half, ctx):
        return ref.at[ctx] if half == 0 else ref.at[2 * self.count - 1 - ctx]


def kv_gather_kernel(outers, own, full, zs, zr, ys, yr, cs, cr, local):
    at = Place()
    block_of = Blocks(outers * INNER)
    sib, unused = at.relative(0, 1, 0)
    side, unused = at.relative(1, 0, 0)
    other = [lax.rem(at.outer + r, outers) for r in range(outers)]
    back = [lax.rem(at.outer + outers - r, outers) for r in range(outers)]
    far = [(other[r] * INNER + at.inner, at.w) for r in range(1, outers)]
    meet([sib, side] + far)
    z_copies, y_copies, c_copies, keeps = {}, {}, {}, []
    for half in range(2):
        mine = block_of(full, half, at.c)
        keep = pltpu.make_async_copy(own.at[half], mine, local.at[half])
        keep.start()
        keeps.append(keep)
        for r in range(1, outers):
            copy = remote(own.at[half], mine, zs.at[half, r], zr.at[half, r], far[r - 1])
            copy.start()
            z_copies[half, r] = copy
        for send, recv, into, device in ((ys, yr, y_copies, side), (cs, cr, c_copies, sib)):
            copy = remote(own.at[half], mine, send.at[half, 0], recv.at[half, 0], device)
            copy.start()
            into[half, 0] = copy
    inner_side = at.inner + 2 - 4 * at.y
    for r in range(outers):
        for half in range(2):
            if r > 0:
                z_copies[half, r].wait_recv()
                block = block_of(full, half, back[r] * INNER + at.inner)
                for send, recv, into, device in ((ys, yr, y_copies, side), (cs, cr, c_copies, sib)):
                    copy = remote(block, block, send.at[half, r], recv.at[half, r], device)
                    copy.start()
                    into[half, r] = copy
    for r in range(outers):
        for half in range(2):
            y_copies[half, r].wait_recv()
            block = block_of(full, half, back[r] * INNER + inner_side)
            copy = remote(block, block, cs.at[half, outers + r], cr.at[half, outers + r], sib)
            copy.start()
            c_copies[half, outers + r] = copy
    for copy in list(z_copies.values()) + list(y_copies.values()):
        copy.wait_send()
    for copy in c_copies.values():
        copy.wait()
    for keep in keeps:
        keep.wait()


def kv_gather(own, ctx_count):
    outers = ctx_count // INNER
    return comm_call(
        functools.partial(kv_gather_kernel, outers),
        jax.ShapeDtypeStruct((2 * ctx_count,) + own.shape[1:], own.dtype),
        [VMEM],
        ANY,
        [DMA((2, outers))] * 4 + [DMA((2, 2 * outers))] * 2 + [DMA((2,))],
        2,
        "kv_gather",
    )(own)


def plane_reduce_kernel(count, *refs):
    parts, picks = refs[:count], refs[count]
    outs, picks_o = refs[count + 1 : 2 * count + 1], refs[2 * count + 1]
    near, summed, far, ss, sr, xs, xr, ps, pr, pl_sem = refs[2 * count + 2 :]
    at = Place()
    meet([at.relative(*bits)[0] for bits in OTHERS])
    sib, unused = at.relative(0, 1, 0)
    first = []
    for index in range(count):
        copy = remote(
            parts[index].at[:, 1 - at.core], near.at[index], ss.at[index], sr.at[index], sib
        )
        copy.start()
        first.append(copy)
    keep = pltpu.make_async_copy(picks.at[at.j], picks_o.at[at.j], pl_sem)
    keep.start()
    small = []
    for slot, bits in enumerate(OTHERS):
        device, j_to = at.relative(*bits)
        copy = remote(picks.at[j_to], picks_o.at[at.j], ps.at[slot], pr.at[slot], device)
        copy.start()
        small.append(copy)
    second = []
    for index in range(count):
        first[index].wait_recv()
        for y in range(2):
            for w in range(2):
                total = parts[index][y, at.core, w].astype(F32) + near[index, y, w].astype(F32)
                summed[index, y, w] = total.astype(BF16)
        for slot, (dy, dc, dw) in enumerate(XY):
            device, unused = at.relative(dy, dc, dw)
            y = at.y + dy * (1 - 2 * at.y)
            w = at.w + dw * (1 - 2 * at.w)
            copy = remote(
                summed.at[index, y, w], far.at[index, slot], xs.at[index, slot], xr.at[index, slot], device
            )
            copy.start()
            second.append(copy)
    for index in range(count):
        total = parts[index][at.y, at.core, at.w].astype(F32) + near[index, at.y, at.w].astype(F32)
        for slot in range(3):
            second[index * 3 + slot].wait_recv()
            total = total + far[index, slot].astype(F32)
        outs[index][...] = total
    keep.wait()
    for copy in small:
        copy.wait()
    for copy in first + second:
        copy.wait_send()


def plane_reduce(parts, picks, ident, name):
    count = len(parts)
    rows, width = parts[0].shape[-2:]
    shape = jax.ShapeDtypeStruct
    return comm_call(
        functools.partial(plane_reduce_kernel, count),
        [shape((rows, width), F32)] * count + [shape(picks.shape, picks.dtype)],
        [VMEM] * (count + 1),
        [VMEM] * (count + 1),
        [
            pltpu.VMEM((count, 2, 2, rows, width), BF16),
            pltpu.VMEM((count, 2, 2, rows, width), BF16),
            pltpu.VMEM((count, 3, rows, width), BF16),
            DMA((count,)),
            DMA((count,)),
            DMA((count, 3)),
            DMA((count, 3)),
            DMA((7,)),
            DMA((7,)),
            DMA,
        ],
        ident,
        name,
        vmem=60 * 2**20,
    )(*[p.reshape(2, 2, 2, rows, width) for p in parts], picks)


def owners_kernel(devices, count, near_count, *refs):
    total = count + near_count
    parts, nears = refs[:count], refs[count:total]
    outs, near_outs = refs[total : total + count], refs[total + count : 2 * total]
    send, recv, local, nsend, nrecv, nlocal = refs[2 * total :]
    at = Place()
    me = at.c * 2 + at.w
    rows = D // devices

    def device_of(r):
        index = lax.rem(me + r, devices)
        return index, (index // 2, lax.rem(index, 2))

    def rows_of(ref, index):
        return ref.at[pl.ds(pl.multiple_of(index * rows, rows), rows), :]

    barrier = pltpu.get_barrier_semaphore()

    def greet(r, carry):
        unused, device = device_of(r)
        pl.semaphore_signal(barrier, inc=1, device_id=device, device_id_type=MESH)
        return carry

    lax.fori_loop(1, devices, greet, 0)
    pl.semaphore_wait(barrier, devices - 1)

    def copy_of(k, r):
        index, device = device_of(r)
        return remote(rows_of(parts[k], index), outs[k].at[me], send.at[k, r], recv.at[k, r], device)

    def start(r, carry):
        for k in range(count):
            copy_of(k, r).start()
        return carry

    lax.fori_loop(1, devices, start, 0)

    near_copies = []
    for k in range(near_count):
        for slot, bits in enumerate(OTHERS):
            device, j_to = at.relative(*bits)
            copy = remote(
                nears[k].at[:, j_to], near_outs[k].at[at.j], nsend.at[k, slot], nrecv.at[k, slot], device
            )
            copy.start()
            near_copies.append(copy)
    keeps = []
    for k in range(count):
        keep = pltpu.make_async_copy(rows_of(parts[k], me), outs[k].at[me], local.at[k])
        keep.start()
        keeps.append(keep)
    for k in range(near_count):
        keep = pltpu.make_async_copy(nears[k].at[:, at.j], near_outs[k].at[at.j], nlocal.at[k])
        keep.start()
        keeps.append(keep)

    def finish(r, carry):
        for k in range(count):
            copy_of(k, r).wait()
        return carry

    lax.fori_loop(1, devices, finish, 0)
    for copy in near_copies:
        copy.wait()
    for keep in keeps:
        keep.wait()


def owners(parts, nears, devices, ident, name):
    count, near_count = len(parts), len(nears)
    rows = D // devices
    shape = jax.ShapeDtypeStruct
    shapes = [shape((devices, rows, part.shape[-1]), part.dtype) for part in parts]
    for near in nears:
        lead, members, near_rows, width = near.shape
        shapes.append(shape((members, lead, near_rows, width), near.dtype))
    return comm_call(
        functools.partial(owners_kernel, devices, count, near_count),
        shapes,
        [VMEM] * (count + near_count),
        [VMEM] * (count + near_count),
        [
            DMA((count, devices)),
            DMA((count, devices)),
            DMA((count,)),
            DMA((near_count, 7)),
            DMA((near_count, 7)),
            DMA((near_count,)),
        ],
        ident,
        name,
        vmem=60 * 2**20,
    )(*parts, *nears)


CHUNK = 256
PAIRS = KV_HEADS // 2
NEVER = -1e30


def low_lanes(shape):
    return lax.broadcasted_iota(jnp.int32, shape, 1) < HEAD_DIM


def spread(block):
    a, b = block[:, :128], block[:, 128:]
    low = low_lanes(a.shape)
    zero = jnp.zeros_like(a)
    return jnp.concatenate(
        [
            jnp.where(low, a, zero),
            jnp.where(low, pltpu.roll(a, HEAD_DIM, 1), zero),
            jnp.where(low, zero, pltpu.roll(b, HEAD_DIM, 1)),
            jnp.where(low, zero, b),
        ],
        axis=0,
    )


def unspread(four):
    rows = four.shape[0] // 4
    r0, r1, r2, r3 = (four[k * rows : (k + 1) * rows] for k in range(4))
    low = low_lanes(r0.shape)
    return jnp.concatenate(
        [
            jnp.where(low, r0, pltpu.roll(r1, HEAD_DIM, 1)),
            jnp.where(low, pltpu.roll(r2, HEAD_DIM, 1), r3),
        ],
        axis=1,
    )


def turn(values, cosine, sine):
    lane = lax.broadcasted_iota(jnp.int32, cosine.shape, 1)
    first = lane % HEAD_DIM < HEAD_DIM // 2
    blocks = []
    for start in range(0, values.shape[1], 128):
        u = values[:, start : start + 128]
        swapped = jnp.where(first, pltpu.roll(u, 96, 1), pltpu.roll(u, 32, 1))
        blocks.append(u * cosine + swapped * sine)
    return jnp.concatenate(blocks, axis=1)


def dot_nt(a, b):
    return lax.dot_general(a, b, (((1,), (1,)), ((), ())), preferred_element_type=F32)


def dot_tn(a, b):
    return lax.dot_general(a, b, (((0,), (0,)), ((), ())), preferred_element_type=F32)


def dot_nn(a, b):
    return jnp.dot(a, b, preferred_element_type=F32)


def attend_kernel(
    info,
    q_ref,
    kv_ref,
    start_ref,
    tok_ref,
    wo_ref,
    small_ref,
    route_ref,
    prio_ref,
    raw_ref,
    total_ref,
    mixed_ref,
    sum_ref,
    hid_ref,
    gate_ref,
    kept_ref,
    acc,
    acc_l,
):
    rows = q_ref.shape[0] // 2
    width = PAIRS * 128
    for half in range(2):
        base = info[4 + half]
        q_four = []
        for pair in range(PAIRS):
            block = q_ref[pl.ds(half * rows, rows), pl.ds(pair * 256, 256)].astype(F32) * ATT_MULT
            q_four.append(spread(block).astype(BF16))
        acc[...] = jnp.zeros_like(acc)
        acc_l[...] = jnp.zeros_like(acc_l)
        first = start_ref[pl.ds(half * rows, rows), :]
        place = base + lax.broadcasted_iota(jnp.int32, (rows, 1), 0)

        def step(chunk, carry):
            at_row = pl.multiple_of(chunk * CHUNK, CHUNK)
            key_pos = at_row + lax.broadcasted_iota(jnp.int32, (1, CHUNK), 1)
            bias = jnp.where((key_pos >= first) & (key_pos <= place), 0.0, NEVER)
            bias = jnp.concatenate([bias] * 4, axis=0)
            for pair in range(PAIRS):
                key = kv_ref[pl.ds(at_row, CHUNK), pl.ds(pair * 128, 128)]
                value = kv_ref[pl.ds(at_row, CHUNK), pl.ds(width + pair * 128, 128)]
                e = jnp.exp(dot_nt(q_four[pair], key) + bias)
                part = e[:, :128]
                for k in range(1, CHUNK // 128):
                    part = part + e[:, k * 128 : (k + 1) * 128]
                acc_l[pair] += part
                acc[pair] += dot_nn(e.astype(BF16), value)
            return carry

        lax.fori_loop(info[half], info[2 + half], step, 0)
        for pair in range(PAIRS):
            total = jnp.sum(acc_l[pair], axis=1, keepdims=True)
            total = jnp.broadcast_to(total, (4 * rows, 128))
            here = pl.ds(half * rows, rows), pl.ds(pair * 256, 256)
            raw_ref[here] = unspread(acc[pair] / total)
            total_ref[here] = unspread(total)
    mixed = raw_ref[...].astype(BF16)
    mixed_ref[...] = mixed
    first_sum = tok_ref[...].astype(F32) + RES_MULT * dot_nn(mixed, wo_ref[...])
    sum_ref[...] = first_sum
    scale = lax.rsqrt(jnp.mean(first_sum * first_sum, axis=1, keepdims=True) + EPS)
    gain_two = small_ref[pl.ds(EXPERTS + 1, 1), :].astype(F32)
    hidden = (first_sum * scale * gain_two).astype(BF16)
    hid_ref[...] = hidden

    logits = dot_nt(small_ref[...], hidden)[:EXPERTS]
    count = 2 * rows
    expert = lax.broadcasted_iota(jnp.int32, (EXPERTS, count), 0)
    routed = jnp.zeros((EXPERTS, count), F32)
    prio = jnp.zeros((EXPERTS, count), F32)
    for k in range(TOPK):
        same = expert == route_ref[pl.ds(k, 1), :]
        routed = jnp.where(same, 1.0, routed)
        prio = jnp.where(same, prio_ref[pl.ds(k, 1), :].astype(F32), prio)
    chosen = routed > 0.0
    order = lax.broadcasted_iota(jnp.int32, (EXPERTS, count), 1).astype(F32)
    key = jnp.where(chosen, prio * float(count) + order, 65536.0 * count)
    key_cols = jnp.concatenate([key, jnp.zeros((count - EXPERTS, count), F32)], axis=0).T
    ranks = []
    for e in range(EXPERTS):
        ahead = jnp.where(key_cols[:, e : e + 1] < key[e : e + 1, :], 1.0, 0.0)
        ranks.append(jnp.sum(ahead, axis=0, keepdims=True))
    rank = jnp.concatenate(ranks, axis=0)
    top = jnp.max(jnp.where(chosen, logits, -3e38), axis=0, keepdims=True)
    weight = jnp.where(chosen, jnp.exp(logits - top), 0.0)
    gate_ref[...] = weight / jnp.sum(weight, axis=0, keepdims=True)
    kept_ref[...] = jnp.where(chosen & (rank < CAP), 1.0, 0.0)


def local_call(kernel, out_shape, in_specs, scratch, name, cost, vmem):
    return pl.pallas_call(
        kernel,
        out_shape=out_shape,
        in_specs=in_specs,
        out_specs=[VMEM] * len(out_shape),
        scratch_shapes=scratch,
        compiler_params=pltpu.CompilerParams(vmem_limit_bytes=vmem),
        cost_estimate=pl.CostEstimate(flops=cost, bytes_accessed=16 * 2**20, transcendentals=2**21),
        name=name,
    )


SMEM = pl.BlockSpec(memory_space=pltpu.SMEM)


def attend(info, queries, kv_all, start, tokens, output_w, small, routes, priority):
    shape = jax.ShapeDtypeStruct
    count, width = queries.shape
    return local_call(
        attend_kernel,
        [
            shape((count, width), F32),
            shape((count, width), F32),
            shape((count, width), BF16),
            shape((count, D), F32),
            shape((count, D), BF16),
            shape((EXPERTS, count), F32),
            shape((EXPERTS, count), F32),
        ],
        [SMEM] + [VMEM] * 8,
        [pltpu.VMEM((PAIRS, 2 * count, 128), F32), pltpu.VMEM((PAIRS, 2 * count, 128), F32)],
        "attend",
        4 * 2**30,
        60 * 2**20,
    )(info, queries, kv_all, start, tokens, output_w, small, routes, priority)


def back_kernel(
    info,
    hg_ref,
    pick_ref,
    gate_ref,
    kept_ref,
    small_ref,
    sum_ref,
    cot_ref,
    wo_ref,
    raw_ref,
    total_ref,
    q_ref,
    kv_ref,
    start_ref,
    cos_ref,
    sin_ref,
    dy_ref,
    da_ref,
    dq_ref,
    dkv_ref,
    rows_ref,
    q_four,
    n_four,
    d_rows,
    dq_acc,
    kv_acc,
):
    count = q_ref.shape[0]
    rows = count // 2
    width = PAIRS * 128
    small = small_ref[...]
    gain_two = small[EXPERTS + 1 : EXPERTS + 2].astype(F32)
    parts = []
    for i in range(INNER):
        parts.append(pick_ref[2 * i, pl.ds(0, OWN), :] + pick_ref[2 * i + 1, pl.ds(0, OWN), :])
    gate = gate_ref[...]
    gate_grad = kept_ref[...] * jnp.concatenate(parts, axis=0)
    logit_grad = gate * (gate_grad - jnp.sum(gate * gate_grad, axis=0, keepdims=True))
    logit_grad = jnp.concatenate(
        [logit_grad, jnp.zeros((small.shape[0] - EXPERTS, count), F32)], axis=0
    ).astype(BF16)
    hidden_grad = hg_ref[...] + dot_tn(logit_grad, small)
    first_sum = sum_ref[...]
    scale = lax.rsqrt(jnp.mean(first_sum * first_sum, axis=1, keepdims=True) + EPS)
    normed = first_sum * scale
    hidden = (normed * gain_two).astype(BF16)
    router_rows = dot_nn(logit_grad, hidden)
    rows_ref[...] = router_rows
    rows_ref[pl.ds(EXPERTS + 1, 1), :] = jnp.sum(hidden_grad * normed, axis=0, keepdims=True)
    normed_grad = hidden_grad * gain_two
    first_grad = cot_ref[...].astype(F32) + scale * (
        normed_grad - normed * jnp.mean(normed_grad * normed, axis=1, keepdims=True)
    )
    dy_ref[...] = first_grad
    attn_grad = (RES_MULT * first_grad).astype(BF16)
    da_ref[...] = attn_grad
    mixed_grad = dot_nt(attn_grad, wo_ref[...]).astype(BF16).astype(F32)
    total = total_ref[...]
    numer = mixed_grad / total
    lost = mixed_grad * raw_ref[...] / total
    for half in range(2):
        here = slice(half * rows, (half + 1) * rows)
        for pair in range(PAIRS):
            cols = slice(pair * 256, (pair + 1) * 256)
            slot = half * PAIRS + pair
            q_four[slot] = spread(q_ref[here, cols].astype(F32) * ATT_MULT).astype(BF16)
            n_four[slot] = spread(numer[here, cols]).astype(BF16)
            d_rows[slot] = -jnp.sum(spread(lost[here, cols]).T, axis=0, keepdims=True)
    dq_acc[...] = jnp.zeros_like(dq_acc)

    def step(chunk, carry):
        at_row = pl.multiple_of(chunk * CHUNK, CHUNK)
        kv_acc[...] = jnp.zeros_like(kv_acc)
        key_pos = at_row + lax.broadcasted_iota(jnp.int32, (CHUNK, 1), 0)
        for half in range(2):

            @pl.when((chunk >= info[half]) & (chunk < info[2 + half]))
            def _():
                first = start_ref[pl.ds(half, 1), :]
                place = info[4 + half] + lax.broadcasted_iota(jnp.int32, (1, 4 * rows), 1) % rows
                bias = jnp.where((key_pos >= first) & (key_pos <= place), 0.0, NEVER)
                for pair in range(PAIRS):
                    slot = half * PAIRS + pair
                    key = kv_ref[pl.ds(at_row, CHUNK), pl.ds(pair * 128, 128)]
                    value = kv_ref[pl.ds(at_row, CHUNK), pl.ds(width + pair * 128, 128)]
                    e = jnp.exp(dot_nt(key, q_four[slot]) + bias)
                    through = dot_nt(value, n_four[slot])
                    dz = (e * (through + d_rows[slot])).astype(BF16)
                    kv_acc[:, pl.ds(pair * 128, 128)] += dot_nn(dz, q_four[slot])
                    kv_acc[:, pl.ds(width + pair * 128, 128)] += dot_nn(e.astype(BF16), n_four[slot])
                    dq_acc[slot] += dot_tn(dz, key)

        dkv_ref[pl.ds(at_row, CHUNK), :] = kv_acc[...].astype(BF16)
        return carry

    lax.fori_loop(0, kv_ref.shape[0] // CHUNK, step, 0)
    cosine = cos_ref[...]
    sine = -sin_ref[...]
    for half in range(2):
        here = slice(half * rows, (half + 1) * rows)
        for pair in range(PAIRS):
            block = ATT_MULT * unspread(dq_acc[half * PAIRS + pair])
            dq_ref[here, pair * 256 : (pair + 1) * 256] = turn(
                block, cosine[here], sine[here]
            ).astype(BF16)


def back(info, hidden_grad, picks, gate, kept, small, first_sum, cot, output_w, raw, total, queries, kv_all, start, cosine, sine):
    shape = jax.ShapeDtypeStruct
    count, width = queries.shape
    return local_call(
        back_kernel,
        [
            shape((count, D), F32),
            shape((count, D), BF16),
            shape((count, width), BF16),
            shape(kv_all.shape, BF16),
            shape((32, D), F32),
        ],
        [SMEM] + [VMEM] * 15,
        [
            pltpu.VMEM((2 * PAIRS, 2 * count, 128), BF16),
            pltpu.VMEM((2 * PAIRS, 2 * count, 128), BF16),
            pltpu.VMEM((2 * PAIRS, 1, 2 * count), F32),
            pltpu.VMEM((2 * PAIRS, 2 * count, 128), F32),
            pltpu.VMEM((CHUNK, 2 * PAIRS * 128), F32),
        ],
        "back",
        8 * 2**30,
        60 * 2**20,
    )(info, hidden_grad, picks, gate, kept, small, first_sum, cot, output_w, raw, total, queries, kv_all, start, cosine, sine)


def finish_kernel(
    outers,
    part,
    moe,
    sum_ref,
    dq_ref,
    da_ref,
    dy_ref,
    tok_ref,
    small_ref,
    cos_ref,
    sin_ref,
    wqkv_ref,
    left_one,
    left_mixed,
    rows_ref,
    out_ref,
    token_ref,
    attn_ref,
    small_o,
    half_in,
    y_in,
    z_in,
    m_near,
    m_x,
    m_y,
    qkv,
    swap,
    swapped,
    ss,
    sr,
    ys,
    yr,
    zs,
    zr,
    ns,
    nr,
    ws,
    wr,
):
    at = Place()
    blocks, rows, full = part.shape
    width = full // 2
    count = 2 * rows
    sib, unused = at.relative(0, 1, 0)
    side, unused = at.relative(1, 0, 0)
    across, unused = at.relative(0, 0, 1)
    other = [lax.rem(at.outer + r, outers) for r in range(outers)]
    far = [(other[r] * INNER + at.inner, at.w) for r in range(1, outers)]
    meet([at.relative(*bits)[0] for bits in OTHERS] + far)

    def own_block(half, o, y, core):
        index = (o * 2 + y) * 2 + core
        return index if half == 0 else blocks - 1 - index

    first = {}
    for k in range(2):
        cols = pl.ds(k * width, width)
        for y in range(2):
            for h in range(2):
                for o in range(outers):
                    copy = remote(
                        part.at[own_block(h, o, y, 1 - at.core), :, cols],
                        half_in.at[y, h, o, :, cols],
                        ss.at[k, y, h, o],
                        sr.at[k, y, h, o],
                        sib,
                    )
                    copy.start()
                    first[k, y, h, o] = copy
    near = remote(moe.at[:, 1 - at.core], m_near, ns.at[0], nr.at[0], sib)
    near.start()
    second = []
    for k in range(2):
        cols = pl.ds(k * width, width)
        for y in range(2):
            for h in range(2):
                for o in range(outers):
                    first[k, y, h, o].wait_recv()
                    total = part[own_block(h, o, y, at.core), :, cols].astype(F32) + half_in[
                        y, h, o, :, cols
                    ].astype(F32)
                    half_in[y, h, o, :, cols] = total.astype(BF16)
        copy = remote(
            half_in.at[1 - at.y, :, :, :, cols], y_in.at[:, :, :, cols], ys.at[k], yr.at[k], side
        )
        copy.start()
        second.append(copy)
    near.wait_recv()
    for y in range(2):
        for w in range(2):
            total = moe[y, at.core, w].astype(F32) + m_near[y, w].astype(F32)
            m_near[y, w] = total.astype(BF16)
    cross = remote(m_near.at[:, 1 - at.w], m_x, ns.at[1], nr.at[1], across)
    cross.start()
    third = []

    def z_send(k):
        cols = pl.ds(k * width, width)
        second[k].wait_recv()
        for o in range(outers):
            for h in range(2):
                total = half_in[at.y, h, o, :, cols].astype(F32) + y_in[h, o, :, cols].astype(F32)
                half_in[at.y, h, o, :, cols] = total.astype(BF16)
        for r in range(1, outers):
            copy = remote(
                half_in.at[at.y, :, other[r], :, cols],
                z_in.at[r, :, :, cols],
                zs.at[k, r],
                zr.at[k, r],
                far[r - 1],
            )
            copy.start()
            third.append(copy)

    z_send(0)
    cross.wait_recv()
    for y in range(2):
        total = m_near[y, at.w].astype(F32) + m_x[y].astype(F32)
        m_x[y] = total.astype(BF16)
    along = remote(m_x.at[1 - at.y], m_y, ns.at[2], nr.at[2], side)
    along.start()
    z_send(1)
    qkv[:, : HEADS * HEAD_DIM] = dq_ref[...]
    along.wait_recv()
    moe_sum = m_x[at.y].astype(F32) + m_y[...].astype(F32)
    out_ref[...] = (sum_ref[...] + RES_MULT * moe_sum).astype(BF16)
    tok = tok_ref[...].astype(F32)
    scale = lax.rsqrt(jnp.mean(tok * tok, axis=1, keepdims=True) + EPS)
    normed = tok * scale
    gain_one = small_ref[pl.ds(EXPERTS, 1), :].astype(F32)
    for copy in third:
        copy.wait_recv()
    cosine = cos_ref[...]
    sine = -sin_ref[...]
    base = HEADS * HEAD_DIM
    for h in range(2):
        here = slice(h * rows, (h + 1) * rows)
        total = half_in[at.y, h, at.outer].astype(F32)
        for r in range(1, outers):
            total = total + z_in[r, h].astype(F32)
        qkv[here, base : base + width] = turn(total[:, :width], cosine[here], sine[here]).astype(BF16)
        qkv[here, base + width :] = total[:, width:].astype(BF16)
    wide = full * 2 // PLANE
    for j in range(PLANE):
        swap[j, :, :wide] = qkv[:, j * wide : (j + 1) * wide]
        swap[j, :, wide:] = da_ref[:, j * (D // PLANE) : (j + 1) * (D // PLANE)]
    swaps = []
    for slot, bits in enumerate(OTHERS):
        device, j_to = at.relative(*bits)
        copy = remote(swap.at[j_to], swapped.at[at.j], ws.at[slot], wr.at[slot], device)
        copy.start()
        swaps.append(copy)
    swapped[at.j] = swap[at.j]
    hidden_grad = dot_nt(qkv[...], wqkv_ref[...])
    small = rows_ref[...]
    gain_grad = jnp.sum(hidden_grad * normed, axis=0, keepdims=True)
    line = lax.broadcasted_iota(jnp.int32, small.shape, 0)
    small = jnp.where(line == EXPERTS, gain_grad, small)
    small = jnp.concatenate([small, jnp.zeros((128 - small.shape[0], D), F32)], axis=0)
    small_o[...] = small.T.astype(BF16)
    hidden_grad = hidden_grad * gain_one
    token_ref[...] = dy_ref[...] + scale * (
        hidden_grad - normed * jnp.mean(hidden_grad * normed, axis=1, keepdims=True)
    )
    for copy in swaps:
        copy.wait_recv()
    all_rows = PLANE * count
    grads = swapped[...].reshape(all_rows, wide + D // PLANE)
    attn_ref[:, :wide] = dot_tn(left_one[...], grads[:, :wide]).astype(BF16)
    attn_ref[:, wide:] = dot_tn(left_mixed[...], grads[:, wide:]).astype(BF16)
    for copy in list(first.values()) + second + third + swaps + [near, cross, along]:
        copy.wait_send()


def finish(part, moe, arrays, ctx_count):
    outers = ctx_count // INNER
    blocks, rows, full = part.shape
    count = 2 * rows
    shape = jax.ShapeDtypeStruct
    columns = 3 * D // PLANE
    return comm_call(
        functools.partial(finish_kernel, outers),
        [
            shape((count, D), BF16),
            shape((count, D), F32),
            shape((D, columns), BF16),
            shape((D, 128), BF16),
        ],
        [VMEM] * (2 + len(arrays)),
        [VMEM] * 4,
        [
            pltpu.VMEM((2, 2, outers, rows, full), BF16),
            pltpu.VMEM((2, outers, rows, full), BF16),
            pltpu.VMEM((outers, 2, rows, full), BF16),
            pltpu.VMEM((2, 2, count, D), BF16),
            pltpu.VMEM((2, count, D), BF16),
            pltpu.VMEM((count, D), BF16),
            pltpu.VMEM((count, 2 * full), BF16),
            pltpu.VMEM((PLANE, count, columns), BF16),
            pltpu.VMEM((PLANE, count, columns), BF16),
            DMA((2, 2, 2, outers)),
            DMA((2, 2, 2, outers)),
            DMA((2,)),
            DMA((2,)),
            DMA((2, outers)),
            DMA((2, outers)),
            DMA((3,)),
            DMA((3,)),
            DMA((7,)),
            DMA((7,)),
        ],
        3,
        "finish",
        vmem=62 * 2**20,
    )(part, moe.reshape(2, 2, 2, count, D), *arrays)


def experts_kernel(
    info,
    hid_ref,
    cot_ref,
    gate_ref,
    w1_ref,
    w2_ref,
    moe_ref,
    part_ref,
    pick_ref,
    give_ref,
    keep_ref,
    hid_t,
    cot_t,
    inner,
    gate_cols,
    pick_cols,
    moe_acc,
    part_acc,
    grad,
    act_kept,
):
    e = pl.program_id(0)
    tokens = hid_ref.shape[0]
    count = tokens // PLANE
    units = w2_ref.shape[-1]
    planes, rows = give_ref.shape[1:3]
    step_rows = 2 * count
    lane = lax.broadcasted_iota(jnp.int32, (step_rows, 128), 1)

    @pl.when(e == 0)
    def _():
        hid_t[...] = hid_ref[...].T
        cot_t[...] = cot_ref[...].T
        moe_acc[...] = jnp.zeros_like(moe_acc)
        part_acc[...] = jnp.zeros_like(part_acc)
        pick_cols[...] = jnp.zeros_like(pick_cols)
        for j in range(PLANE):
            block = jnp.concatenate(
                [gate_ref[j], jnp.zeros((128 - EXPERTS, count), F32)], axis=0
            )
            gate_cols[pl.ds(j * count, count), :] = block.T

    inner[...] = w1_ref[0].reshape(D, 2 * units)

    def forward(step, carry):
        here = pl.ds(pl.multiple_of(step * step_rows, step_rows), step_rows)
        gate = jnp.sum(
            jnp.where(lane == info[0] + e, gate_cols[here, :], 0.0), axis=1, keepdims=True
        )
        both = dot_nn(hid_ref[here, :], inner[...])
        gv, uv = both[:, :units], both[:, units:]
        back_act = RES_MULT * dot_nn(cot_ref[here, :], w2_ref[0])
        sig = jax.nn.sigmoid(gv)
        silu = gv * sig
        act = silu * uv
        pick = jnp.sum(act * back_act, axis=1, keepdims=True)
        pick_cols[here, :] = jnp.where(lane == e, pick, pick_cols[here, :])
        kept = (gate * act).astype(BF16)
        act_kept[here, :] = kept
        back_act = gate * back_act
        slope = sig * (1.0 + gv * (1.0 - sig))
        low = jnp.concatenate([back_act * uv * slope, back_act * silu], axis=1).astype(BF16)
        grad[here, :] = low
        part_acc[here, :] += dot_nt(low, inner[...])
        moe_acc[here, :] += dot_nt(kept, w2_ref[0])
        return carry

    lax.fori_loop(0, tokens // step_rows, forward, 0)

    def weights(step, carry):
        for ref, side in ((give_ref, 1 - info[1]), (keep_ref, info[1])):
            here = pl.ds(pl.multiple_of((2 * step + side) * rows, rows), rows)
            ref[0, step, :, : 2 * units] = dot_nn(hid_t[here, :], grad[...]).astype(BF16)
            ref[0, step, :, 2 * units :] = (RES_MULT * dot_nn(cot_t[here, :], act_kept[...])).astype(
                BF16
            )
        return carry

    lax.fori_loop(0, planes, weights, 0)

    @pl.when(e == OWN - 1)
    def _():
        moe_ref[...] = moe_acc[...].astype(BF16)
        part_ref[...] = part_acc[...].astype(BF16)
        for j in range(PLANE):
            pick_ref[j] = pick_cols[pl.ds(j * count, count), :].T[:8]


def experts(info, hidden, cot, gates, expert_in, expert_out, outers):
    tokens = hidden.shape[0]
    count = tokens // PLANE
    units = expert_out.shape[-1]
    rows = D // outers
    shape = jax.ShapeDtypeStruct

    def whole(dims):
        return pl.BlockSpec(dims, lambda e, info: (0,) * len(dims))

    grads = shape((OWN, outers // 2, rows, 3 * units), BF16)
    grad_spec = pl.BlockSpec((1,) + grads.shape[1:], lambda e, info: (e, 0, 0, 0))
    return pl.pallas_call(
        experts_kernel,
        out_shape=[
            shape((tokens, D), BF16),
            shape((tokens, D), BF16),
            shape((PLANE, 8, count), F32),
            grads,
            grads,
        ],
        grid_spec=pltpu.PrefetchScalarGridSpec(
            num_scalar_prefetch=1,
            grid=(OWN,),
            in_specs=[
                whole((tokens, D)),
                whole((tokens, D)),
                whole(gates.shape),
                pl.BlockSpec((1, D, 2, units), lambda e, info: (info[0] + e, 0, 0, 0)),
                pl.BlockSpec((1, D, units), lambda e, info: (info[0] + e, 0, 0)),
            ],
            out_specs=[
                whole((tokens, D)),
                whole((tokens, D)),
                whole((PLANE, 8, count)),
                grad_spec,
                grad_spec,
            ],
            scratch_shapes=[
                pltpu.VMEM((D, tokens), BF16),
                pltpu.VMEM((D, tokens), BF16),
                pltpu.VMEM((D, 2 * units), BF16),
                pltpu.VMEM((tokens, 128), F32),
                pltpu.VMEM((tokens, 128), F32),
                pltpu.VMEM((tokens, D), F32),
                pltpu.VMEM((tokens, D), F32),
                pltpu.VMEM((tokens, 2 * units), BF16),
                pltpu.VMEM((tokens, units), BF16),
            ],
        ),
        compiler_params=pltpu.CompilerParams(vmem_limit_bytes=60 * 2**20),
        cost_estimate=pl.CostEstimate(
            flops=20 * 2**30, bytes_accessed=32 * 2**20, transcendentals=2**20
        ),
        name="experts",
    )(info, hidden, cot, gates, expert_in, expert_out)


def rms_scale(values):
    return lax.rsqrt(jnp.mean(values * values, axis=-1, keepdims=True) + EPS)


def rotate(values, position, sign):
    half_dim = values.shape[-1] // 2
    frequency = jnp.exp(
        -jnp.log(jnp.float32(THETA))
        * jnp.arange(half_dim, dtype=jnp.float32)
        * (2.0 / values.shape[-1])
    )
    angles = position.astype(jnp.float32)[:, None] * frequency[None, :]
    cosine = jnp.cos(angles)[:, None, :]
    sine_part = sign * jnp.sin(angles)[:, None, :]
    lower_part = values[..., :half_dim]
    upper_part = values[..., half_dim:]
    return jnp.concatenate(
        [
            lower_part * cosine - upper_part * sine_part,
            upper_part * cosine + lower_part * sine_part,
        ],
        axis=-1,
    )


def body(
    tokens,
    w_query,
    w_key,
    w_value,
    w_output,
    attn_gain,
    w_router,
    expert_in,
    expert_out,
    moe_gain,
    segments,
    routes,
    priority,
    cotangent,
):
    ctx_count = lax.axis_size("ctx")
    ctx_index = lax.axis_index("ctx")
    devices = ctx_count * 2
    outers = ctx_count // INNER
    owner_rows = D // devices
    block_rows = tokens.shape[2]
    half_rows = block_rows * ctx_count
    tok_count = 2 * block_rows
    plane_rows = PLANE * tok_count
    group_size = HEADS // KV_HEADS
    kv_width = KV_HEADS * HEAD_DIM
    f32 = jnp.float32
    bf16 = jnp.bfloat16
    first_expert = (ctx_index % INNER) * OWN

    small = jnp.concatenate(
        [w_router.T, attn_gain[None], moe_gain[None], jnp.zeros((14, w_router.shape[0]), bf16)]
    )
    cot_own = cotangent.reshape(tok_count, D)
    plane_groups = [
        [base + member for member in range(PLANE)] for base in range(0, devices, PLANE)
    ]

    def gather_plane(block):
        return lax.all_gather(
            block, ("ctx", "wsh"), axis=0, tiled=True, axis_index_groups=plane_groups
        )

    qkv_w, small_all = gather_weights(w_query, w_key, w_value, small)
    output_w = lax.all_gather(w_output, "wsh", axis=0, tiled=True)
    cot_all = gather_plane(cot_own)
    small_all = small_all.transpose(1, 0, 2).reshape(32, D)
    router_t = small_all[:EXPERTS]
    gain_one_f = small_all[EXPERTS].astype(f32)
    gain_two_f = small_all[EXPERTS + 1].astype(f32)

    token_rows = tokens.reshape(tok_count, D).astype(f32)
    scale_one = rms_scale(token_rows)
    normed_one = token_rows * scale_one
    hidden_one = (normed_one * gain_one_f).astype(bf16)
    qkv_lin = jnp.dot(hidden_one, qkv_w, preferred_element_type=f32)
    block_total = 2 * ctx_count
    block_ids = jnp.stack([ctx_index, block_total - 1 - ctx_index])
    query_pos = block_ids[:, None] * block_rows + jnp.arange(block_rows, dtype=jnp.int32)[None, :]
    flat_pos = query_pos.reshape(tok_count)
    segment_ids = segments[0]
    query_seg = jnp.stack(
        [
            lax.dynamic_slice_in_dim(segment_ids, block_ids[half] * block_rows, block_rows)
            for half in range(2)
        ]
    )
    query_start = jnp.sum(
        (segment_ids[None, None, :] < query_seg[:, :, None]).astype(jnp.int32), axis=-1
    )
    info = jnp.concatenate(
        [
            query_start[:, 0] // CHUNK,
            ((block_ids + 1) * block_rows + CHUNK - 1) // CHUNK,
            block_ids * block_rows,
            jnp.zeros((2,), jnp.int32),
        ]
    )
    start_cols = query_start.reshape(tok_count, 1)
    start_rows = jnp.tile(query_start, (1, 4))
    frequency = jnp.exp(
        -jnp.log(jnp.float32(THETA))
        * jnp.arange(HEAD_DIM // 2, dtype=jnp.float32)
        * (2.0 / HEAD_DIM)
    )
    angles = flat_pos.astype(f32)[:, None] * frequency[None, :]
    cosine, sine = jnp.cos(angles), jnp.sin(angles)
    cosine = jnp.concatenate([cosine] * 4, axis=1)
    sine = jnp.concatenate([-sine, sine] * 2, axis=1)
    rot_query = rotate(qkv_lin[:, :1024].reshape(tok_count, HEADS, HEAD_DIM), flat_pos, 1.0)
    rot_key = rotate(qkv_lin[:, 1024:1536].reshape(tok_count, KV_HEADS, HEAD_DIM), flat_pos, 1.0)
    queries = rot_query.astype(bf16).reshape(tok_count, HEADS * HEAD_DIM)
    kv_own = jnp.concatenate(
        [rot_key.astype(bf16).reshape(tok_count, kv_width), qkv_lin[:, 1536:].astype(bf16)], axis=1
    ).reshape(2, block_rows, 2 * kv_width)
    kv_all = kv_gather(kv_own, ctx_count).reshape(block_total * block_rows, 2 * kv_width)
    token_low = tokens.reshape(tok_count, D)
    attn_raw, attn_total, mixed, first_sum, hidden_two, gate, kept = attend(
        info,
        queries,
        kv_all,
        start_cols,
        token_low,
        output_w,
        small_all,
        routes.reshape(tok_count, TOPK).T,
        priority.reshape(tok_count, TOPK).T,
    )

    hidden_all, gates_all = plane_gather([hidden_two, gate * kept], 4, "gather_hidden")
    left_one = gather_plane(hidden_one)
    left_mixed = gather_plane(mixed)
    outer_index = ctx_index // INNER
    moe_part, hidden_part, picks, give, keep = experts(
        jnp.stack([first_expert, outer_index % 2]).astype(jnp.int32),
        hidden_all.reshape(plane_rows, D),
        cot_all,
        gates_all,
        expert_in,
        expert_out,
        outers,
    )

    def exchange(rows, bit):
        pairs = [(member, member ^ (bit * INNER)) for member in range(ctx_count)]
        return lax.ppermute(rows, "ctx", pairs)

    def halve(total, bit):
        side = (outer_index // bit) % 2
        split = total.reshape(total.shape[0], total.shape[1] // 2, 2, *total.shape[2:])
        return [
            lax.dynamic_index_in_dim(split, which, 2, keepdims=False) for which in (1 - side, side)
        ]

    def add(kept_rows, arrived):
        return (kept_rows.astype(f32) + arrived.astype(f32)).astype(bf16)

    portions = [slice(0, OWN // 2), slice(OWN // 2, OWN)]
    arrived = [exchange(give[portion], 1) for portion in portions]
    kept_rows = [keep[portion] for portion in portions]
    hidden_grad, picks_all = plane_reduce(
        [hidden_part.reshape(PLANE, tok_count, D)], picks, 5, "reduce_hidden"
    )
    first_grad, attn_grad, query_lin_grad, kv_terms, small_rows = back(
        info,
        hidden_grad,
        picks_all,
        gate,
        kept,
        small_all,
        first_sum,
        cot_own,
        output_w,
        attn_raw,
        attn_total,
        queries,
        kv_all,
        start_rows,
        cosine,
        sine,
    )
    bit = 2
    while bit < outers:
        if bit == 2:
            arrived[0], kv_terms = lax.optimization_barrier((arrived[0], kv_terms))
        for member in range(2):
            total = add(kept_rows[member], arrived[member])
            given, kept_rows[member] = halve(total, bit)
            if bit == 2 and member == 0:
                given, kv_terms = lax.optimization_barrier((given, kv_terms))
            arrived[member] = exchange(given, bit)
        bit *= 2
    output, token_grad, attn_part, small_part = finish(
        kv_terms.reshape(block_total, block_rows, 2 * kv_width),
        moe_part,
        [
            first_sum,
            query_lin_grad,
            attn_grad,
            first_grad,
            token_low,
            small_all,
            cosine,
            sine,
            qkv_w,
            left_one,
            left_mixed,
            small_rows,
        ],
        ctx_count,
    )
    near = jnp.concatenate(
        [add(kept_rows[member], arrived[member]) for member in range(2)], axis=0
    ).reshape(OWN, PLANE, owner_rows, -1)
    attn_in, small_in, near_in = owners([attn_part, small_part], [near], devices, 7, "owners")
    hidden_units = expert_out.shape[-1]
    qkv_cols = 2048 // PLANE
    attn_sum = jnp.sum(
        attn_in.astype(f32).reshape(outers, PLANE, owner_rows, 3 * D // PLANE), axis=0
    ).transpose(1, 0, 2)
    qkv_sum = attn_sum[:, :, :qkv_cols].reshape(owner_rows, 2048)
    output_sum = attn_sum[:, :, qkv_cols:].reshape(owner_rows, D)
    near_in = near_in.astype(f32)
    inner_sum = (
        near_in[..., : 2 * hidden_units]
        .reshape(INNER, 2, OWN, owner_rows, 2, hidden_units)
        .transpose(0, 2, 3, 4, 1, 5)
        .reshape(EXPERTS, owner_rows, 2, 2 * hidden_units)
    )
    outer_sum = (
        near_in[..., 2 * hidden_units :]
        .reshape(INNER, 2, OWN, owner_rows, hidden_units)
        .transpose(0, 2, 3, 1, 4)
        .reshape(EXPERTS, owner_rows, 2 * hidden_units)
    )
    small_sum = jnp.sum(small_in.astype(f32), axis=0)
    return (
        output.reshape(tokens.shape),
        token_grad.reshape(tokens.shape),
        qkv_sum[:, :1024],
        qkv_sum[:, 1024:1536],
        qkv_sum[:, 1536:],
        output_sum,
        small_sum[:, EXPERTS],
        small_sum[:, :EXPERTS],
        inner_sum,
        outer_sum,
        small_sum[:, EXPERTS + 1],
    )


def solution(mesh):
    placed = (
        P("wsh", None, "ctx", None),
        P("wsh", None),
        P("wsh", None),
        P("wsh", None),
        P("wsh", None),
        P("wsh"),
        P("wsh", None),
        P(None, None, None, "wsh"),
        P(None, None, "wsh"),
        P("wsh"),
        P("wsh", None),
        P("wsh", None, "ctx", None),
        P("wsh", None, "ctx", None),
        P("wsh", None, "ctx", None),
    )
    return jax.shard_map(
        body,
        mesh=mesh,
        in_specs=placed,
        out_specs=(
            P("wsh", None, "ctx", None),
            P("wsh", None, "ctx", None),
            P(("ctx", "wsh"), None),
            P(("ctx", "wsh"), None),
            P(("ctx", "wsh"), None),
            P(("ctx", "wsh"), None),
            P(("ctx", "wsh")),
            P(("ctx", "wsh"), None),
            P(None, ("ctx", "wsh"), None, None),
            P(None, ("ctx", "wsh"), None),
            P(("ctx", "wsh")),
        ),
        check_vma=False,
    )
```

time: 753 us -> 443 us (0.59)
  the two profiles are of different devices: /device:TPU:31 before, /device:TPU:0 now
where the time goes in v2:
time: 443 us; the launch traced here: 442 us
  Pallas kernels  331 us (75%)
  local copies, waits for them, and re-layouts  36.8 us (8%)
  waiting for transfers between devices  34.8 us (8%)
  other arithmetic  15 us (3%)
  between operations  14.2 us (3%)
  starting transfers between devices  6.96 us (2%)
    pallas_call x1, Pallas kernels, finish(): comm_call(functools.partial(finish_kernel, outers), [shape((count, D), BF...  101 us
    pallas_call x1, Pallas kernels, gather_weights(): comm_call(weights_kernel, [shape((D, 2048), BF16), shape((2,) + small.sha...  45.2 us
    pallas_call x1, Pallas kernels, kv_gather(): comm_call(functools.partial(kv_gather_kernel, outers), jax.ShapeDtypeStru...  42.3 us
    pallas_call x1, Pallas kernels, owners(): comm_call(functools.partial(owners_kernel, devices, count, near_count), s...  41.3 us
    pallas_call x1, Pallas kernels, experts(): pl.pallas_call(experts_kernel, out_shape=[shape((tokens, D), BF16), shape...  40.7 us
    ppermute x4, waiting for transfers between devices, exchange(): return lax.ppermute(rows, 'ctx', pairs)  33.4 us
    pallas_call x1, Pallas kernels, plane_reduce(): comm_call(functools.partial(plane_reduce_kernel, count), [shape((rows, wi...  20.6 us
    pallas_call x1, Pallas kernels, plane_gather(): comm_call(functools.partial(plane_gather_kernel, count), [jax.ShapeDtypeS...  18.9 us
  transfers between devices with their start and end apart: 8, of which 2 were waited for; matrix products, arithmetic and copies ran while one was open for 6% of the time, Pallas kernels for 66%

profile of v2, /device:TPU:0, one launch (start us, length us, event | category | flops | bytes accessed | tf_op | source)
XLA Modules:
  0.0 442.1 jit_solution(408838078028239732)
XLA Ops:
  7.3 0.7 all-gather.5.cloned.1.call-update
  8.0 0.7 all-gather.7.cloned.1.call-update
  8.7 0.7 broadcast_in_dim.6
  9.4 0.7 broadcast_in_dim.7
  10.1 1.1 multiply_reduce_fusion
  11.5 1.0 copy-done.3
  12.5 45.2 %gather_weights.1 = (bf16[1024,2048]{1,0:T(8,128)(2,1)S(1)}, bf16[2,32,512]{2,1,0:T(8,128)(2,1)S(1)}) custom-call(bf16[512,1024]{1,0:T(8,128)(2,1)S(1)} %copy-done.1, bf16[512,512]{1,0:T(8,128)(2,1)S(1)} %copy-done.2, bf16[512,512]{1,0:T(8,128)(2,1)S(1)} %copy-done.3, bf16[32,512]{1,0:T(8,128)(2,1)S(1)} %maximum_maximum_fusion.small), custom_call_target="tpu_custom_call" | custom-call | tf_op jit(solution)/shard_map/gather_weights/pallas_call | solution.py:202
  57.7 1.9 copy-done
  59.7 0.8 multiply_convert_fusion
  60.6 3.0 fusion.3
  63.7 0.6 copy-done.15
  64.4 0.3 convert_reduce_fusion.1
  64.7 0.8 reshape.264.start_ref
  65.7 0.3 fusion
  66.2 0.1 copy.102
  66.4 0.1 reshape.263
  66.6 0.2 copy.117
  66.7 0.7 pad_maximum_fusion.2.own
  67.5 42.3 %kv_gather.1 = bf16[32,64,1024]{2,1,0:T(8,128)(2,1)} custom-call(bf16[2,64,1024]{2,1,0:T(8,128)(2,1)} %pad_maximum_fusion.2.own), custom_call_target="tpu_custom_call" | custom-call | tf_op jit(solution)/shard_map/kv_gather/pallas_call | solution.py:272
  109.8 0.2 copy.98
  110.1 0.9 copy.109.q_ref
  111.0 0.6 copy.118
  111.6 0.7 reshape.243
  112.3 0.7 reshape.244
  113.0 0.6 pad_add_fusion.1.info
  113.6 0.1 slice_reduce_fusion.2
  113.8 0.6 pad_add_fusion.3.info
  114.4 8.1 %attend.1 = (f32[128,1024]{1,0:T(8,128)}, f32[128,1024]{1,0:T(8,128)}, bf16[128,1024]{1,0:T(8,128)(2,1)}, f32[128,1024]{1,0:T(8,128)}, bf16[128,1024]{1,0:T(8,12...) custom-call(s32[8]{0:T(128)} %pad_add_fusion.3.info, bf16[128,1024]{1,0:T(8,128)(2,1)} %copy.109.q_ref, ...), custom_call_target="tpu_custom_call" | custom-call | flops 4294967296 | bytes 16777216 | tf_op jit(solution)/shard_map/attend/pallas_call | solution.py:624
  122.5 1.3 mul.175.refs_1_
  123.8 18.9 %gather_hidden.1 = (bf16[8,128,1024]{2,1,0:T(8,128)(2,1)}, f32[8,16,128]{2,1,0:T(8,128)}) custom-call(bf16[128,1024]{1,0:T(8,128)(2,1)} %get-tuple-element.47.refs_0_, f32[16,128]{1,0:T(8,128)} %mul.175.refs_1_), custom_call_target="tpu_custom_call" | custom-call | tf_op jit(solution)/shard_map/gather_hidden/pallas_call | solution.py:145
  142.8 40.7 %experts.1 = (bf16[1024,1024]{1,0:T(8,128)(2,1)}, bf16[1024,1024]{1,0:T(8,128)(2,1)}, f32[8,8,128]{2,1,0:T(8,128)}, bf16[4,2,256,768]{3,2,1,0:T(8,128)(2,1)}, bf16[4,2,256,768]{3,2,1,0:T(8,128)(2,1)}) custom-call(s32[2]{0:T(128)} %pad_add_fusion.1.info, bf16[1024,1024]{1,0:T(8,128)(2,1)} %bitcast.87, ...), custom_call_target="tpu_custom_call" | custom-call | flops 21474836480 | bytes 33554432 | tf_op jit(solution)/shard_map/experts/pallas_call | solution.py:1096
  183.6 3.8 fusion.1
  187.3 1.5 collective-permute-start
  188.9 0.5 collective-permute-start.2
  189.4 0.7 tile.10.start_ref
  190.0 0.8 pad_maximum_fusion.4
  190.9 20.6 %reduce_hidden.1 = (f32[128,1024]{1,0:T(8,128)}, f32[8,8,128]{2,1,0:T(8,128)}) custom-call(bf16[2,2,2,128,1024]{4,3,2,1,0:T(8,128)(2,1)} %bitcast.63, f32[8,8,128]{2,1,0:T(8,128)} %get-tuple-element.55.refs_1_), custom_call_target="tpu_custom_call" | custom-call | tf_op jit(solution)/shard_map/reduce_hidden/pallas_call | solution.py:338
  211.5 13.1 %back.1 = (f32[128,1024]{1,0:T(8,128)}, bf16[128,1024]{1,0:T(8,128)(2,1)}, bf16[128,1024]{1,0:T(8,128)(2,1)}, bf16[2048,1024]{1,0:T(8,128)(2,1)}, f32[32,1024]{1,0:T(8,128)}) custom-call(s32[8]{0:T(128)} %pad_add_fusion.3.info, f32[128,1024]{1,0:T(8,128)} %get-tuple-element.56.hg_ref, f32[8,8,128]{2,1,0:T(8,128)} %get-tuple-element.57.pick_ref, ...), custom_call_target="tpu_custom_call" | custom-call | flops 8589934592 | bytes 16777216 | tf_op jit(solution)/shard_map/back/pallas_call | solution.py:754
  224.5 0.2 collective-permute-done
  224.8 33.1 %collective-permute-done.2 = bf16[2,2,256,768]{3,2,1,0:T(8,128)(2,1)S(1)} collective-permute-done((bf16[2,2,256,768]{3,2,1,0:T(8,128)(2,1)}, bf16[2,2,256,768]{3,2,1,0:T(8,128)(2,1)S(1)}, u32[]{:S(2)}, u32[]{:S(2)}) %collective-permute-start.2) | collective-permute-done | bytes 1572896 | tf_op jit(solution)/shard_map/ppermute | solution.py:1293
  257.9 1.2 copy-done.9
  259.1 3.6 add_convert_fusion
  262.7 1.1 constant_dynamic-slice_fusion.1
  263.8 4.8 %collective-permute-start.1 = (bf16[2,1,256,768]{3,2,1,0:T(8,128)(2,1)}, bf16[2,1,256,768]{3,2,1,0:T(8,128)(2,1)}, u32[]{:S(2)}, u32[]{:S(2)}) collective-permute-start(bf16[2,1,256,768]{3,2,1,0:T(8,128)(2,1)} %constant_dynamic-slice_fusion.1), channel_id=1, source_target_pairs={{0,16},{2,18},{4,20},{6,22},{8,24},{10,26},{12,28},{14,30},{16,0},... | collective-permute-start | bytes 2359304 | tf_op jit(solution)/shard_map/ppermute | solution.py:1293
  268.5 0.9 constant_dynamic-slice_fusion
  269.5 101.0 %finish.1 = (bf16[128,1024]{1,0:T(8,128)(2,1)}, f32[128,1024]{1,0:T(8,128)}, bf16[1024,384]{1,0:T(8,128)(2,1)}, bf16[1024,128]{1,0:T(8,128)(2,1)}) custom-call(bf16[32,64,1024]{2,1,0:T(8,128)(2,1)} %bitcast.60, bf16[2,2,2,128,1024]{4,3,2,1,0:T(8,128)(2,1)} %bitcast.65, f32[128,1024]{1,0:T(8,128)} %get-tuple-element.58.sum_ref, ...), custom_call_target="tpu_custom_call" | custom-call | tf_op jit(solution)/shard_map/finish/pallas_call | solution.py:958
  370.5 1.6 add_convert_fusion.3
  372.1 1.3 add_convert_fusion.2
  373.4 1.3 pad_maximum_fusion
  374.7 41.3 %owners.1 = (bf16[32,32,384]{2,1,0:T(8,128)(2,1)}, bf16[32,32,128]{2,1,0:T(8,128)(2,1)}, bf16[8,4,32,768]{3,2,1,0:T(8,128)(2,1)}) custom-call(bf16[1024,384]{1,0:T(8,128)(2,1)} %get-tuple-element.73.refs_0_, bf16[1024,128]{1,0:T(8,128)(2,1)} %get-tuple-element.74.refs_1_, bf16[4,8,32,768]{3,2,1,0:T(8,128)(2,1)} %bitcast.56), custom_call_target="tpu_custom_call" | custom-call | tf_op jit(solution)/shard_map/owners/pallas_call | solution.py:437
  416.0 1.6 slice.109
  417.9 1.0 copy-done.10
  419.0 0.7 fusion.2
  419.7 0.7 slice.103
  420.4 0.7 copy_bitcast_fusion
  421.0 2.3 reshape.256
  423.4 3.2 copy.114
  426.6 3.4 reshape.257
  430.0 0.8 copy.115
  430.8 1.8 reshape.259
  432.7 0.7 slice_reduce_fusion
  433.4 0.7 copy.116
  434.1 0.7 copy.124
  434.8 0.8 copy.125
  (76 shorter events, 1.7 us)
Async XLA Ops:
  7.2 4.2 copy-start.14
  7.2 4.3 copy-start.1
  7.2 4.3 copy-start.2
  7.2 107.2 %all-gather.5.cloned.1.call-start = ((), (), s32[]{:S(2)}) async-start(), calls=%async_computation | async-start | bytes 3145728 | tf_op jit(solution)/shard_map/all_gather | solution.py:1212
  7.9 134.9 %all-gather.7.cloned.1.call-start = ((), (), s32[]{:S(2)}) async-start(), calls=%async_computation.1 | async-start | bytes 2359296 | tf_op jit(solution)/shard_map/all_gather | solution.py:1207
  8.7 260.8 %all-gather.9.cloned.1.call-start = ((), (), s32[]{:S(2)}) async-start(), calls=%async_computation.2 | async-start | bytes 2359296 | tf_op jit(solution)/shard_map/all_gather | solution.py:1207
  11.5 1.0 copy-start.3
  12.5 47.2 %copy-start.7 = (bf16[1,2,64,1024]{3,2,1,0:T(8,128)(2,1)S(1)}, bf16[1,2,64,1024]{3,2,1,0:T(8,128)(2,1)}, u32[]{:S(2)}) copy-start(bf16[1,2,64,1024]{3,2,1,0:T(8,128)(2,1)} %param.14) | copy-start | bytes 786436
  57.7 2.0 copy-start
  60.6 208.9 %all-gather.11.cloned.1.call-start = ((), (), s32[]{:S(2)}) async-start(), calls=%async_computation.3 | async-start | bytes 2359296 | tf_op jit(solution)/shard_map/all_gather | solution.py:1207
  63.6 2.8 copy-start.6
  63.6 0.7 copy-start.15
  67.4 42.3 %slice-start = ((f32[128,2048]{1,0:T(8,128)}), f32[128,1024]{1,0:T(8,128)S(1)}, s32[]{:S(2)}) async-start(f32[128,2048]{1,0:T(8,128)} %copy-done.6), calls=%async_computation.4 | async-start | bytes 1048576 | tf_op jit(solution)/shard_map/slice | solution.py:1257
  109.8 1.8 copy-start.16
  109.8 2.5 copy-start.17
  187.3 37.4 %collective-permute-start = (bf16[2,2,256,768]{3,2,1,0:T(8,128)(2,1)}, bf16[2,2,256,768]{3,2,1,0:T(8,128)(2,1)S(1)}, u32[]{:S(2)}, u32[]{:S(2)}) collective-permute-start(bf16[2,2,256,768]{3,2,1,0:T(8,128)(2,1)} %get-tuple-element.128), channel_id=1, source_target_pairs={{0,8},{2,10},{4,12},{6,14},{8,0},{10,2},{12,4},{14,6},{16,24},{18,... | collective-permute-start | bytes 4718600 | tf_op jit(solution)/shard_map/ppermute | solution.py:1293
  188.9 69.0 %collective-permute-start.2 = (bf16[2,2,256,768]{3,2,1,0:T(8,128)(2,1)}, bf16[2,2,256,768]{3,2,1,0:T(8,128)(2,1)S(1)}, u32[]{:S(2)}, u32[]{:S(2)}) collective-permute-start(bf16[2,2,256,768]{3,2,1,0:T(8,128)(2,1)} %get-tuple-element.127), channel_id=1, source_target_pairs={{0,8},{2,10},{4,12},{6,14},{8,0},{10,2},{12,4},{14,6},{16,24},{18,... | collective-permute-start | bytes 4718600 | tf_op jit(solution)/shard_map/ppermute | solution.py:1293
  224.8 33.2 %copy-start.8 = (bf16[2,2,256,768]{3,2,1,0:T(8,128)(2,1)}, bf16[2,2,256,768]{3,2,1,0:T(8,128)(2,1)S(1)}, u32[]{:S(2)}) copy-start(bf16[2,2,256,768]{3,2,1,0:T(8,128)(2,1)S(1)} %collective-permute-done) | copy-start | bytes 4718596
  257.9 1.2 copy-start.9
  262.7 6.8 %copy-start.4 = (bf16[2,2,256,768]{3,2,1,0:T(8,128)(2,1)}, bf16[2,2,256,768]{3,2,1,0:T(8,128)(2,1)S(1)}, u32[]{:S(2)}) copy-start(bf16[2,2,256,768]{3,2,1,0:T(8,128)(2,1)S(1)} %get-tuple-element.126) | copy-start | bytes 4718596
  263.8 106.7 %collective-permute-start.1 = (bf16[2,1,256,768]{3,2,1,0:T(8,128)(2,1)}, bf16[2,1,256,768]{3,2,1,0:T(8,128)(2,1)}, u32[]{:S(2)}, u32[]{:S(2)}) collective-permute-start(bf16[2,1,256,768]{3,2,1,0:T(8,128)(2,1)} %constant_dynamic-slice_fusion.1), channel_id=1, source_target_pairs={{0,16},{2,18},{4,20},{6,22},{8,24},{10,26},{12,28},{14,30},{16,0},... | collective-permute-start | bytes 2359304 | tf_op jit(solution)/shard_map/ppermute | solution.py:1293
  269.5 102.6 %collective-permute-start.3 = (bf16[2,1,256,768]{3,2,1,0:T(8,128)(2,1)}, bf16[2,1,256,768]{3,2,1,0:T(8,128)(2,1)}, u32[]{:S(2)}, u32[]{:S(2)}) collective-permute-start(bf16[2,1,256,768]{3,2,1,0:T(8,128)(2,1)} %constant_dynamic-slice_fusion), channel_id=1, source_target_pairs={{0,16},{2,18},{4,20},{6,22},{8,24},{10,26},{12,28},{14,30},{16,0},... | collective-permute-start | bytes 2359304 | tf_op jit(solution)/shard_map/ppermute | solution.py:1293
  416.0 1.7 copy-start.5
  417.7 1.1 copy-start.10
  430.8 1.8 copy-start.13
  430.8 3.3 copy-start.12
  430.8 3.9 copy-start.11
Sparse Core Ops, SparseCore 0:
  9.6 53.0 all-gather.4
  64.6 37.0 all-gather.6
  104.1 26.0 all-gather.8
  142.9 29.7 all-gather.10

commit v3 on v2

v3 whole, which is shorter than its diff:
```python
import functools

import jax
import jax.numpy as jnp
from jax import lax
from jax.experimental import pallas as pl
from jax.experimental.pallas import tpu as pltpu
from jax.sharding import PartitionSpec as P

D = 1024
HEADS = 16
KV_HEADS = 8
HEAD_DIM = 64
TOPK = 8
EXPERTS = 16
CAP = 80
PLANE = 8
INNER = 4
OWN = EXPERTS // INNER
FIRST = OWN // 2


RES_MULT = 0.22
ATT_MULT = 0.015625
EPS = 1e-06
THETA = 10000.0

MESH = pl.DeviceIdType.MESH
F32 = jnp.float32
BF16 = jnp.bfloat16
ANY = pl.BlockSpec(memory_space=pl.ANY)
VMEM = pl.BlockSpec(memory_space=pltpu.VMEM)


class Place:
    def __init__(self):
        self.c = lax.axis_index("ctx")
        self.w = lax.axis_index("wsh")
        self.core = self.c % 2
        self.y = (self.c // 2) % 2
        self.inner = self.c % INNER
        self.outer = self.c // INNER
        self.z = self.outer % 2
        self.q = self.z * 2 + self.core
        self.j = self.q * 2 + self.w
        self.beside = (self.c + 2 - 4 * self.y, self.w)

    def relative(self, dz, dc, dw):
        z = self.z + dz * (1 - 2 * self.z)
        core = self.core + dc * (1 - 2 * self.core)
        w = self.w + dw * (1 - 2 * self.w)
        ctx = self.c + INNER * (z - self.z) + core - self.core
        return (ctx, w), (z * 2 + core) * 2 + w


OTHERS = [(a, b, d) for a in range(2) for b in range(2) for d in range(2) if a + b + d]
XY = [(0, 0, 1), (1, 0, 0), (1, 0, 1)]


def meet(devices):
    barrier = pltpu.get_barrier_semaphore()
    for device in devices:
        pl.semaphore_signal(barrier, inc=1, device_id=device, device_id_type=MESH)
    pl.semaphore_wait(barrier, len(devices))


def remote(src, dst, send, recv, device):
    return pltpu.make_async_remote_copy(
        src_ref=src,
        dst_ref=dst,
        send_sem=send,
        recv_sem=recv,
        device_id=device,
        device_id_type=MESH,
    )


def comm_call(kernel, out_shape, in_specs, out_specs, scratch, ident, name, vmem=None, us=20):
    return pl.pallas_call(
        kernel,
        out_shape=out_shape,
        in_specs=in_specs,
        out_specs=out_specs,
        scratch_shapes=scratch,
        compiler_params=pltpu.CompilerParams(
            collective_id=ident, has_side_effects=True, vmem_limit_bytes=vmem
        ),
        cost_estimate=pl.CostEstimate(
            flops=us * 10**9, bytes_accessed=us * 3 * 2**20, transcendentals=0
        ),
        name=name,
    )


DMA = pltpu.SemaphoreType.DMA


def room(arrays, scratch=(), spare=12):
    total = 0
    for array in list(arrays) + list(scratch):
        inner = getattr(array, "inner_aval", array)
        size = jnp.dtype(inner.dtype).itemsize
        for extent in inner.shape:
            size *= extent
        total += size
    return min(total + spare * 2**20, 62 * 2**20)


class Halving:
    def __init__(self, at, outers, sums, arrived, send, recv):
        self.at, self.sums, self.arrived = at, sums, arrived
        self.send, self.recv = send, recv
        self.bits = [2**k for k in range(1, outers.bit_length() - 1)]
        self.levels = [(0, outers // 2)]
        for bit in self.bits:
            start, many = self.levels[-1]
            self.levels.append((start + many, many // 2))
        self.copies = []

    def device(self, bit):
        at = self.at
        return (at.c + INNER * bit * (1 - 2 * ((at.outer // bit) % 2)), at.w)

    def start(self, step):
        bit = self.bits[step]
        side = (self.at.outer // bit) % 2
        start, many = self.levels[step]
        for m in range(many // 2):
            copy = remote(
                self.sums.at[start + 2 * m + 1 - side],
                self.arrived.at[start + m],
                self.send.at[start + m],
                self.recv.at[start + m],
                self.device(bit),
            )
            copy.start()
            self.copies.append(copy)

    def add(self, step):
        side = (self.at.outer // self.bits[step]) % 2
        start, many = self.levels[step]
        after, half = self.levels[step + 1]
        for m in range(half):
            self.copies[len(self.copies) - half + m].wait_recv()
            total = self.sums[start + 2 * m + side].astype(F32) + self.arrived[start + m].astype(F32)
            self.sums[after + m] = total.astype(BF16)

    def finish(self):
        for step in range(len(self.bits)):
            if step > 0:
                self.start(step)
            self.add(step)
        for copy in self.copies:
            copy.wait_send()
        return self.sums[self.levels[-1][0]]


def gather_start(at, pairs, send, recv, local):
    copies = []
    for index, (src, dst) in enumerate(pairs):
        keep = pltpu.make_async_copy(src, dst.at[at.j], local.at[index])
        keep.start()
        sends = []
        for slot, bits in enumerate(XY + [(0, 1, 0)]):
            device, unused = at.relative(*bits)
            copy = remote(src, dst.at[at.j], send.at[index, slot], recv.at[index, slot], device)
            copy.start()
            sends.append(copy)
        copies.append((keep, sends))
    return copies


def gather_pass(at, pairs, copies, send, recv):
    sib, unused = at.relative(0, 1, 0)
    passed = []
    for slot, bits in enumerate(XY):
        unused, j_from = at.relative(*bits)
        for index, (src, dst) in enumerate(pairs):
            copies[index][1][slot].wait_recv()
            block = dst.at[j_from]
            copy = remote(
                block, block, send.at[index, 4 + slot], recv.at[index, 4 + slot], sib
            )
            copy.start()
            passed.append(copy)
    return passed


def gather_wait(copies, passed):
    for keep, sends in copies:
        keep.wait()
        sends[3].wait_recv()
        for copy in sends:
            copy.wait_send()
    for copy in passed:
        copy.wait()


def turn(values, cosine, sine):
    lane = lax.broadcasted_iota(jnp.int32, cosine.shape, 1)
    first = lane % HEAD_DIM < HEAD_DIM // 2
    blocks = []
    for start in range(0, values.shape[1], 128):
        u = values[:, start : start + 128]
        swapped = jnp.where(first, pltpu.roll(u, 96, 1), pltpu.roll(u, 32, 1))
        blocks.append(u * cosine + swapped * sine)
    return jnp.concatenate(blocks, axis=1)


def dot_nt(a, b):
    return lax.dot_general(a, b, (((1,), (1,)), ((), ())), preferred_element_type=F32)


def dot_tn(a, b):
    return lax.dot_general(a, b, (((0,), (0,)), ((), ())), preferred_element_type=F32)


def dot_nn(a, b):
    return jnp.dot(a, b, preferred_element_type=F32)


def owners_kernel(devices, count, near_count, *refs):
    total = count + near_count
    parts, nears = refs[:count], refs[count:total]
    outs, near_outs = refs[total : total + count], refs[total + count : 2 * total]
    send, recv, local, nsend, nrecv, nlocal = refs[2 * total :]
    at = Place()
    me = at.c * 2 + at.w
    rows = D // devices

    def device_of(r):
        index = lax.rem(me + r, devices)
        return index, (index // 2, lax.rem(index, 2))

    def rows_of(ref, index):
        return ref.at[pl.ds(pl.multiple_of(index * rows, rows), rows), :]

    barrier = pltpu.get_barrier_semaphore()

    def greet(r, carry):
        unused, device = device_of(r)
        pl.semaphore_signal(barrier, inc=1, device_id=device, device_id_type=MESH)
        return carry

    lax.fori_loop(1, devices, greet, 0)
    pl.semaphore_wait(barrier, devices - 1)

    def copy_of(k, r):
        index, device = device_of(r)
        return remote(rows_of(parts[k], index), outs[k].at[me], send.at[k, r], recv.at[k, r], device)

    def start(r, carry):
        for k in range(count):
            copy_of(k, r).start()
        return carry

    lax.fori_loop(1, devices, start, 0)

    near_copies = []
    for k in range(near_count):
        for slot, bits in enumerate(OTHERS):
            device, j_to = at.relative(*bits)
            copy = remote(
                nears[k].at[:, j_to], near_outs[k].at[at.j], nsend.at[k, slot], nrecv.at[k, slot], device
            )
            copy.start()
            near_copies.append(copy)
    keeps = []
    for k in range(count):
        keep = pltpu.make_async_copy(rows_of(parts[k], me), outs[k].at[me], local.at[k])
        keep.start()
        keeps.append(keep)
    for k in range(near_count):
        keep = pltpu.make_async_copy(nears[k].at[:, at.j], near_outs[k].at[at.j], nlocal.at[k])
        keep.start()
        keeps.append(keep)

    def finish(r, carry):
        for k in range(count):
            copy_of(k, r).wait()
        return carry

    lax.fori_loop(1, devices, finish, 0)
    for copy in near_copies:
        copy.wait()
    for keep in keeps:
        keep.wait()


def owners(parts, nears, devices, ident, name):
    count, near_count = len(parts), len(nears)
    rows = D // devices
    shape = jax.ShapeDtypeStruct
    shapes = [shape((devices, rows, part.shape[-1]), part.dtype) for part in parts]
    for near in nears:
        lead, members, near_rows, width = near.shape
        shapes.append(shape((members, lead, near_rows, width), near.dtype))
    return comm_call(
        functools.partial(owners_kernel, devices, count, near_count),
        shapes,
        [ANY] * (count + near_count),
        [VMEM] * (count + near_count),
        [
            DMA((count, devices)),
            DMA((count, devices)),
            DMA((count,)),
            DMA((near_count, 7)),
            DMA((near_count, 7)),
            DMA((near_count,)),
        ],
        ident,
        name,
        vmem=60 * 2**20,
    )(*parts, *nears)


CHUNK = 256
PAIRS = KV_HEADS // 2
NEVER = -1e30


def low_lanes(shape):
    return lax.broadcasted_iota(jnp.int32, shape, 1) < HEAD_DIM


def spread(block):
    a, b = block[:, :128], block[:, 128:]
    low = low_lanes(a.shape)
    zero = jnp.zeros_like(a)
    return jnp.concatenate(
        [
            jnp.where(low, a, zero),
            jnp.where(low, pltpu.roll(a, HEAD_DIM, 1), zero),
            jnp.where(low, zero, pltpu.roll(b, HEAD_DIM, 1)),
            jnp.where(low, zero, b),
        ],
        axis=0,
    )


def unspread(four):
    rows = four.shape[0] // 4
    r0, r1, r2, r3 = (four[k * rows : (k + 1) * rows] for k in range(4))
    low = low_lanes(r0.shape)
    return jnp.concatenate(
        [
            jnp.where(low, r0, pltpu.roll(r1, HEAD_DIM, 1)),
            jnp.where(low, pltpu.roll(r2, HEAD_DIM, 1), r3),
        ],
        axis=1,
    )


DOCS = 8


def reach(starts, place):
    first = jnp.zeros_like(place)
    for d in range(1, DOCS):
        first = jnp.where(place >= starts[d], starts[d], first)
    return first


def half_span(half, rows, keys):
    block = lax.axis_index("ctx")
    if half == 1:
        block = keys // rows - 1 - block
    base = block * rows
    return base, (base + rows + CHUNK - 1) // CHUNK


def key_block(kv, chunk, rows, col):
    many = CHUNK // rows
    picked = kv[pl.ds(chunk * many, many), :, pl.ds(col, 128)]
    return picked.reshape(CHUNK, 128)


def attend_rows(
    starts,
    q_ref,
    kv_ref,
    tok_ref,
    wo_ref,
    small_ref,
    route_ref,
    prio_ref,
    raw_ref,
    total_ref,
    mixed_ref,
    sum_ref,
    hid_ref,
    gate_ref,
    kept_ref,
    send_ref,
    acc,
    acc_l,
):
    rows = q_ref.shape[0] // 2
    width = PAIRS * 128
    keys = kv_ref.shape[0] * rows
    for half in range(2):
        base, chunks = half_span(half, rows, keys)
        q_four = []
        for pair in range(PAIRS):
            block = q_ref[pl.ds(half * rows, rows), pl.ds(pair * 256, 256)].astype(F32) * ATT_MULT
            q_four.append(spread(block).astype(BF16))
        acc[...] = jnp.zeros_like(acc)
        acc_l[...] = jnp.zeros_like(acc_l)
        place = base + lax.broadcasted_iota(jnp.int32, (rows, 1), 0)
        first = reach(starts, place)

        def step(chunk, carry):
            at_row = pl.multiple_of(chunk * CHUNK, CHUNK)
            key_pos = at_row + lax.broadcasted_iota(jnp.int32, (1, CHUNK), 1)
            bias = jnp.where((key_pos >= first) & (key_pos <= place), 0.0, NEVER)
            bias = jnp.concatenate([bias] * 4, axis=0)
            for pair in range(PAIRS):
                key = key_block(kv_ref, chunk, rows, pair * 128)
                value = key_block(kv_ref, chunk, rows, width + pair * 128)
                e = jnp.exp(dot_nt(q_four[pair], key) + bias)
                part = e[:, :128]
                for k in range(1, CHUNK // 128):
                    part = part + e[:, k * 128 : (k + 1) * 128]
                acc_l[pair] += part
                acc[pair] += dot_nn(e.astype(BF16), value)
            return carry

        lax.fori_loop(0, chunks, step, 0)
        for pair in range(PAIRS):
            total = jnp.sum(acc_l[pair], axis=1, keepdims=True)
            total = jnp.broadcast_to(total, (4 * rows, 128))
            here = pl.ds(half * rows, rows), pl.ds(pair * 256, 256)
            raw_ref[here] = unspread(acc[pair] / total)
            total_ref[here] = unspread(total)
    mixed = raw_ref[...].astype(BF16)
    mixed_ref[...] = mixed
    first_sum = tok_ref[...].astype(F32) + RES_MULT * dot_nn(mixed, wo_ref[...])
    sum_ref[...] = first_sum
    scale = lax.rsqrt(jnp.mean(first_sum * first_sum, axis=1, keepdims=True) + EPS)
    gain_two = small_ref[pl.ds(EXPERTS + 1, 1), :].astype(F32)
    hidden = (first_sum * scale * gain_two).astype(BF16)
    hid_ref[...] = hidden

    logits = dot_nt(small_ref[...], hidden)[:EXPERTS]
    count = 2 * rows
    expert = lax.broadcasted_iota(jnp.int32, (EXPERTS, count), 0)
    routed = jnp.zeros((EXPERTS, count), F32)
    prio = jnp.zeros((EXPERTS, count), F32)
    for k in range(TOPK):
        line = [
            jnp.concatenate([ref[0, pl.ds(k, 1), :], ref[1, pl.ds(k, 1), :]], axis=1)
            for ref in (route_ref, prio_ref)
        ]
        same = expert == line[0]
        routed = jnp.where(same, 1.0, routed)
        prio = jnp.where(same, line[1].astype(F32), prio)
    chosen = routed > 0.0
    order = lax.broadcasted_iota(jnp.int32, (EXPERTS, count), 1).astype(F32)
    key = jnp.where(chosen, prio * float(count) + order, 65536.0 * count)
    key_cols = jnp.concatenate([key, jnp.zeros((count - EXPERTS, count), F32)], axis=0).T
    ranks = []
    for e in range(EXPERTS):
        ahead = jnp.where(key_cols[:, e : e + 1] < key[e : e + 1, :], 1.0, 0.0)
        ranks.append(jnp.sum(ahead, axis=0, keepdims=True))
    rank = jnp.concatenate(ranks, axis=0)
    top = jnp.max(jnp.where(chosen, logits, -3e38), axis=0, keepdims=True)
    weight = jnp.where(chosen, jnp.exp(logits - top), 0.0)
    gate = weight / jnp.sum(weight, axis=0, keepdims=True)
    kept = jnp.where(chosen & (rank < CAP), 1.0, 0.0)
    gate_ref[...] = gate
    kept_ref[...] = kept
    send_ref[...] = gate * kept


SMEM = pl.BlockSpec(memory_space=pltpu.SMEM)


def finish_kernel(
    outers,
    part,
    moe,
    sum_ref,
    dq_ref,
    da_ref,
    dy_ref,
    tok_ref,
    small_ref,
    cos_ref,
    sin_ref,
    wqkv_in,
    left_in,
    rows_ref,
    z_ref,
    out_ref,
    token_ref,
    attn_ref,
    small_o,
    z_o,
    wqkv_ref,
    left_ref,
    z_sums,
    z_in_rows,
    own,
    half_in,
    y_in,
    z_in,
    m_near,
    m_x,
    m_y,
    qkv,
    swap,
    swapped,
    ss,
    sr,
    ys,
    yr,
    zs,
    zr,
    ns,
    nr,
    ws,
    wr,
    vs,
    vr,
    ls,
    os,
):
    at = Place()
    blocks, rows, full = part.shape
    loads = [
        pltpu.make_async_copy(wqkv_in, wqkv_ref, ls.at[0]),
        pltpu.make_async_copy(left_in, left_ref, ls.at[1]),
    ]
    for copy in loads:
        copy.start()
    width = full // 2
    cuts = 4
    step_width = full // cuts
    count = 2 * rows
    sib, unused = at.relative(0, 1, 0)
    side = at.beside
    along_to, unused = at.relative(1, 0, 0)
    across, unused = at.relative(0, 0, 1)
    other = [lax.rem(at.outer + r, outers) for r in range(outers)]
    far = [(other[r] * INNER + at.inner, at.w) for r in range(1, outers)]
    rest = [
        Halving(at, outers, z_sums.at[e], z_in_rows.at[e], vs.at[e], vr.at[e])
        for e in range(z_sums.shape[0])
    ]
    for e in range(len(rest)):
        z_sums[e, pl.ds(0, outers // 2)] = z_ref[:, e]
    meet([at.relative(*bits)[0] for bits in OTHERS] + far + [at.beside])
    if outers > 2:
        rest[0].start(0)

    def own_block(half, o, y, core):
        index = (o * 2 + y) * 2 + core
        return index if half == 0 else blocks - 1 - index

    own_loads = []
    for y in range(2):
        for h in range(2):
            for o in range(outers):
                copy = pltpu.make_async_copy(
                    part.at[own_block(h, o, y, at.core)], own.at[y, h, o], os.at[y, h, o]
                )
                copy.start()
                own_loads.append(copy)
    first = {}
    for k in range(cuts):
        cols = pl.ds(k * step_width, step_width)
        for y in range(2):
            for h in range(2):
                for o in range(outers):
                    copy = remote(
                        part.at[own_block(h, o, y, 1 - at.core), :, cols],
                        half_in.at[y, h, o, :, cols],
                        ss.at[k, y, h, o],
                        sr.at[k, y, h, o],
                        sib,
                    )
                    copy.start()
                    first[k, y, h, o] = copy
    near = remote(moe.at[:, 1 - at.core], m_near, ns.at[0], nr.at[0], sib)
    near.start()
    for copy in own_loads:
        copy.wait()
    second = []
    for k in range(cuts):
        cols = pl.ds(k * step_width, step_width)
        for y in range(2):
            for h in range(2):
                for o in range(outers):
                    first[k, y, h, o].wait_recv()
                    total = own[y, h, o, :, cols].astype(F32) + half_in[
                        y, h, o, :, cols
                    ].astype(F32)
                    half_in[y, h, o, :, cols] = total.astype(BF16)
        copy = remote(
            half_in.at[1 - at.y, :, :, :, cols], y_in.at[:, :, :, cols], ys.at[k], yr.at[k], side
        )
        copy.start()
        second.append(copy)
    near.wait_recv()
    for y in range(2):
        for w in range(2):
            total = moe[y, at.core, w].astype(F32) + m_near[y, w].astype(F32)
            m_near[y, w] = total.astype(BF16)
    cross = remote(m_near.at[:, 1 - at.w], m_x, ns.at[1], nr.at[1], across)
    cross.start()
    third = []

    def z_send(k):
        cols = pl.ds(k * step_width, step_width)
        second[k].wait_recv()
        for o in range(outers):
            for h in range(2):
                total = half_in[at.y, h, o, :, cols].astype(F32) + y_in[h, o, :, cols].astype(F32)
                half_in[at.y, h, o, :, cols] = total.astype(BF16)
        for r in range(1, outers):
            copy = remote(
                half_in.at[at.y, :, other[r], :, cols],
                z_in.at[r, :, :, cols],
                zs.at[k, r],
                zr.at[k, r],
                far[r - 1],
            )
            copy.start()
            third.append(copy)

    z_send(0)
    z_send(1)
    cross.wait_recv()
    for y in range(2):
        total = m_near[y, at.w].astype(F32) + m_x[y].astype(F32)
        m_x[y] = total.astype(BF16)
    along = remote(m_x.at[1 - at.z], m_y, ns.at[2], nr.at[2], along_to)
    along.start()
    for k in range(2, cuts):
        z_send(k)
    qkv[:, : HEADS * HEAD_DIM] = dq_ref[...]
    along.wait_recv()
    moe_sum = m_x[at.z].astype(F32) + m_y[...].astype(F32)
    out_ref[...] = (sum_ref[...] + RES_MULT * moe_sum).astype(BF16)
    tok = tok_ref[...].astype(F32)
    scale = lax.rsqrt(jnp.mean(tok * tok, axis=1, keepdims=True) + EPS)
    normed = tok * scale
    gain_one = small_ref[pl.ds(EXPERTS, 1), :].astype(F32)
    for copy in third:
        copy.wait_recv()
    if outers > 2:
        for halving in rest[1:]:
            halving.start(0)
    cosine = cos_ref[...]
    sine = -sin_ref[...]
    base = HEADS * HEAD_DIM
    for h in range(2):
        here = slice(h * rows, (h + 1) * rows)
        total = half_in[at.y, h, at.outer].astype(F32)
        for r in range(1, outers):
            total = total + z_in[r, h].astype(F32)
        qkv[here, base : base + width] = turn(total[:, :width], cosine[here], sine[here]).astype(BF16)
        qkv[here, base + width :] = total[:, width:].astype(BF16)
    wide = full * 2 // PLANE
    for j in range(PLANE):
        swap[j, :, :wide] = qkv[:, j * wide : (j + 1) * wide]
        swap[j, :, wide:] = da_ref[:, j * (D // PLANE) : (j + 1) * (D // PLANE)]
    swaps = []
    for slot, bits in enumerate(OTHERS):
        device, j_to = at.relative(*bits)
        copy = remote(swap.at[j_to], swapped.at[at.j], ws.at[slot], wr.at[slot], device)
        copy.start()
        swaps.append(copy)
    swapped[at.j] = swap[at.j]
    for copy in loads:
        copy.wait()
    hidden_grad = dot_nt(qkv[...], wqkv_ref[...])
    small = rows_ref[...]
    gain_grad = jnp.sum(hidden_grad * normed, axis=0, keepdims=True)
    line = lax.broadcasted_iota(jnp.int32, small.shape, 0)
    small = jnp.where(line == EXPERTS, gain_grad, small)
    small = jnp.concatenate([small, jnp.zeros((128 - small.shape[0], D), F32)], axis=0)
    small_o[...] = small.T.astype(BF16)
    hidden_grad = hidden_grad * gain_one
    token_ref[...] = dy_ref[...] + scale * (
        hidden_grad - normed * jnp.mean(hidden_grad * normed, axis=1, keepdims=True)
    )
    for copy in swaps:
        copy.wait_recv()
    all_rows = PLANE * count
    left_one = left_ref[0].reshape(all_rows, D)
    left_mixed = left_ref[1].reshape(all_rows, D)
    grads = swapped[...].reshape(all_rows, wide + D // PLANE)
    attn_ref[:, :wide] = dot_tn(left_one, grads[:, :wide]).astype(BF16)
    attn_ref[:, wide:] = dot_tn(left_mixed, grads[:, wide:]).astype(BF16)
    for e in range(len(rest)):
        z_o[e] = rest[e].finish()
    for copy in list(first.values()) + second + third + swaps + [near, cross, along]:
        copy.wait_send()


def finish(part, moe, arrays, z_half, ctx_count):
    outers = ctx_count // INNER
    blocks, rows, full = part.shape
    count = 2 * rows
    shape = jax.ShapeDtypeStruct
    columns = 3 * D // PLANE
    return comm_call(
        functools.partial(finish_kernel, outers),
        [
            shape((count, D), BF16),
            shape((count, D), F32),
            shape((D, columns), BF16),
            shape((D, 128), BF16),
            shape(z_half.shape[1:], BF16),
        ],
        [ANY] + [VMEM] * (len(arrays) - 2) + [ANY] * 2 + [VMEM] * 2,
        [VMEM] * 5,
        [
            pltpu.VMEM((D, 2 * full), BF16),
            pltpu.VMEM((2, PLANE, count, D), BF16),
            pltpu.VMEM((z_half.shape[1], outers) + z_half.shape[2:], BF16),
            pltpu.VMEM((z_half.shape[1], outers) + z_half.shape[2:], BF16),
            pltpu.VMEM((2, 2, outers, rows, full), BF16),
            pltpu.VMEM((2, 2, outers, rows, full), BF16),
            pltpu.VMEM((2, outers, rows, full), BF16),
            pltpu.VMEM((outers, 2, rows, full), BF16),
            pltpu.VMEM((2, 2, count, D), BF16),
            pltpu.VMEM((2, count, D), BF16),
            pltpu.VMEM((count, D), BF16),
            pltpu.VMEM((count, 2 * full), BF16),
            pltpu.VMEM((PLANE, count, columns), BF16),
            pltpu.VMEM((PLANE, count, columns), BF16),
            DMA((4, 2, 2, outers)),
            DMA((4, 2, 2, outers)),
            DMA((4,)),
            DMA((4,)),
            DMA((4, outers)),
            DMA((4, outers)),
            DMA((3,)),
            DMA((3,)),
            DMA((7,)),
            DMA((7,)),
            DMA((z_half.shape[1], outers)),
            DMA((z_half.shape[1], outers)),
            DMA((2,)),
            DMA((2, 2, outers)),
        ],
        3,
        "finish",
        vmem=63 * 2**20,
        us=60,
    )(part, moe.reshape(2, 2, 2, count, D), *arrays, z_half)


def gate_columns(gates, cols):
    count = gates.shape[-1]
    for j in range(PLANE):
        block = jnp.concatenate([gates[j], jnp.zeros((128 - EXPERTS, count), F32)], axis=0)
        cols[pl.ds(j * count, count), :] = block.T


def expert_step(both, back_act, gate, units):
    gv, uv = both[:, :units], both[:, units:]
    sig = jax.nn.sigmoid(gv)
    silu = gv * sig
    act = silu * uv
    pick = jnp.sum(act * back_act, axis=1, keepdims=True)
    kept = (gate * act).astype(BF16)
    back_act = gate * back_act
    slope = sig * (1.0 + gv * (1.0 - sig))
    low = jnp.concatenate([back_act * uv * slope, back_act * silu], axis=1).astype(BF16)
    return kept, pick, low


def lane_of(cols, lane):
    at = lax.broadcasted_iota(jnp.int32, cols.shape, 1)
    return jnp.sum(jnp.where(at == lane, cols, 0.0), axis=1, keepdims=True)


def opening_kernel(
    outers,
    starts,
    tok_ref,
    wq,
    wk,
    wv,
    wo,
    small,
    cot,
    cos_ref,
    sin_ref,
    route_ref,
    prio_ref,
    expert_in,
    expert_out,
    wqkv_o,
    wo_o,
    small_o,
    q_o,
    hid_o,
    kv_o,
    raw_o,
    total_o,
    mixed_o,
    sum_o,
    gate_o,
    kept_o,
    pick_o,
    z_o,
    part_o,
    kept_units_o,
    grad_o,
    left_o,
    wqkv,
    wout,
    own,
    tok_v,
    cos_v,
    sin_v,
    kv,
    cot_v,
    raw,
    out_w,
    inner_w,
    acc,
    acc_l,
    hid_two,
    gate_send,
    hid,
    gates,
    cot_t,
    backs,
    cols,
    pick_cols,
    staged,
    y_in,
    xs,
    xr,
    fs,
    fr,
    ls,
    zs,
    zr,
    ys,
    yr,
    cs,
    cr,
    hs,
    gs,
    gr,
    gl,
    es,
    ts,
    tr,
    tl,
    gd,
    us,
    ur,
    ul,
    vs,
    vr,
):
    at = Place()
    blocks, rows = kv.shape[:2]
    units = out_w.shape[-1]
    experts = at.q * OWN
    sib, unused = at.relative(0, 1, 0)
    partner, j_partner = at.relative(0, 0, 1)
    side, j_side = at.relative(1, 0, 0)
    unused, j_cross = at.relative(1, 0, 1)
    steps = sorted({1, outers - 1})
    far = [(lax.rem(at.outer + r, outers) * INNER + at.inner, at.w) for r in steps]
    expert_loads = {}

    def load_expert(e):
        copy = pltpu.make_async_copy(expert_in.at[experts + e], raw.at[e % 2], es.at[e % 2])
        copy.start()
        expert_loads[e] = copy

    def shape_expert(e):
        expert_loads[e].wait()
        inner_w[:, e * 2 * units : (e + 1) * 2 * units] = raw[e % 2].reshape(D, 2 * units)
        if e + 2 < OWN:
            load_expert(e + 2)

    out_loads = [
        pltpu.make_async_copy(expert_out.at[experts + e], out_w.at[e], es.at[2 + e])
        for e in range(OWN)
    ]
    for copy in out_loads:
        copy.start()
    load_expert(0)
    load_expert(1)
    meet([at.relative(*bits)[0] for bits in XY + [(0, 1, 0)]] + far + [at.beside])

    pieces = [(wk, wqkv, 1024), (wv, wqkv, 1536), (wq, wqkv, 0), (wo, wout, 0)]
    sends, passed, keeps = {}, {}, []

    def give(index):
        src, dst, col = pieces[index]
        depth, width = src.shape
        half = depth // 2
        copy = remote(
            src.at[pl.ds(at.core * half, half), :],
            dst.at[pl.ds(at.w * depth + at.core * half, half), pl.ds(col, width)],
            xs.at[index],
            xr.at[index],
            partner,
        )
        copy.start()
        sends[index] = copy

    def pass_on(index):
        src, dst, col = pieces[index]
        depth, width = src.shape
        half = depth // 2
        sends[index].wait_recv()
        piece = dst.at[pl.ds((1 - at.w) * depth + at.core * half, half), pl.ds(col, width)]
        copy = remote(piece, piece, fs.at[index], fr.at[index], sib)
        copy.start()
        passed[index] = copy

    wide = small.shape[1]
    mine = small_o.at[:, pl.ds(at.w * wide, wide)]
    gains = remote(small, mine, xs.at[4], xr.at[4], partner)
    gains.start()
    give(0)
    give(1)
    cot_sib = remote(cot, cot_v.at[at.j], gs.at[0], gr.at[0], sib)
    cot_sib.start()
    cot_side = remote(cot, cot_v.at[at.j], gs.at[1], gr.at[1], side)
    cot_side.start()
    cot_keep = pltpu.make_async_copy(cot, cot_v.at[at.j], gl)
    cot_keep.start()
    for index, (src, dst, col) in enumerate(pieces):
        depth, width = src.shape
        keep = pltpu.make_async_copy(
            src, dst.at[pl.ds(at.w * depth, depth), pl.ds(col, width)], ls.at[index]
        )
        keep.start()
        keeps.append(keep)
    loads = [
        pltpu.make_async_copy(src, dst, hs.at[4 + index])
        for index, (src, dst) in enumerate(
            ((tok_ref, tok_v), (cos_ref, cos_v), (sin_ref, sin_v), (small, mine))
        )
    ]
    for copy in loads:
        copy.start()
    for copy in loads:
        copy.wait()
    tok = tok_v[...].astype(F32)
    normed = tok * lax.rsqrt(jnp.mean(tok * tok, axis=1, keepdims=True) + EPS)
    gains.wait_recv()
    hidden = (normed * small_o[pl.ds(EXPERTS, 1), :].astype(F32)).astype(BF16)
    hid_o[...] = hidden
    cosine, sine = cos_v[...], sin_v[...]

    pass_on(0)
    pass_on(1)
    cot_across = remote(cot, cot_v.at[at.j], gs.at[2], gr.at[2], partner)
    cot_across.start()
    keeps[0].wait()
    keeps[1].wait()
    passed[0].wait_recv()
    key = dot_nn(hidden, wqkv[:, 1024:1536])
    key = turn(key, cosine, sine).astype(BF16)
    passed[1].wait_recv()
    value = dot_nn(hidden, wqkv[:, 1536:]).astype(BF16)
    width = key.shape[1]
    for half in range(2):
        own[half, :, :width] = key[half * rows : (half + 1) * rows]
        own[half, :, width:] = value[half * rows : (half + 1) * rows]

    def block_of(half, ctx):
        return kv.at[ctx] if half == 0 else kv.at[blocks - 1 - ctx]

    last = outers - 1
    hops = [(0, 0, 0)] + [
        (step, sign, step if sign < 0 else last + step)
        for step in range(1, outers)
        for sign in (-1, 1)
    ]

    def source(step, sign):
        return at.outer + sign * step

    def exists(step, sign):
        place = source(step, sign)
        return (place >= 0) & (place <= last)

    def block_from(half, step, sign, inner):
        place = lax.rem(source(step, sign) + outers, outers)
        return block_of(half, place * INNER + inner)

    below = (lax.rem(at.outer + last, outers) * INNER + at.inner, at.w)
    above = (lax.rem(at.outer + 1, outers) * INNER + at.inner, at.w)
    inner_side = at.inner + 2 - 4 * at.y

    def z_copy(half, slot, step, sign):
        src = own.at[half] if step == 0 else block_from(half, step, sign, at.inner)
        dst = block_from(half, step, sign, at.inner)
        slot_there = step + 1 if sign < 0 else last + step + 1
        return remote(
            src,
            dst,
            zs.at[half, slot_there],
            zr.at[half, slot_there],
            above if sign < 0 else below,
        )

    def y_copy(half, slot, step, sign):
        src = own.at[half] if step == 0 else block_from(half, step, sign, at.inner)
        dst = block_from(half, step, sign, at.inner)
        return remote(src, dst, ys.at[half, slot], yr.at[half, slot], at.beside)

    def c_copy(half, slot, step, sign, inner, base):
        src = (
            own.at[half]
            if step == 0 and base == 0
            else block_from(half, step, sign, inner)
        )
        dst = block_from(half, step, sign, inner)
        return remote(src, dst, cs.at[half, base + slot], cr.at[half, base + slot], sib)

    spots = 2 * outers - 1

    def spread_from(step, sign, slot, halves=(0, 1)):
        for half in halves:
            if step == 0:
                for way in (-1, 1):

                    @pl.when((at.outer < last) if way < 0 else (at.outer > 0))
                    def _():
                        z_copy(half, 0, 0, way).start()

            elif step < last:

                @pl.when((at.outer < last) if sign < 0 else (at.outer > 0))
                def _():
                    z_copy(half, slot, step, sign).start()

            y_copy(half, slot, step, sign).start()
            c_copy(half, slot, step, sign, at.inner, 0).start()

    spread_from(0, 0, 0)
    for half in range(2):
        keep = pltpu.make_async_copy(own.at[half], block_of(half, at.c), hs.at[half])
        keep.start()
        keeps.append(keep)

    def y_arrived(step, sign, slot):
        for half in range(2):
            y_copy(half, slot, step, sign).wait_recv()
            c_copy(half, slot, step, sign, inner_side, spots).start()

    def z_arrived(want):
        for step, sign, slot in hops[1:]:
            if step == want:

                @pl.when(exists(step, sign))
                def _():
                    for half in range(2):
                        z_copy(half, slot, step - 1, sign).wait_recv()
                        spread_from(step, sign, slot, (half,))

    def sides_arrived(want):
        for step, sign, slot in hops[1:]:
            if step == want:

                @pl.when(exists(step, sign))
                def _():
                    y_arrived(step, sign, slot)

    shape_expert(0)
    cot_across.wait_recv()
    give(2)
    cot_on = []

    def cot_pass(slot, j_from, device):
        block = cot_v.at[j_from]
        copy = remote(block, block, gs.at[slot], gr.at[slot], device)
        copy.start()
        cot_on.append(copy)

    cot_pass(3, j_partner, side)
    cot_pass(4, j_partner, sib)
    cot_side.wait_recv()
    cot_pass(5, j_side, sib)
    z_arrived(1)
    y_arrived(0, 0, 0)
    shape_expert(1)
    pass_on(2)
    give(3)
    shape_expert(2)
    if outers > 2:
        z_arrived(2)
    keeps[2].wait()
    passed[2].wait_recv()
    q_o[...] = turn(dot_nn(hidden, wqkv[:, :1024]), cosine, sine).astype(BF16)
    store = pltpu.make_async_copy(wqkv, wqkv_o, hs.at[2])
    store.start()
    shape_expert(3)
    sides_arrived(1)
    for step in range(3, outers):
        z_arrived(step)
        sides_arrived(step - 1)
    if outers > 2:
        sides_arrived(last)
    pass_on(3)
    cot_on[0].wait_recv()
    cot_pass(6, j_cross, sib)
    keeps[3].wait()
    passed[3].wait_recv()
    store_out = pltpu.make_async_copy(wout, wo_o, hs.at[3])
    store_out.start()
    def sibling_brought(step, sign, slot):
        for half in range(2):
            c_copy(half, slot, step, sign, at.inner, 0).wait_recv()
            c_copy(half, slot, step, sign, inner_side, spots).wait_recv()

    sibling_brought(0, 0, 0)
    for step, sign, slot in hops[1:]:

        @pl.when(exists(step, sign))
        def _():
            sibling_brought(step, sign, slot)

    for keep in keeps[4:]:
        keep.wait()
    store_kv = pltpu.make_async_copy(kv, kv_o, hs.at[4])
    store_kv.start()
    attend_rows(
        starts,
        q_o,
        kv,
        tok_v,
        wout,
        small_o,
        route_ref,
        prio_ref,
        raw_o,
        total_o,
        mixed_o,
        sum_o,
        hid_two,
        gate_o,
        kept_o,
        gate_send,
        acc,
        acc_l,
    )

    pairs = [(hid_two, hid), (gate_send, gates)]
    copies = gather_start(at, pairs, ts, tr, tl)
    for copy in [cot_sib] + cot_on[1:]:
        copy.wait_recv()
    cot_keep.wait()
    for copy in out_loads:
        copy.wait()
    tokens = cot_v.shape[0] * cot_v.shape[1]
    cot_rows = cot_v[...].reshape(tokens, D)
    cot_t[...] = cot_rows.T
    for e in range(OWN):
        backs[:, e * units : (e + 1) * units] = (RES_MULT * dot_nn(cot_rows, out_w[e])).astype(BF16)
    gather_wait(copies, gather_pass(at, pairs, copies, ts, tr))
    gate_columns(gates, cols)
    left_pairs = [(hid_o, left_o.at[0]), (mixed_o, left_o.at[1])]
    left_copies = gather_start(at, left_pairs, us, ur, ul)
    store_out.wait()
    passed[3].wait_send()
    hid_t = wout
    hid_t[...] = hid[...].reshape(tokens, D).T
    y_sends = [
        remote(staged.at[e, :, :, 1 - at.y], y_in.at[e], vs.at[e], vr.at[e], at.beside)
        for e in range(FIRST)
    ]
    at_lane = lax.broadcasted_iota(jnp.int32, cols.shape, 1)
    pick_cols[...] = jnp.zeros(pick_cols.shape, F32)
    store.wait()
    for index in range(3):
        passed[index].wait_send()
    low_all = wqkv

    def expert(e, carry):
        wide = pl.ds(pl.multiple_of(e * 2 * units, 2 * units), 2 * units)
        tall = pl.ds(pl.multiple_of(e * units, units), units)
        both = dot_nn(hid[...].reshape(tokens, D), inner_w[:, wide])
        kept, pick, low = expert_step(
            both, backs[:, tall].astype(F32), lane_of(cols[...], experts + e), units
        )
        backs[:, tall] = kept
        low_all[:, wide] = low
        pick_cols[...] = jnp.where(at_lane == e, pick, pick_cols[...])

        shape = staged.shape[1:5]
        staged[e, :, :, :, :, : 2 * units] = (
            dot_nn(hid_t[...], low).astype(BF16).reshape(*shape, 2 * units)
        )
        staged[e, :, :, :, :, 2 * units :] = (
            (RES_MULT * dot_nn(cot_t[...], kept)).astype(BF16).reshape(*shape, units)
        )
        for now in range(OWN):

            @pl.when(e == now)
            def _():
                if now < FIRST:
                    y_sends[now].start()
                else:
                    pltpu.make_async_copy(
                        staged.at[now], grad_o.at[now - FIRST], gd.at[now - FIRST]
                    ).start()

        return carry

    lax.fori_loop(0, OWN, expert, 0)
    left_passed = gather_pass(at, left_pairs, left_copies, us, ur)
    count = hid.shape[1]
    for j in range(PLANE):
        pick_o[j] = pick_cols[j * count : (j + 1) * count, :].T[:8]
    store_kept = pltpu.make_async_copy(backs, kept_units_o, hs.at[5])
    store_kept.start()
    for j in range(PLANE):
        here = slice(j * count, (j + 1) * count)
        hid[j] = dot_nt(low_all[here, :], inner_w[...]).astype(BF16)
    store_part = pltpu.make_async_copy(hid, part_o, hs.at[6])
    store_part.start()

    def settle(step, sign, slot):
        for half in range(2):
            if step == 0:
                for way in (-1, 1):

                    @pl.when((at.outer < last) if way < 0 else (at.outer > 0))
                    def _():
                        z_copy(half, 0, 0, way).wait_send()

            elif step < last:

                @pl.when((at.outer < last) if sign < 0 else (at.outer > 0))
                def _():
                    z_copy(half, slot, step, sign).wait_send()

            y_copy(half, slot, step, sign).wait_send()
            c_copy(half, slot, step, sign, at.inner, 0).wait_send()
            c_copy(half, slot, step, sign, inner_side, spots).wait_send()

    settle(0, 0, 0)
    for step, sign, slot in hops[1:]:

        @pl.when(exists(step, sign))
        def _():
            settle(step, sign, slot)

    for copy in sends.values():
        copy.wait_send()
    for copy in [gains, cot_sib, cot_side, cot_across] + cot_on:
        copy.wait_send()
    for e in range(FIRST):
        y_sends[e].wait()
        total = staged[e, :, :, at.y].astype(F32) + y_in[e].astype(F32)
        z_o[:, e] = total.astype(BF16)
    gather_wait(left_copies, left_passed)
    for copy in [store_kv, store_kept, store_part]:
        copy.wait()
    for e in range(FIRST, OWN):
        pltpu.make_async_copy(staged.at[e], grad_o.at[e - FIRST], gd.at[e - FIRST]).wait()


def opening(
    starts, tokens, wq, wk, wv, wo, small, cot, cosine, sine, routes, priority, expert_in, expert_out, ctx_count
):
    outers = ctx_count // INNER
    shape = jax.ShapeDtypeStruct
    count = tokens.shape[0]
    rows = count // 2
    width = wk.shape[1] + wv.shape[1]
    heads = wq.shape[1]
    wide = heads + width
    units = expert_out.shape[-1]
    many = PLANE * count
    blocks = 2 * ctx_count
    z_rows = D // (2 * outers)
    vm = pltpu.VMEM
    return comm_call(
        functools.partial(opening_kernel, outers),
        [
            shape((D, wide), BF16),
            shape((D, D), BF16),
            shape((small.shape[0], D), BF16),
            shape((count, heads), BF16),
            shape((count, D), BF16),
            shape((blocks, rows, width), BF16),
            shape((count, heads), F32),
            shape((count, heads), F32),
            shape((count, heads), BF16),
            shape((count, D), F32),
            shape((EXPERTS, count), F32),
            shape((EXPERTS, count), F32),
            shape((PLANE, 8, count), F32),
            shape((outers // 2, FIRST, 2, z_rows, 3 * units), BF16),
            shape((PLANE, count, D), BF16),
            shape((many, OWN * units), BF16),
            shape((OWN - FIRST, outers // 2, 2, 2, z_rows, 3 * units), BF16),
            shape((2, PLANE, count, D), BF16),
        ],
        [SMEM] + [ANY] * 9 + [VMEM] * 2 + [ANY] * 2,
        [ANY] * 2 + [VMEM] * 3 + [ANY] + [VMEM] * 8 + [ANY] * 4,
        [
            vm((D, wide), BF16),
            vm((D, D), BF16),
            vm((2, rows, width), BF16),
            vm((count, D), BF16),
            vm(cosine.shape, F32),
            vm(sine.shape, F32),
            vm((blocks, rows, width), BF16),
            vm((PLANE, count, D), BF16),
            vm((2, D, 2, units), BF16),
            vm((OWN, D, units), BF16),
            vm((D, OWN * 2 * units), BF16),
            vm((PAIRS, 2 * count, 128), F32),
            vm((PAIRS, 2 * count, 128), F32),
            vm((count, D), BF16),
            vm((EXPERTS, count), F32),
            vm((PLANE, count, D), BF16),
            vm((PLANE, EXPERTS, count), F32),
            vm((D, many), BF16),
            vm((many, OWN * units), BF16),
            vm((many, 128), F32),
            vm((many, 128), F32),
            vm((OWN, outers // 2, 2, 2, z_rows, 3 * units), BF16),
            vm((FIRST, outers // 2, 2, z_rows, 3 * units), BF16),
            DMA((5,)),
            DMA((5,)),
            DMA((4,)),
            DMA((4,)),
            DMA((4,)),
        ]
        + [DMA((2, 2 * outers))] * 4
        + [DMA((2, 4 * outers))] * 2
        + [DMA((8,)), DMA((7,)), DMA((7,)), DMA]
        + [DMA((2 + OWN,)), DMA((2, 7)), DMA((2, 7)), DMA((2,)), DMA((2,))]
        + [DMA((2, 7)), DMA((2, 7)), DMA((2,)), DMA((FIRST,)), DMA((FIRST,))],
        1,
        "opening",
        vmem=64 * 2**20,
        us=100,
    )(starts, tokens, wq, wk, wv, wo, small, cot, cosine, sine, routes, priority, expert_in, expert_out)


def turning_kernel(
    outers,
    starts,
    z_ref,
    grad_in,
    part_in,
    pick_send,
    kept_in,
    expert_out,
    gate_ref,
    kept_ref,
    small_ref,
    sum_ref,
    cot_ref,
    wo_in,
    raw_ref,
    total_ref,
    q_ref,
    kv_in,
    cos_ref,
    sin_ref,
    dy_ref,
    da_ref,
    dq_ref,
    rows_ref,
    moe_o,
    near_o,
    z_o,
    dkv_ref,
    part,
    kept_all,
    out_w,
    wout,
    kv,
    near,
    far_in,
    picks_all,
    q_four,
    n_four,
    d_rows,
    dq_acc,
    kv_acc,
    kv_out,
    z_sums,
    z_in,
    y_own,
    y_in,
    ls,
    ss,
    sr,
    xs,
    xr,
    ps,
    pr,
    vs,
    vr,
    us,
    ur,
    ks,
):
    at = Place()
    count = q_ref.shape[0]
    rows = count // 2
    width = PAIRS * 128
    keys = kv.shape[0] * rows
    units = out_w.shape[-1]
    experts = at.q * OWN
    loads = [
        pltpu.make_async_copy(src, dst, ls.at[index])
        for index, (src, dst) in enumerate(
            ((part_in, part), (kept_in, kept_all), (wo_in, wout), (kv_in, kv))
        )
    ]
    weights = [
        pltpu.make_async_copy(expert_out.at[experts + e], out_w.at[e], ls.at[4 + e])
        for e in range(OWN)
    ]
    for copy in loads + weights:
        copy.start()
    rest = Halving(at, outers, z_sums, z_in, vs, vr)
    z_sums[pl.ds(0, outers // 2)] = z_ref[...]
    own_rows = []
    for e in range(OWN - FIRST):
        copy = pltpu.make_async_copy(
            grad_in.at[e, :, :, at.y], y_own.at[e], ls.at[4 + OWN + e]
        )
        copy.start()
        own_rows.append(copy)
    meet(
        [at.relative(*bits)[0] for bits in OTHERS]
        + [at.beside]
        + [rest.device(bit) for bit in rest.bits]
    )
    sib, unused = at.relative(0, 1, 0)
    loads[0].wait()
    first = remote(part.at[:, 1 - at.core], near, ss, sr, sib)
    first.start()
    y_sends = []
    for e in range(OWN - FIRST):
        copy = remote(grad_in.at[e, :, :, 1 - at.y], y_in.at[e], us.at[e], ur.at[e], at.beside)
        copy.start()
        y_sends.append(copy)
    if rest.bits:
        rest.start(0)
    small_copies = []
    for slot, bits in enumerate(OTHERS):
        device, j_to = at.relative(*bits)
        copy = remote(pick_send.at[j_to], picks_all.at[at.j], ps.at[slot], pr.at[slot], device)
        copy.start()
        small_copies.append(copy)
    picks_all[at.j] = pick_send[at.j]
    first.wait_recv()
    for y in range(2):
        for w in range(2):
            total = part[y, at.core, w].astype(F32) + near[y, w].astype(F32)
            near[y, w] = total.astype(BF16)
    second = []
    for slot, (dy, dc, dw) in enumerate(XY):
        device, unused = at.relative(dy, dc, dw)
        z = at.z + dy * (1 - 2 * at.z)
        w = at.w + dw * (1 - 2 * at.w)
        copy = remote(near.at[z, w], far_in.at[slot], xs.at[slot], xr.at[slot], device)
        copy.start()
        second.append(copy)

    loads[1].wait()
    for copy in weights:
        copy.wait()

    def moe_rows(j, carry):
        here = pl.ds(pl.multiple_of(j * count, count), count)
        total = dot_nt(kept_all[here, :units], out_w[0])
        for e in range(1, OWN):
            total = total + dot_nt(kept_all[here, e * units : (e + 1) * units], out_w[e])
        moe_o[j] = total.astype(BF16)
        return carry

    lax.fori_loop(0, PLANE, moe_rows, 0)
    hidden_sum = near[at.z, at.w].astype(F32)
    for slot in range(3):
        second[slot].wait_recv()
        hidden_sum = hidden_sum + far_in[slot].astype(F32)
    for copy in [first] + second:
        copy.wait_send()
    small = small_ref[...]
    gain_two = small[EXPERTS + 1 : EXPERTS + 2].astype(F32)
    for copy in small_copies:
        copy.wait()
    parts = []
    for i in range(INNER):
        parts.append(picks_all[2 * i, pl.ds(0, OWN), :] + picks_all[2 * i + 1, pl.ds(0, OWN), :])
    gate = gate_ref[...]
    gate_grad = kept_ref[...] * jnp.concatenate(parts, axis=0)
    logit_grad = gate * (gate_grad - jnp.sum(gate * gate_grad, axis=0, keepdims=True))
    logit_grad = jnp.concatenate(
        [logit_grad, jnp.zeros((small.shape[0] - EXPERTS, count), F32)], axis=0
    ).astype(BF16)
    hidden_grad = hidden_sum + dot_tn(logit_grad, small)
    first_sum = sum_ref[...]
    scale = lax.rsqrt(jnp.mean(first_sum * first_sum, axis=1, keepdims=True) + EPS)
    normed = first_sum * scale
    hidden = (normed * gain_two).astype(BF16)
    router_rows = dot_nn(logit_grad, hidden)
    rows_ref[...] = router_rows
    rows_ref[pl.ds(EXPERTS + 1, 1), :] = jnp.sum(hidden_grad * normed, axis=0, keepdims=True)
    normed_grad = hidden_grad * gain_two
    first_grad = cot_ref[...].astype(F32) + scale * (
        normed_grad - normed * jnp.mean(normed_grad * normed, axis=1, keepdims=True)
    )
    dy_ref[...] = first_grad
    attn_grad = (RES_MULT * first_grad).astype(BF16)
    da_ref[...] = attn_grad
    loads[2].wait()
    mixed_grad = dot_nt(attn_grad, wout[...]).astype(BF16).astype(F32)
    total = total_ref[...]
    numer = mixed_grad / total
    lost = mixed_grad * raw_ref[...] / total
    for half in range(2):
        here = slice(half * rows, (half + 1) * rows)
        for pair in range(PAIRS):
            cols = slice(pair * 256, (pair + 1) * 256)
            slot = half * PAIRS + pair
            q_four[slot] = spread(q_ref[here, cols].astype(F32) * ATT_MULT).astype(BF16)
            n_four[slot] = spread(numer[here, cols]).astype(BF16)
            d_rows[slot] = -jnp.sum(spread(lost[here, cols]).T, axis=0, keepdims=True)
    dq_acc[...] = jnp.zeros_like(dq_acc)
    loads[3].wait()

    def kv_store(chunk):
        many = CHUNK // rows
        return pltpu.make_async_copy(
            kv_out.at[chunk % 2], dkv_ref.at[pl.ds(chunk * many, many)], ks.at[chunk % 2]
        )

    def step(chunk, carry):
        at_row = pl.multiple_of(chunk * CHUNK, CHUNK)
        kv_acc[...] = jnp.zeros_like(kv_acc)
        key_pos = at_row + lax.broadcasted_iota(jnp.int32, (CHUNK, 1), 0)
        for half in range(2):
            base, chunks = half_span(half, rows, keys)

            @pl.when(chunk < chunks)
            def _():
                place = base + lax.broadcasted_iota(jnp.int32, (1, 4 * rows), 1) % rows
                first = reach(starts, place)
                bias = jnp.where((key_pos >= first) & (key_pos <= place), 0.0, NEVER)
                for pair in range(PAIRS):
                    slot = half * PAIRS + pair
                    key = key_block(kv, chunk, rows, pair * 128)
                    value = key_block(kv, chunk, rows, width + pair * 128)
                    e = jnp.exp(dot_nt(key, q_four[slot]) + bias)
                    through = dot_nt(value, n_four[slot])
                    dz = (e * (through + d_rows[slot])).astype(BF16)
                    kv_acc[:, pl.ds(pair * 128, 128)] += dot_nn(dz, q_four[slot])
                    kv_acc[:, pl.ds(width + pair * 128, 128)] += dot_nn(e.astype(BF16), n_four[slot])
                    dq_acc[slot] += dot_tn(dz, key)

        many = CHUNK // rows

        @pl.when(chunk >= 2)
        def _():
            kv_store(chunk - 2).wait()

        kv_out[chunk % 2] = kv_acc[...].astype(BF16).reshape(many, rows, 2 * width)
        kv_store(chunk).start()
        return carry

    lax.fori_loop(0, keys // CHUNK, step, 0)
    cosine = cos_ref[...]
    sine = -sin_ref[...]
    for half in range(2):
        here = slice(half * rows, (half + 1) * rows)
        for pair in range(PAIRS):
            block = ATT_MULT * unspread(dq_acc[half * PAIRS + pair])
            dq_ref[here, pair * 256 : (pair + 1) * 256] = turn(
                block, cosine[here], sine[here]
            ).astype(BF16)
    for chunk in range(keys // CHUNK - 2, keys // CHUNK):
        kv_store(chunk).wait()
    near_o[...] = rest.finish()
    for copy in own_rows:
        copy.wait()
    for e in range(OWN - FIRST):
        y_sends[e].wait()
        total = y_own[e].astype(F32) + y_in[e].astype(F32)
        z_o[:, e] = total.astype(BF16)


def turning(
    outers, starts, z_first, grads, part, picks, kept_units, expert_out, gate, kept, small, first_sum, cot, output_w, raw, total, queries, kv_all, cosine, sine
):
    shape = jax.ShapeDtypeStruct
    count, width = queries.shape
    units = expert_out.shape[-1]
    vm = pltpu.VMEM
    return comm_call(
        functools.partial(turning_kernel, outers),
        [
            shape((count, D), F32),
            shape((count, D), BF16),
            shape((count, width), BF16),
            shape((32, D), F32),
            shape((PLANE, count, D), BF16),
            shape(z_first.shape[1:], BF16),
            shape((outers // 2, OWN - FIRST) + z_first.shape[2:], BF16),
            shape(kv_all.shape, BF16),
        ],
        [SMEM, VMEM, ANY, ANY, VMEM, ANY, ANY] + [VMEM] * 5 + [ANY] + [VMEM] * 3 + [ANY] + [VMEM] * 2,
        [VMEM] * 7 + [ANY],
        [
            vm((2, 2, 2, count, D), BF16),
            vm(kept_units.shape, BF16),
            vm((OWN, D, units), BF16),
            vm((D, D), BF16),
            vm(kv_all.shape, BF16),
            vm((2, 2, count, D), BF16),
            vm((3, count, D), BF16),
            vm((PLANE, 8, count), F32),
            vm((2 * PAIRS, 2 * count, 128), BF16),
            vm((2 * PAIRS, 2 * count, 128), BF16),
            vm((2 * PAIRS, 1, 2 * count), F32),
            vm((2 * PAIRS, 2 * count, 128), F32),
            vm((CHUNK, 2 * PAIRS * 128), F32),
            vm((2, CHUNK // (count // 2), count // 2, 2 * PAIRS * 128), BF16),
            vm((outers,) + z_first.shape[1:], BF16),
            vm((outers,) + z_first.shape[1:], BF16),
            vm((OWN - FIRST, outers // 2) + z_first.shape[2:], BF16),
            vm((OWN - FIRST, outers // 2) + z_first.shape[2:], BF16),
            DMA((4 + OWN + OWN - FIRST,)),
            DMA,
            DMA,
            DMA((3,)),
            DMA((3,)),
            DMA((7,)),
            DMA((7,)),
            DMA((outers,)),
            DMA((outers,)),
            DMA((OWN - FIRST,)),
            DMA((OWN - FIRST,)),
            DMA((2,)),
        ],
        5,
        "turning",
        vmem=62 * 2**20,
        us=35,
    )(
        starts,
        z_first,
        grads,
        part.reshape(2, 2, 2, count, D),
        picks,
        kept_units,
        expert_out,
        gate,
        kept,
        small,
        first_sum,
        cot,
        output_w,
        raw,
        total,
        queries,
        kv_all,
        cosine,
        sine,
    )


def assemble_kernel(
    outers, attn_in, small_in, near_one, near, wq, wk, wv, wo, small, inner, outer
):
    qkv_cols = wq.shape[1] * 2 // PLANE
    devices = outers * PLANE
    for j in range(PLANE):
        z, core, w = j // 4, (j // 2) % 2, j % 2
        total = 0.0
        for above in range(outers // 2):
            for y in range(2):
                source = (((above * 2 + z) * 2 + y) * 2 + core) * 2 + w
                total = total + attn_in[source].astype(F32)
        col = j * qkv_cols
        ref, base = (wq, 0) if col < 1024 else (wk, 1024) if col < 1536 else (wv, 1536)
        ref[:, col - base : col - base + qkv_cols] = total[:, :qkv_cols]
        wo[:, j * (D // PLANE) : (j + 1) * (D // PLANE)] = total[:, qkv_cols:]
    total = small_in[0].astype(F32)
    for i in range(1, devices):
        total = total + small_in[i].astype(F32)
    small[...] = total
    rows = wq.shape[0]
    units = outer.shape[-1] // 2
    for j in range(PLANE):
        cols = slice((j % 2) * units, (j % 2 + 1) * units)
        for k in range(OWN):
            e = (j // 2) * OWN + k
            block = (near_one[j, k] if k < FIRST else near[j, k - FIRST]).astype(F32)
            inner[e, :, :, cols] = block[:, : 2 * units].reshape(rows, 2, units)
            outer[e, :, cols] = block[:, 2 * units :]


def assemble(attn_in, small_in, near_one, near, outers):
    rows = attn_in.shape[1]
    units = near.shape[-1] // 3
    shape = jax.ShapeDtypeStruct
    outs = [
        shape((rows, 1024), F32),
        shape((rows, 512), F32),
        shape((rows, 512), F32),
        shape((rows, D), F32),
        shape((rows, 128), F32),
        shape((EXPERTS, rows, 2, 2 * units), F32),
        shape((EXPERTS, rows, 2 * units), F32),
    ]
    return pl.pallas_call(
        functools.partial(assemble_kernel, outers),
        out_shape=outs,
        in_specs=[VMEM] * 4,
        out_specs=[VMEM] * 7,
        compiler_params=pltpu.CompilerParams(
            vmem_limit_bytes=room([attn_in, small_in, near_one, near] * 2 + outs)
        ),
        name="assemble",
    )(attn_in, small_in, near_one, near)


def body(
    tokens,
    w_query,
    w_key,
    w_value,
    w_output,
    attn_gain,
    w_router,
    expert_in,
    expert_out,
    moe_gain,
    segments,
    routes,
    priority,
    cotangent,
):
    ctx_count = lax.axis_size("ctx")
    ctx_index = lax.axis_index("ctx")
    devices = ctx_count * 2
    outers = ctx_count // INNER
    owner_rows = D // devices
    block_rows = tokens.shape[2]
    half_rows = block_rows * ctx_count
    tok_count = 2 * block_rows
    f32 = jnp.float32
    bf16 = jnp.bfloat16

    small = jnp.concatenate(
        [w_router.T, attn_gain[None], moe_gain[None], jnp.zeros((14, w_router.shape[0]), bf16)]
    )
    cot_own = cotangent.reshape(tok_count, D)
    block_total = 2 * ctx_count
    block_ids = jnp.stack([ctx_index, block_total - 1 - ctx_index])
    query_pos = block_ids[:, None] * block_rows + jnp.arange(block_rows, dtype=jnp.int32)[None, :]
    flat_pos = query_pos.reshape(tok_count)
    starts = jnp.sum(
        (segments < jnp.arange(DOCS, dtype=jnp.int32)[:, None]).astype(jnp.int32), axis=1
    )
    frequency = jnp.exp(
        -jnp.log(jnp.float32(THETA))
        * jnp.arange(HEAD_DIM // 2, dtype=jnp.float32)
        * (2.0 / HEAD_DIM)
    )
    angles = flat_pos.astype(f32)[:, None] * frequency[None, :]
    cosine, sine = jnp.cos(angles), jnp.sin(angles)
    cosine = jnp.concatenate([cosine] * 4, axis=1)
    sine = jnp.concatenate([-sine, sine] * 2, axis=1)
    token_low = tokens.reshape(tok_count, D)
    (
        qkv_w,
        output_w,
        small_all,
        queries,
        hidden_one,
        kv_all,
        attn_raw,
        attn_total,
        mixed,
        first_sum,
        gate,
        kept,
        picks,
        first_half,
        part,
        kept_units,
        expert_grads,
        left,
    ) = opening(
        starts,
        token_low,
        w_query,
        w_key,
        w_value,
        w_output,
        small,
        cot_own,
        cosine,
        sine,
        routes[0].transpose(0, 2, 1),
        priority[0].transpose(0, 2, 1),
        expert_in,
        expert_out,
        ctx_count,
    )
    (
        first_grad,
        attn_grad,
        query_lin_grad,
        small_rows,
        moe_part,
        near_one,
        second_half,
        kv_terms,
    ) = turning(
        outers,
        starts,
        first_half,
        expert_grads,
        part,
        picks,
        kept_units,
        expert_out,
        gate,
        kept,
        small_all,
        first_sum,
        cot_own,
        output_w,
        attn_raw,
        attn_total,
        queries,
        kv_all,
        cosine,
        sine,
    )
    output, token_grad, attn_part, small_part, near = finish(
        kv_terms,
        moe_part,
        [
            first_sum,
            query_lin_grad,
            attn_grad,
            first_grad,
            token_low,
            small_all,
            cosine,
            sine,
            qkv_w,
            left,
            small_rows,
        ],
        second_half,
        ctx_count,
    )
    attn_in, small_in, near_one, near = owners(
        [attn_part, small_part],
        [
            rows.reshape(-1, PLANE, owner_rows, rows.shape[-1])
            for rows in (near_one, near)
        ],
        devices,
        7,
        "owners",
    )
    query_sum, key_sum, value_sum, output_sum, small_sum, inner_sum, outer_sum = assemble(
        attn_in, small_in, near_one, near, outers
    )
    return (
        output.reshape(tokens.shape),
        token_grad.reshape(tokens.shape),
        query_sum,
        key_sum,
        value_sum,
        output_sum,
        small_sum[:, EXPERTS],
        small_sum[:, :EXPERTS],
        inner_sum,
        outer_sum,
        small_sum[:, EXPERTS + 1],
    )


def solution(mesh):
    placed = (
        P("wsh", None, "ctx", None),
        P("wsh", None),
        P("wsh", None),
        P("wsh", None),
        P("wsh", None),
        P("wsh"),
        P("wsh", None),
        P(None, None, None, "wsh"),
        P(None, None, "wsh"),
        P("wsh"),
        P("wsh", None),
        P("wsh", None, "ctx", None),
        P("wsh", None, "ctx", None),
        P("wsh", None, "ctx", None),
    )
    return jax.shard_map(
        body,
        mesh=mesh,
        in_specs=placed,
        out_specs=(
            P("wsh", None, "ctx", None),
            P("wsh", None, "ctx", None),
            P(("ctx", "wsh"), None),
            P(("ctx", "wsh"), None),
            P(("ctx", "wsh"), None),
            P(("ctx", "wsh"), None),
            P(("ctx", "wsh")),
            P(("ctx", "wsh"), None),
            P(None, ("ctx", "wsh"), None, None),
            P(None, ("ctx", "wsh"), None),
            P(("ctx", "wsh")),
        ),
        check_vma=False,
    )
```

time: 443 us -> 310 us (0.70); the launches traced: 442 us -> 304 us
  Pallas kernels: 331 us -> 291 us
  waiting for transfers between devices: 34.8 us -> 0 us
  local copies, waits for them, and re-layouts: 36.8 us -> 8.74 us
  between operations: 14.2 us -> 0.95 us
  other arithmetic: 15 us -> 4.03 us
  starting transfers between devices: 6.96 us -> 0 us
    ppermute x4 -> x0, waiting for transfers between devices: 33.4 us -> none  [exchange(): return lax.ppermute(rows, 'ctx', pairs)]
    pallas_call x1, Pallas kernels: 101 us -> 69.5 us  [finish(): comm_call(functools.partial(finish_kernel, outers), [shape((count, D), BF...]
    pallas_call x7 -> x3, Pallas kernels: 189 us -> 175 us  [the longest x1 120 us: opening(): comm_call(functools.partial(opening_kernel, outers), [shape((D, wide), BF...]
    reshape x9 -> x0, local copies, waits for them, and re-layouts: 11 us -> none  [the longest x2 5.73 us: body(): inner_sum = near_in[..., :2 * hidden_units].reshape(INNER, 2, OWN, owner_...]
    slice x12 -> x0, local copies, waits for them, and re-layouts: 7.31 us -> none  [the longest x1 3.77 us: body(): arrived = [exchange(give[portion], 1) for portion in portions]]
    convert_element_type x6 -> x1, other arithmetic: 7.37 us -> 0.07 us  [body(): angles = flat_pos.astype(f32)[:, None] * frequency[None, :]]
    ppermute x4 -> x0, starting transfers between devices: 6.81 us -> none  [exchange(): return lax.ppermute(rows, 'ctx', pairs)]
  transfers between devices with their start and end apart: 8 -> 0, of which waited for: 2 -> 0; matrix products, arithmetic and copies ran while one was open for 6% -> 0% of each run, Pallas kernels for 66% -> 0%
where the time goes in v3:
time: 310 us; the launch traced here: 304 us
  Pallas kernels  291 us (94%)
  local copies, waits for them, and re-layouts  8.74 us (3%)
  other arithmetic  4.03 us (1%)
    pallas_call x1, Pallas kernels, opening(): comm_call(functools.partial(opening_kernel, outers), [shape((D, wide), BF...  120 us
    pallas_call x1, Pallas kernels, finish(): comm_call(functools.partial(finish_kernel, outers), [shape((count, D), BF...  69.5 us
    pallas_call x1, Pallas kernels, turning(): comm_call(functools.partial(turning_kernel, outers), [shape((count, D), F...  53.4 us
    pallas_call x1, Pallas kernels, owners(): comm_call(functools.partial(owners_kernel, devices, count, near_count), s...  45.6 us
    unnamed x15, local copies, waits for them, and re-layouts  6.51 us

profile of v3, /device:TPU:0, one launch (start us, length us, event | category | flops | bytes accessed | tf_op | source)
XLA Modules:
  0.0 304.3 jit_solution(8537528822148426257)
XLA Ops:
  0.6 0.1 add_multiply_fusion
  0.7 1.3 convert_reduce_fusion.starts
  2.1 0.1 add_convert_fusion
  2.1 0.1 convert_element_type.15
  2.2 0.1 pad.13.clone
  2.3 0.7 broadcast_in_dim.6
  3.0 0.7 broadcast_in_dim.7
  3.7 1.4 maximum_maximum_fusion.small
  5.1 0.3 fusion
  5.4 0.8 pad_maximum_fusion
  6.2 119.7 %opening.1 = (bf16[1024,2048]{1,0:T(8,128)(2,1)}, bf16[1024,1024]{1,0:T(8,128)(2,1)}, bf16[32,1024]{1,0:T(8,128)(2,1)}, bf16[128,1024]{1,0:T(8,128)(2,1)}, bf16[...) custom-call(s32[8]{0:T(128)} %convert_reduce_fusion.starts, ...), custom_call_target="tpu_custom_call" | custom-call | flops 99999997952 | bytes 314572800 | tf_op jit(solution)/shard_map/opening/pallas_call | solution.py:1286
  125.9 53.4 %turning.1 = (f32[128,1024]{1,0:T(8,128)}, bf16[128,1024]{1,0:T(8,128)(2,1)}, bf16[128,1024]{1,0:T(8,128)(2,1)}, f32[32,1024]{1,0:T(8,128)}, bf16[8,128,1024]{2,...) custom-call(s32[8]{0:T(128)} %convert_reduce_fusion.starts, ...), custom_call_target="tpu_custom_call" | custom-call | flops 35000000512 | bytes 110100480 | tf_op jit(solution)/shard_map/turning/pallas_call | solution.py:1607
  179.3 69.5 %finish.1 = (bf16[128,1024]{1,0:T(8,128)(2,1)}, f32[128,1024]{1,0:T(8,128)}, bf16[1024,384]{1,0:T(8,128)(2,1)}, bf16[1024,128]{1,0:T(8,128)(2,1)}, bf16[2,2,128,768]{3,2,1,0:T(8,128)(2,1)}) custom-call(bf16[32,64,1024]{2,1,0:T(8,128)(2,1)} %get-tuple-element.65.part, bf16[2,2,2,128,1024]{4,3,2,1,0:T(8,128)(2,1)} %bitcast.30, ...), custom_call_target="tpu_custom_call" | custom-call | flops 60000002048 | bytes 188743680 | tf_op jit(solution)/shard_map/finish/pallas_call | solution.py:708
  248.7 0.0 copy-start.5
  248.7 0.0 copy-start.4
  248.8 45.6 %owners.1 = (bf16[32,32,384]{2,1,0:T(8,128)(2,1)}, bf16[32,32,128]{2,1,0:T(8,128)(2,1)}, bf16[8,2,32,768]{3,2,1,0:T(8,128)(2,1)}, bf16[8,2,32,768]{3,2,1,0:T(8,128)(2,1)}) custom-call(bf16[1024,384]{1,0:T(8,128)(2,1)} %get-tuple-element.76.refs_0_, bf16[1024,128]{1,0:T(8,128)(2,1)} %get-tuple-element.77.refs_1_, bf16[2,8,32,768]{3,2,1,0:T(8,128)(2,1)} %bitcast.32, ...), custom_call_target="tpu_custom_call" | custom-call | flops 20000000000 | bytes 62914560 | tf_op jit(solution)/shard_map/owners/pallas_call | solution.py:298
  294.4 0.0 copy-start
  294.4 1.1 copy-done
  295.5 0.0 copy-start.1
  295.5 1.1 copy-done.1
  296.7 0.0 copy-start.2
  296.7 1.1 copy-done.2
  297.8 0.0 copy-start.3
  297.8 0.9 copy-done.3
  298.7 2.5 assemble.1
  301.2 0.7 slice_reduce_fusion
  301.9 0.7 copy.29
  302.6 0.0 copy-done.5
  302.6 0.7 copy.32
  303.3 0.0 copy-done.4
  303.3 0.8 copy.33
  (2 shorter events, 0.0 us)
Async XLA Ops:
  248.7 53.8 %copy-start.5 = (bf16[128,1024]{1,0:T(8,128)(2,1)S(1)}, bf16[128,1024]{1,0:T(8,128)(2,1)}, u32[]{:S(2)}) copy-start(bf16[128,1024]{1,0:T(8,128)(2,1)} %get-tuple-element.74) | copy-start | bytes 786436
  248.7 54.5 %copy-start.4 = (f32[128,1024]{1,0:T(8,128)S(1)}, f32[128,1024]{1,0:T(8,128)}, u32[]{:S(2)}) copy-start(f32[128,1024]{1,0:T(8,128)} %get-tuple-element.75) | copy-start | bytes 1572868
  294.4 1.1 copy-start
  295.5 1.1 copy-start.1
  296.7 1.1 copy-start.2
  297.8 0.9 copy-start.3

commit v4 on v3

--- a/solution.py
+++ b/solution.py
@@ -352,6 +352,13 @@
 
 
 DOCS = 8
+
+
+def doc_starts(segments):
+    return [
+        jnp.sum(jnp.where(segments < d, 1.0, 0.0), axis=1, keepdims=True).astype(jnp.int32)
+        for d in range(DOCS)
+    ]
 
 
 def reach(starts, place):
@@ -491,10 +498,13 @@
     left_in,
     rows_ref,
     z_ref,
+    near_in,
     out_ref,
     token_ref,
     attn_ref,
     small_o,
+    near_o,
+    next_o,
     z_o,
     wqkv_ref,
     left_ref,
@@ -504,6 +514,7 @@
     half_in,
     y_in,
     z_in,
+    m_own,
     m_near,
     m_x,
     m_y,
@@ -524,6 +535,10 @@
     vr,
     ls,
     os,
+    ps,
+    pr,
+    qs,
+    qr,
 ):
     at = Place()
     blocks, rows, full = part.shape
@@ -531,7 +546,15 @@
         pltpu.make_async_copy(wqkv_in, wqkv_ref, ls.at[0]),
         pltpu.make_async_copy(left_in, left_ref, ls.at[1]),
     ]
-    for copy in loads:
+    moe_load = pltpu.make_async_copy(moe.at[:, at.core], m_own, ls.at[2])
+    near_keep = pltpu.make_async_copy(near_in.at[:, at.j], near_o.at[at.j], ls.at[3])
+    z_loads = [
+        pltpu.make_async_copy(
+            z_ref.at[:, e], z_sums.at[e, pl.ds(0, outers // 2)], ls.at[4 + e]
+        )
+        for e in range(z_sums.shape[0])
+    ]
+    for copy in z_loads + [moe_load] + loads + [near_keep]:
         copy.start()
     width = full // 2
     cuts = 4
@@ -547,9 +570,9 @@
         Halving(at, outers, z_sums.at[e], z_in_rows.at[e], vs.at[e], vr.at[e])
         for e in range(z_sums.shape[0])
     ]
-    for e in range(len(rest)):
-        z_sums[e, pl.ds(0, outers // 2)] = z_ref[:, e]
     meet([at.relative(*bits)[0] for bits in OTHERS] + far + [at.beside])
+    for copy in z_loads:
+        copy.wait()
     if outers > 2:
         rest[0].start(0)
 
@@ -581,6 +604,12 @@
                     )
                     copy.start()
                     first[k, y, h, o] = copy
+    nears = []
+    for slot, bits in enumerate(OTHERS):
+        device, j_to = at.relative(*bits)
+        copy = remote(near_in.at[:, j_to], near_o.at[at.j], ps.at[slot], pr.at[slot], device)
+        copy.start()
+        nears.append(copy)
     near = remote(moe.at[:, 1 - at.core], m_near, ns.at[0], nr.at[0], sib)
     near.start()
     for copy in own_loads:
@@ -602,9 +631,10 @@
         copy.start()
         second.append(copy)
     near.wait_recv()
+    moe_load.wait()
     for y in range(2):
         for w in range(2):
-            total = moe[y, at.core, w].astype(F32) + m_near[y, w].astype(F32)
+            total = m_own[y, w].astype(F32) + m_near[y, w].astype(F32)
             m_near[y, w] = total.astype(BF16)
     cross = remote(m_near.at[:, 1 - at.w], m_x, ns.at[1], nr.at[1], across)
     cross.start()
@@ -651,6 +681,22 @@
     if outers > 2:
         for halving in rest[1:]:
             halving.start(0)
+    rest[0].finish()
+    level = rest[0].levels[-1][0]
+    owner_rows = next_o.shape[2]
+
+    def rows_of(j):
+        within = pl.multiple_of(lax.rem(j, 4) * owner_rows, owner_rows)
+        return 0, level, j // 4, pl.ds(within, owner_rows)
+
+    for slot, bits in enumerate(OTHERS):
+        device, j_to = at.relative(*bits)
+        copy = remote(
+            z_sums.at[rows_of(j_to)], next_o.at[at.j, 0], qs.at[slot], qr.at[slot], device
+        )
+        copy.start()
+        nears.append(copy)
+    next_o[at.j, 0] = z_sums[rows_of(at.j)]
     cosine = cos_ref[...]
     sine = -sin_ref[...]
     base = HEADS * HEAD_DIM
@@ -693,13 +739,16 @@
     grads = swapped[...].reshape(all_rows, wide + D // PLANE)
     attn_ref[:, :wide] = dot_tn(left_one, grads[:, :wide]).astype(BF16)
     attn_ref[:, wide:] = dot_tn(left_mixed, grads[:, wide:]).astype(BF16)
-    for e in range(len(rest)):
-        z_o[e] = rest[e].finish()
+    for e in range(1, len(rest)):
+        z_o[e - 1] = rest[e].finish()
+    near_keep.wait()
+    for copy in nears:
+        copy.wait()
     for copy in list(first.values()) + second + third + swaps + [near, cross, along]:
         copy.wait_send()
 
 
-def finish(part, moe, arrays, z_half, ctx_count):
+def finish(part, moe, arrays, z_half, near, ctx_count):
     outers = ctx_count // INNER
     blocks, rows, full = part.shape
     count = 2 * rows
@@ -712,10 +761,12 @@
             shape((count, D), F32),
             shape((D, columns), BF16),
             shape((D, 128), BF16),
-            shape(z_half.shape[1:], BF16),
+            shape((PLANE, near.shape[0]) + near.shape[2:], BF16),
+            shape((PLANE, 1) + near.shape[2:], BF16),
+            shape((z_half.shape[1] - 1,) + z_half.shape[2:], BF16),
         ],
-        [ANY] + [VMEM] * (len(arrays) - 2) + [ANY] * 2 + [VMEM] * 2,
-        [VMEM] * 5,
+        [ANY] * 2 + [VMEM] * (len(arrays) - 3) + [ANY] * 2 + [VMEM] + [ANY] * 2,
+        [VMEM] * 7,
         [
             pltpu.VMEM((D, 2 * full), BF16),
             pltpu.VMEM((2, PLANE, count, D), BF16),
@@ -725,6 +776,7 @@
             pltpu.VMEM((2, 2, outers, rows, full), BF16),
             pltpu.VMEM((2, outers, rows, full), BF16),
             pltpu.VMEM((outers, 2, rows, full), BF16),
+            pltpu.VMEM((2, 2, count, D), BF16),
             pltpu.VMEM((2, 2, count, D), BF16),
             pltpu.VMEM((2, count, D), BF16),
             pltpu.VMEM((count, D), BF16),
@@ -743,14 +795,18 @@
             DMA((7,)),
             DMA((z_half.shape[1], outers)),
             DMA((z_half.shape[1], outers)),
-            DMA((2,)),
+            DMA((4 + z_half.shape[1],)),
             DMA((2, 2, outers)),
+            DMA((7,)),
+            DMA((7,)),
+            DMA((7,)),
+            DMA((7,)),
         ],
         3,
         "finish",
         vmem=63 * 2**20,
         us=60,
-    )(part, moe.reshape(2, 2, 2, count, D), *arrays, z_half)
+    )(part, moe.reshape(2, 2, 2, count, D), *arrays, z_half, near)
 
 
 def gate_columns(gates, cols):
@@ -780,7 +836,7 @@
 
 def opening_kernel(
     outers,
-    starts,
+    seg_ref,
     tok_ref,
     wq,
     wk,
@@ -1132,7 +1188,7 @@
     store_kv = pltpu.make_async_copy(kv, kv_o, hs.at[4])
     store_kv.start()
     attend_rows(
-        starts,
+        doc_starts(seg_ref[...]),
         q_o,
         kv,
         tok_v,
@@ -1305,7 +1361,7 @@
             shape((OWN - FIRST, outers // 2, 2, 2, z_rows, 3 * units), BF16),
             shape((2, PLANE, count, D), BF16),
         ],
-        [SMEM] + [ANY] * 9 + [VMEM] * 2 + [ANY] * 2,
+        [VMEM] + [ANY] * 9 + [VMEM] * 2 + [ANY] * 2,
         [ANY] * 2 + [VMEM] * 3 + [ANY] + [VMEM] * 8 + [ANY] * 4,
         [
             vm((D, wide), BF16),
@@ -1351,7 +1407,7 @@
 
 def turning_kernel(
     outers,
-    starts,
+    seg_ref,
     z_ref,
     grad_in,
     part_in,
@@ -1361,12 +1417,12 @@
     gate_ref,
     kept_ref,
     small_ref,
-    sum_ref,
-    cot_ref,
+    sum_in,
+    cot_in,
     wo_in,
-    raw_ref,
-    total_ref,
-    q_ref,
+    raw_in,
+    total_in,
+    q_in,
     kv_in,
     cos_ref,
     sin_ref,
@@ -1378,6 +1434,11 @@
     near_o,
     z_o,
     dkv_ref,
+    sum_ref,
+    cot_ref,
+    raw_ref,
+    total_ref,
+    q_ref,
     part,
     kept_all,
     out_w,
@@ -1408,6 +1469,7 @@
     us,
     ur,
     ks,
+    rs,
 ):
     at = Place()
     count = q_ref.shape[0]
@@ -1428,8 +1490,9 @@
     ]
     for copy in loads + weights:
         copy.start()
+    z_load = pltpu.make_async_copy(z_ref, z_sums.at[pl.ds(0, outers // 2)], rs.at[5])
+    z_load.start()
     rest = Halving(at, outers, z_sums, z_in, vs, vr)
-    z_sums[pl.ds(0, outers // 2)] = z_ref[...]
     own_rows = []
     for e in range(OWN - FIRST):
         copy = pltpu.make_async_copy(
@@ -1437,6 +1500,21 @@
         )
         copy.start()
         own_rows.append(copy)
+    row_loads = [
+        pltpu.make_async_copy(src, dst, rs.at[index])
+        for index, (src, dst) in enumerate(
+            (
+                (sum_in, sum_ref),
+                (cot_in, cot_ref),
+                (raw_in, raw_ref),
+                (total_in, total_ref),
+                (q_in, q_ref),
+            )
+        )
+    ]
+    for copy in row_loads:
+        copy.start()
+    starts = doc_starts(seg_ref[...])
     meet(
         [at.relative(*bits)[0] for bits in OTHERS]
         + [at.beside]
@@ -1451,6 +1529,7 @@
         copy = remote(grad_in.at[e, :, :, 1 - at.y], y_in.at[e], us.at[e], ur.at[e], at.beside)
         copy.start()
         y_sends.append(copy)
+    z_load.wait()
     if rest.bits:
         rest.start(0)
     small_copies = []
@@ -1475,7 +1554,7 @@
         second.append(copy)
 
     loads[1].wait()
-    for copy in weights:
+    for copy in weights + row_loads:
         copy.wait()
 
     def moe_rows(j, carry):
@@ -1598,7 +1677,7 @@
 
 
 def turning(
-    outers, starts, z_first, grads, part, picks, kept_units, expert_out, gate, kept, small, first_sum, cot, output_w, raw, total, queries, kv_all, cosine, sine
+    outers, segments, z_first, grads, part, picks, kept_units, expert_out, gate, kept, small, first_sum, cot, output_w, raw, total, queries, kv_all, cosine, sine
 ):
     shape = jax.ShapeDtypeStruct
     count, width = queries.shape
@@ -1616,9 +1695,14 @@
             shape((outers // 2, OWN - FIRST) + z_first.shape[2:], BF16),
             shape(kv_all.shape, BF16),
         ],
-        [SMEM, VMEM, ANY, ANY, VMEM, ANY, ANY] + [VMEM] * 5 + [ANY] + [VMEM] * 3 + [ANY] + [VMEM] * 2,
+        [VMEM] + [ANY] * 3 + [VMEM] + [ANY] * 2 + [VMEM] * 3 + [ANY] * 7 + [VMEM] * 2,
         [VMEM] * 7 + [ANY],
         [
+            vm((count, D), F32),
+            vm((count, D), BF16),
+            vm((count, width), F32),
+            vm((count, width), F32),
+            vm((count, width), BF16),
             vm((2, 2, 2, count, D), BF16),
             vm(kept_units.shape, BF16),
             vm((OWN, D, units), BF16),
@@ -1649,13 +1733,14 @@
             DMA((OWN - FIRST,)),
             DMA((OWN - FIRST,)),
             DMA((2,)),
+            DMA((6,)),
         ],
         5,
         "turning",
         vmem=62 * 2**20,
         us=35,
     )(
-        starts,
+        segments,
         z_first,
         grads,
         part.reshape(2, 2, 2, count, D),
@@ -1677,9 +1762,20 @@
     )
 
 
-def assemble_kernel(
-    outers, attn_in, small_in, near_one, near, wq, wk, wv, wo, small, inner, outer
-):
+def assemble_kernel(outers, counts, *refs):
+    size = 2 + len(counts)
+    sources, refs = refs[:size], refs[size:]
+    wq, wk, wv, wo, small, inner, outer = refs[:7]
+    held, sems = refs[7 : 7 + size], refs[7 + size]
+    loads = [
+        pltpu.make_async_copy(sources[k], held[k], sems.at[k]) for k in range(size)
+    ]
+    for copy in loads:
+        copy.start()
+    attn_in, small_in = held[:2]
+    for copy in loads:
+        copy.wait()
+    experts = [(near, k) for near, many in zip(held[2:], counts) for k in range(many)]
     qkv_cols = wq.shape[1] * 2 // PLANE
     devices = outers * PLANE
     for j in range(PLANE):
@@ -1703,14 +1799,16 @@
         cols = slice((j % 2) * units, (j % 2 + 1) * units)
         for k in range(OWN):
             e = (j // 2) * OWN + k
-            block = (near_one[j, k] if k < FIRST else near[j, k - FIRST]).astype(F32)
+            near, at = experts[k]
+            block = near[j, at].astype(F32)
             inner[e, :, :, cols] = block[:, : 2 * units].reshape(rows, 2, units)
             outer[e, :, cols] = block[:, 2 * units :]
 
 
-def assemble(attn_in, small_in, near_one, near, outers):
+def assemble(attn_in, small_in, nears, outers):
     rows = attn_in.shape[1]
-    units = near.shape[-1] // 3
+    units = nears[0].shape[-1] // 3
+    sources = [attn_in, small_in] + nears
     shape = jax.ShapeDtypeStruct
     outs = [
         shape((rows, 1024), F32),
@@ -1722,15 +1820,14 @@
         shape((EXPERTS, rows, 2 * units), F32),
     ]
     return pl.pallas_call(
-        functools.partial(assemble_kernel, outers),
+        functools.partial(assemble_kernel, outers, [near.shape[1] for near in nears]),
         out_shape=outs,
-        in_specs=[VMEM] * 4,
+        in_specs=[ANY] * len(sources),
         out_specs=[VMEM] * 7,
-        compiler_params=pltpu.CompilerParams(
-            vmem_limit_bytes=room([attn_in, small_in, near_one, near] * 2 + outs)
-        ),
+        scratch_shapes=[pltpu.VMEM(a.shape, a.dtype) for a in sources] + [DMA((len(sources),))],
+        compiler_params=pltpu.CompilerParams(vmem_limit_bytes=60 * 2**20),
         name="assemble",
-    )(attn_in, small_in, near_one, near)
+    )(*sources)
 
 
 def body(
@@ -1768,9 +1865,6 @@
     block_ids = jnp.stack([ctx_index, block_total - 1 - ctx_index])
     query_pos = block_ids[:, None] * block_rows + jnp.arange(block_rows, dtype=jnp.int32)[None, :]
     flat_pos = query_pos.reshape(tok_count)
-    starts = jnp.sum(
-        (segments < jnp.arange(DOCS, dtype=jnp.int32)[:, None]).astype(jnp.int32), axis=1
-    )
     frequency = jnp.exp(
         -jnp.log(jnp.float32(THETA))
         * jnp.arange(HEAD_DIM // 2, dtype=jnp.float32)
@@ -1801,7 +1895,7 @@
         expert_grads,
         left,
     ) = opening(
-        starts,
+        segments,
         token_low,
         w_query,
         w_key,
@@ -1828,7 +1922,7 @@
         kv_terms,
     ) = turning(
         outers,
-        starts,
+        segments,
         first_half,
         expert_grads,
         part,
@@ -1848,7 +1942,7 @@
         cosine,
         sine,
     )
-    output, token_grad, attn_part, small_part, near = finish(
+    output, token_grad, attn_part, small_part, near_first, near_next, near = finish(
         kv_terms,
         moe_part,
         [
@@ -1865,20 +1959,18 @@
             small_rows,
         ],
         second_half,
+        near_one.reshape(FIRST, PLANE, owner_rows, -1),
         ctx_count,
     )
-    attn_in, small_in, near_one, near = owners(
+    attn_in, small_in, near_last = owners(
         [attn_part, small_part],
-        [
-            rows.reshape(-1, PLANE, owner_rows, rows.shape[-1])
-            for rows in (near_one, near)
-        ],
+        [near.reshape(-1, PLANE, owner_rows, near.shape[-1])],
         devices,
         7,
         "owners",
     )
     query_sum, key_sum, value_sum, output_sum, small_sum, inner_sum, outer_sum = assemble(
-        attn_in, small_in, near_one, near, outers
+        attn_in, small_in, [near_first, near_next, near_last], outers
     )
     return (
         output.reshape(tokens.shape),

time: 310 us -> 300 us (0.968)
  Pallas kernels: 291 us -> 285 us
    pallas_call x1, Pallas kernels: 45.6 us -> 32.1 us  [owners(): comm_call(functools.partial(owners_kernel, devices, count, near_count), s...]
    pallas_call x1, Pallas kernels: 69.5 us -> 75 us  [finish(): comm_call(functools.partial(finish_kernel, outers), [shape((count, D), BF...]
    unnamed x15 -> x7, local copies, waits for them, and re-layouts: 6.51 us -> 2.89 us
where the time goes in v4:
time: 300 us; the launch traced here: 294 us
  Pallas kernels  285 us (95%)
  local copies, waits for them, and re-layouts  5.92 us (2%)
    pallas_call x1, Pallas kernels, opening(): comm_call(functools.partial(opening_kernel, outers), [shape((D, wide), BF...  119 us
    pallas_call x1, Pallas kernels, finish(): comm_call(functools.partial(finish_kernel, outers), [shape((count, D), BF...  75 us
    pallas_call x1, Pallas kernels, turning(): comm_call(functools.partial(turning_kernel, outers), [shape((count, D), F...  54.1 us
    pallas_call x1, Pallas kernels, owners(): comm_call(functools.partial(owners_kernel, devices, count, near_count), s...  32.1 us

profile of v4, /device:TPU:0, one launch (start us, length us, event | category | flops | bytes accessed | tf_op | source)
XLA Modules:
  0.0 294.5 jit_solution(6449040800490147568)
XLA Ops:
  0.6 0.1 add_multiply_fusion
  0.7 0.1 add_convert_fusion
  0.8 0.1 convert_element_type.11
  0.9 0.1 pad.13.clone
  1.0 0.7 broadcast_in_dim.6
  1.7 0.7 broadcast_in_dim.14
  2.3 1.4 maximum_maximum_fusion.small
  3.8 0.3 fusion
  4.1 0.8 pad_maximum_fusion
  4.9 119.3 %opening.1 = (bf16[1024,2048]{1,0:T(8,128)(2,1)}, bf16[1024,1024]{1,0:T(8,128)(2,1)}, bf16[32,1024]{1,0:T(8,128)(2,1)}, bf16[128,1024]{1,0:T(8,128)(2,1)}, bf16[...) custom-call(s32[1,2048]{1,0:T(1,128)} %seg_ref.3, ...), custom_call_target="tpu_custom_call" | custom-call | flops 99999997952 | bytes 314572800 | tf_op jit(solution)/shard_map/opening/pallas_call | solution.py:1342
  124.2 54.1 %turning.1 = (f32[128,1024]{1,0:T(8,128)}, bf16[128,1024]{1,0:T(8,128)(2,1)}, bf16[128,1024]{1,0:T(8,128)(2,1)}, f32[32,1024]{1,0:T(8,128)}, bf16[8,128,1024]{2,...) custom-call(s32[1,2048]{1,0:T(1,128)} %seg_ref.3, ...), custom_call_target="tpu_custom_call" | custom-call | flops 35000000512 | bytes 110100480 | tf_op jit(solution)/shard_map/turning/pallas_call | solution.py:1686
  178.3 75.0 %finish.1 = (bf16[128,1024]{1,0:T(8,128)(2,1)}, f32[128,1024]{1,0:T(8,128)}, bf16[1024,384]{1,0:T(8,128)(2,1)}, bf16[1024,128]{1,0:T(8,128)(2,1)}, bf16[8,2,32,7...) custom-call(bf16[32,64,1024]{2,1,0:T(8,128)(2,1)} %get-tuple-element.66.part, ...), custom_call_target="tpu_custom_call" | custom-call | flops 60000002048 | bytes 188743680 | tf_op jit(solution)/shard_map/finish/pallas_call | solution.py:757
  253.3 0.0 copy-start.1
  253.3 32.1 %owners.1 = (bf16[32,32,384]{2,1,0:T(8,128)(2,1)}, bf16[32,32,128]{2,1,0:T(8,128)(2,1)}, bf16[8,1,32,768]{3,2,1,0:T(8,128)(2,1)}) custom-call(bf16[1024,384]{1,0:T(8,128)(2,1)} %get-tuple-element.78.refs_0_, bf16[1024,128]{1,0:T(8,128)(2,1)} %get-tuple-element.79.refs_1_, bf16[1,8,32,768]{3,2,1,0:T(8,128)(2,1)} %bitcast.31), custom_call_target="tpu_custom_call" | custom-call | flops 20000000000 | bytes 62914560 | tf_op jit(solution)/shard_map/owners/pallas_call | solution.py:298
  285.4 0.0 copy-start
  285.4 4.2 %assemble.1 = (f32[32,1024]{1,0:T(8,128)}, f32[32,512]{1,0:T(8,128)}, f32[32,512]{1,0:T(8,128)}, f32[32,1024]{1,0:T(8,128)}, f32[32,128]{1,0:T(8,128)}, /*index=...) custom-call(bf16[32,32,384]{2,1,0:T(8,128)(2,1)} %get-tuple-element.81.refs_0_, ...), custom_call_target="tpu_custom_call" | custom-call | tf_op jit(solution)/shard_map/assemble/pallas_call | solution.py:1822
  289.7 1.5 slice_reduce_fusion
  291.2 1.4 copy.28
  292.6 0.0 copy-done.1
  292.6 0.7 copy.31
  293.3 0.0 copy-done
  293.3 0.8 copy.32
  (2 shorter events, 0.0 us)
Async XLA Ops:
  253.3 39.3 %copy-start.1 = (bf16[128,1024]{1,0:T(8,128)(2,1)S(1)}, bf16[128,1024]{1,0:T(8,128)(2,1)}, u32[]{:S(2)}) copy-start(bf16[128,1024]{1,0:T(8,128)(2,1)} %get-tuple-element.76) | copy-start | bytes 786436
  285.4 7.8 %copy-start = (f32[128,1024]{1,0:T(8,128)S(1)}, f32[128,1024]{1,0:T(8,128)}, u32[]{:S(2)}) copy-start(f32[128,1024]{1,0:T(8,128)} %get-tuple-element.77) | copy-start | bytes 1572868

commit v5 on v4

--- a/solution.py
+++ b/solution.py
@@ -17,6 +17,7 @@
 PLANE = 8
 INNER = 4
 OWN = EXPERTS // INNER
+PIECES = 2
 FIRST = OWN // 2
 
 
@@ -106,8 +107,17 @@
     return min(total + spare * 2**20, 62 * 2**20)
 
 
+def far_first(outers):
+    return outers == 4
+
+
+def far_partner(at):
+    return (at.c + INNER * 2 * (1 - 2 * (at.outer // 2)), at.w)
+
+
 class Halving:
-    def __init__(self, at, outers, sums, arrived, send, recv):
+    def __init__(self, at, outers, sums, arrived, send, recv, cols=slice(None)):
+        self.cols = cols
         self.at, self.sums, self.arrived = at, sums, arrived
         self.send, self.recv = send, recv
         self.bits = [2**k for k in range(1, outers.bit_length() - 1)]
@@ -117,6 +127,9 @@
             self.levels.append((start + many, many // 2))
         self.copies = []
 
+    def pick(self, index):
+        return index, slice(None), slice(None), self.cols
+
     def device(self, bit):
         at = self.at
         return (at.c + INNER * bit * (1 - 2 * ((at.outer // bit) % 2)), at.w)
@@ -127,8 +140,8 @@
         start, many = self.levels[step]
         for m in range(many // 2):
             copy = remote(
-                self.sums.at[start + 2 * m + 1 - side],
-                self.arrived.at[start + m],
+                self.sums.at[self.pick(start + 2 * m + 1 - side)],
+                self.arrived.at[self.pick(start + m)],
                 self.send.at[start + m],
                 self.recv.at[start + m],
                 self.device(bit),
@@ -142,8 +155,9 @@
         after, half = self.levels[step + 1]
         for m in range(half):
             self.copies[len(self.copies) - half + m].wait_recv()
-            total = self.sums[start + 2 * m + side].astype(F32) + self.arrived[start + m].astype(F32)
-            self.sums[after + m] = total.astype(BF16)
+            total = self.sums[self.pick(start + 2 * m + side)].astype(F32)
+            total = total + self.arrived[self.pick(start + m)].astype(F32)
+            self.sums[self.pick(after + m)] = total.astype(BF16)
 
     def finish(self):
         for step in range(len(self.bits)):
@@ -152,7 +166,7 @@
             self.add(step)
         for copy in self.copies:
             copy.wait_send()
-        return self.sums[self.levels[-1][0]]
+        return self.sums[self.pick(self.levels[-1][0])]
 
 
 def gather_start(at, pairs, send, recv, local):
@@ -864,6 +878,7 @@
     kept_o,
     pick_o,
     z_o,
+    za_o,
     part_o,
     kept_units_o,
     grad_o,
@@ -891,6 +906,7 @@
     pick_cols,
     staged,
     y_in,
+    za_in,
     xs,
     xr,
     fs,
@@ -916,6 +932,8 @@
     ul,
     vs,
     vr,
+    fas,
+    far_r,
 ):
     at = Place()
     blocks, rows = kv.shape[:2]
@@ -948,7 +966,10 @@
         copy.start()
     load_expert(0)
     load_expert(1)
-    meet([at.relative(*bits)[0] for bits in XY + [(0, 1, 0)]] + far + [at.beside])
+    meet(
+        [at.relative(*bits)[0] for bits in XY + [(0, 1, 0)]] + far + [at.beside]
+        + ([far_partner(at)] if far_first(outers) else [])
+    )
 
     pieces = [(wk, wqkv, 1024), (wv, wqkv, 1536), (wq, wqkv, 0), (wo, wout, 0)]
     sends, passed, keeps = {}, {}, []
@@ -1228,10 +1249,24 @@
     passed[3].wait_send()
     hid_t = wout
     hid_t[...] = hid[...].reshape(tokens, D).T
+    late = [slice(None)] * FIRST
+    if far_first(outers):
+        late[0] = pl.ds(units, 2 * units)
     y_sends = [
-        remote(staged.at[e, :, :, 1 - at.y], y_in.at[e], vs.at[e], vr.at[e], at.beside)
+        remote(
+            staged.at[e, :, :, 1 - at.y, :, late[e]],
+            y_in.at[e, :, :, :, late[e]],
+            vs.at[e],
+            vr.at[e],
+            at.beside,
+        )
         for e in range(FIRST)
     ]
+    upper = at.outer // 2
+    if far_first(outers):
+        far_send = remote(
+            staged.at[0, 1 - upper, :, :, :, pl.ds(0, units)], za_in, fas, far_r, far_partner(at)
+        )
     at_lane = lax.broadcasted_iota(jnp.int32, cols.shape, 1)
     pick_cols[...] = jnp.zeros(pick_cols.shape, F32)
     store.wait()
@@ -1242,20 +1277,25 @@
     def expert(e, carry):
         wide = pl.ds(pl.multiple_of(e * 2 * units, 2 * units), 2 * units)
         tall = pl.ds(pl.multiple_of(e * units, units), units)
-        both = dot_nn(hid[...].reshape(tokens, D), inner_w[:, wide])
-        kept, pick, low = expert_step(
-            both, backs[:, tall].astype(F32), lane_of(cols[...], experts + e), units
-        )
-        backs[:, tall] = kept
-        low_all[:, wide] = low
-        pick_cols[...] = jnp.where(at_lane == e, pick, pick_cols[...])
+        many = tokens // PIECES
+        groups = PLANE // PIECES
+        for piece in range(PIECES):
+            here = slice(piece * many, (piece + 1) * many)
+            rows_in = hid[piece * groups : (piece + 1) * groups].reshape(many, D)
+            both = dot_nn(rows_in, inner_w[:, wide])
+            kept, pick, low = expert_step(
+                both, backs[here, tall].astype(F32), lane_of(cols[here, :], experts + e), units
+            )
+            backs[here, tall] = kept
+            low_all[here, wide] = low
+            pick_cols[here, :] = jnp.where(at_lane[here] == e, pick, pick_cols[here, :])
 
         shape = staged.shape[1:5]
         staged[e, :, :, :, :, : 2 * units] = (
-            dot_nn(hid_t[...], low).astype(BF16).reshape(*shape, 2 * units)
+            dot_nn(hid_t[...], low_all[:, wide]).astype(BF16).reshape(*shape, 2 * units)
         )
         staged[e, :, :, :, :, 2 * units :] = (
-            (RES_MULT * dot_nn(cot_t[...], kept)).astype(BF16).reshape(*shape, units)
+            (RES_MULT * dot_nn(cot_t[...], backs[:, tall])).astype(BF16).reshape(*shape, units)
         )
         for now in range(OWN):
 
@@ -1263,6 +1303,8 @@
             def _():
                 if now < FIRST:
                     y_sends[now].start()
+                    if now == 0 and far_first(outers):
+                        far_send.start()
                 else:
                     pltpu.make_async_copy(
                         staged.at[now], grad_o.at[now - FIRST], gd.at[now - FIRST]
@@ -1277,9 +1319,10 @@
         pick_o[j] = pick_cols[j * count : (j + 1) * count, :].T[:8]
     store_kept = pltpu.make_async_copy(backs, kept_units_o, hs.at[5])
     store_kept.start()
-    for j in range(PLANE):
-        here = slice(j * count, (j + 1) * count)
-        hid[j] = dot_nt(low_all[here, :], inner_w[...]).astype(BF16)
+    for j in range(0, PLANE, 4):
+        here = slice(j * count, (j + 4) * count)
+        rows_out = dot_nt(low_all[here, :], inner_w[...]).astype(BF16)
+        hid[j : j + 4] = rows_out.reshape(4, count, D)
     store_part = pltpu.make_async_copy(hid, part_o, hs.at[6])
     store_part.start()
 
@@ -1315,8 +1358,13 @@
         copy.wait_send()
     for e in range(FIRST):
         y_sends[e].wait()
-        total = staged[e, :, :, at.y].astype(F32) + y_in[e].astype(F32)
-        z_o[:, e] = total.astype(BF16)
+        total = staged[e, :, :, at.y, :, late[e]].astype(F32)
+        total = total + y_in[e, :, :, :, late[e]].astype(F32)
+        z_o[:, e, :, :, late[e]] = total.astype(BF16)
+    if far_first(outers):
+        far_send.wait()
+        total = staged[0, upper, :, :, :, :units].astype(F32) + za_in[...].astype(F32)
+        za_o[...] = total.astype(BF16)
     gather_wait(left_copies, left_passed)
     for copy in [store_kv, store_kept, store_part]:
         copy.wait()
@@ -1356,13 +1404,14 @@
             shape((EXPERTS, count), F32),
             shape((PLANE, 8, count), F32),
             shape((outers // 2, FIRST, 2, z_rows, 3 * units), BF16),
+            shape((2, 2, z_rows, units), BF16),
             shape((PLANE, count, D), BF16),
             shape((many, OWN * units), BF16),
             shape((OWN - FIRST, outers // 2, 2, 2, z_rows, 3 * units), BF16),
             shape((2, PLANE, count, D), BF16),
         ],
         [VMEM] + [ANY] * 9 + [VMEM] * 2 + [ANY] * 2,
-        [ANY] * 2 + [VMEM] * 3 + [ANY] + [VMEM] * 8 + [ANY] * 4,
+        [ANY] * 2 + [VMEM] * 3 + [ANY] + [VMEM] * 9 + [ANY] * 4,
         [
             vm((D, wide), BF16),
             vm((D, D), BF16),
@@ -1387,6 +1436,7 @@
             vm((many, 128), F32),
             vm((OWN, outers // 2, 2, 2, z_rows, 3 * units), BF16),
             vm((FIRST, outers // 2, 2, z_rows, 3 * units), BF16),
+            vm((2, 2, z_rows, units), BF16),
             DMA((5,)),
             DMA((5,)),
             DMA((4,)),
@@ -1397,7 +1447,7 @@
         + [DMA((2, 4 * outers))] * 2
         + [DMA((8,)), DMA((7,)), DMA((7,)), DMA]
         + [DMA((2 + OWN,)), DMA((2, 7)), DMA((2, 7)), DMA((2,)), DMA((2,))]
-        + [DMA((2, 7)), DMA((2, 7)), DMA((2,)), DMA((FIRST,)), DMA((FIRST,))],
+        + [DMA((2, 7)), DMA((2, 7)), DMA((2,)), DMA((FIRST,)), DMA((FIRST,)), DMA, DMA],
         1,
         "opening",
         vmem=64 * 2**20,
@@ -1409,6 +1459,7 @@
     outers,
     seg_ref,
     z_ref,
+    za_ref,
     grad_in,
     part_in,
     pick_send,
@@ -1457,6 +1508,8 @@
     z_in,
     y_own,
     y_in,
+    za_own,
+    za_in,
     ls,
     ss,
     sr,
@@ -1470,6 +1523,8 @@
     ur,
     ks,
     rs,
+    zas,
+    zar,
 ):
     at = Place()
     count = q_ref.shape[0]
@@ -1490,9 +1545,20 @@
     ]
     for copy in loads + weights:
         copy.start()
-    z_load = pltpu.make_async_copy(z_ref, z_sums.at[pl.ds(0, outers // 2)], rs.at[5])
-    z_load.start()
-    rest = Halving(at, outers, z_sums, z_in, vs, vr)
+    z_loads = [
+        pltpu.make_async_copy(z_ref.at[:, e], z_sums.at[e, pl.ds(0, outers // 2)], rs.at[5 + e])
+        for e in range(FIRST)
+    ]
+    za_load = pltpu.make_async_copy(za_ref.at[:, at.y], za_own, rs.at[5 + FIRST])
+    for copy in z_loads + [za_load]:
+        copy.start()
+    late = [slice(None)] * FIRST
+    if far_first(outers):
+        late[0] = pl.ds(units, 2 * units)
+    rest = [
+        Halving(at, outers, z_sums.at[e], z_in.at[e], vs.at[e], vr.at[e], late[e])
+        for e in range(FIRST)
+    ]
     own_rows = []
     for e in range(OWN - FIRST):
         copy = pltpu.make_async_copy(
@@ -1518,8 +1584,16 @@
     meet(
         [at.relative(*bits)[0] for bits in OTHERS]
         + [at.beside]
-        + [rest.device(bit) for bit in rest.bits]
+        + [rest[0].device(bit) for bit in rest[0].bits]
     )
+    for copy in z_loads:
+        copy.wait()
+    if outers > 2:
+        for halving in rest:
+            halving.start(0)
+    if far_first(outers):
+        za_send = remote(za_ref.at[:, 1 - at.y], za_in, zas, zar, at.beside)
+        za_send.start()
     sib, unused = at.relative(0, 1, 0)
     loads[0].wait()
     first = remote(part.at[:, 1 - at.core], near, ss, sr, sib)
@@ -1529,9 +1603,6 @@
         copy = remote(grad_in.at[e, :, :, 1 - at.y], y_in.at[e], us.at[e], ur.at[e], at.beside)
         copy.start()
         y_sends.append(copy)
-    z_load.wait()
-    if rest.bits:
-        rest.start(0)
     small_copies = []
     for slot, bits in enumerate(OTHERS):
         device, j_to = at.relative(*bits)
@@ -1667,7 +1738,13 @@
             ).astype(BF16)
     for chunk in range(keys // CHUNK - 2, keys // CHUNK):
         kv_store(chunk).wait()
-    near_o[...] = rest.finish()
+    for e in range(FIRST):
+        near_o[e, :, :, late[e]] = rest[e].finish()
+    za_load.wait()
+    if far_first(outers):
+        za_send.wait()
+        total = za_own[...].astype(F32) + za_in[...].astype(F32)
+        near_o[0, :, :, :units] = total.astype(BF16)
     for copy in own_rows:
         copy.wait()
     for e in range(OWN - FIRST):
@@ -1677,7 +1754,7 @@
 
 
 def turning(
-    outers, segments, z_first, grads, part, picks, kept_units, expert_out, gate, kept, small, first_sum, cot, output_w, raw, total, queries, kv_all, cosine, sine
+    outers, segments, z_first, z_far, grads, part, picks, kept_units, expert_out, gate, kept, small, first_sum, cot, output_w, raw, total, queries, kv_all, cosine, sine
 ):
     shape = jax.ShapeDtypeStruct
     count, width = queries.shape
@@ -1695,7 +1772,7 @@
             shape((outers // 2, OWN - FIRST) + z_first.shape[2:], BF16),
             shape(kv_all.shape, BF16),
         ],
-        [VMEM] + [ANY] * 3 + [VMEM] + [ANY] * 2 + [VMEM] * 3 + [ANY] * 7 + [VMEM] * 2,
+        [VMEM] + [ANY] * 4 + [VMEM] + [ANY] * 2 + [VMEM] * 3 + [ANY] * 7 + [VMEM] * 2,
         [VMEM] * 7 + [ANY],
         [
             vm((count, D), F32),
@@ -1717,10 +1794,12 @@
             vm((2 * PAIRS, 2 * count, 128), F32),
             vm((CHUNK, 2 * PAIRS * 128), F32),
             vm((2, CHUNK // (count // 2), count // 2, 2 * PAIRS * 128), BF16),
-            vm((outers,) + z_first.shape[1:], BF16),
-            vm((outers,) + z_first.shape[1:], BF16),
+            vm((FIRST, outers) + z_first.shape[2:], BF16),
+            vm((FIRST, outers) + z_first.shape[2:], BF16),
             vm((OWN - FIRST, outers // 2) + z_first.shape[2:], BF16),
             vm((OWN - FIRST, outers // 2) + z_first.shape[2:], BF16),
+            vm(z_far.shape[:1] + z_far.shape[2:], BF16),
+            vm(z_far.shape[:1] + z_far.shape[2:], BF16),
             DMA((4 + OWN + OWN - FIRST,)),
             DMA,
             DMA,
@@ -1728,12 +1807,14 @@
             DMA((3,)),
             DMA((7,)),
             DMA((7,)),
-            DMA((outers,)),
-            DMA((outers,)),
+            DMA((FIRST, outers)),
+            DMA((FIRST, outers)),
             DMA((OWN - FIRST,)),
             DMA((OWN - FIRST,)),
             DMA((2,)),
-            DMA((6,)),
+            DMA((6 + FIRST,)),
+            DMA,
+            DMA,
         ],
         5,
         "turning",
@@ -1742,6 +1823,7 @@
     )(
         segments,
         z_first,
+        z_far,
         grads,
         part.reshape(2, 2, 2, count, D),
         picks,
@@ -1765,8 +1847,8 @@
 def assemble_kernel(outers, counts, *refs):
     size = 2 + len(counts)
     sources, refs = refs[:size], refs[size:]
-    wq, wk, wv, wo, small, inner, outer = refs[:7]
-    held, sems = refs[7 : 7 + size], refs[7 + size]
+    wq, wk, wv, wo, router, gain_one, gain_two, inner, outer = refs[:9]
+    held, sems = refs[9 : 9 + size], refs[9 + size]
     loads = [
         pltpu.make_async_copy(sources[k], held[k], sems.at[k]) for k in range(size)
     ]
@@ -1792,7 +1874,10 @@
     total = small_in[0].astype(F32)
     for i in range(1, devices):
         total = total + small_in[i].astype(F32)
-    small[...] = total
+    turned = total.T
+    router[...] = turned[:EXPERTS]
+    gain_one[...] = turned[EXPERTS : EXPERTS + 1]
+    gain_two[...] = turned[EXPERTS + 1 : EXPERTS + 2]
     rows = wq.shape[0]
     units = outer.shape[-1] // 2
     for j in range(PLANE):
@@ -1815,7 +1900,9 @@
         shape((rows, 512), F32),
         shape((rows, 512), F32),
         shape((rows, D), F32),
-        shape((rows, 128), F32),
+        shape((EXPERTS, rows), F32),
+        shape((1, rows), F32),
+        shape((1, rows), F32),
         shape((EXPERTS, rows, 2, 2 * units), F32),
         shape((EXPERTS, rows, 2 * units), F32),
     ]
@@ -1823,7 +1910,7 @@
         functools.partial(assemble_kernel, outers, [near.shape[1] for near in nears]),
         out_shape=outs,
         in_specs=[ANY] * len(sources),
-        out_specs=[VMEM] * 7,
+        out_specs=[VMEM] * 9,
         scratch_shapes=[pltpu.VMEM(a.shape, a.dtype) for a in sources] + [DMA((len(sources),))],
         compiler_params=pltpu.CompilerParams(vmem_limit_bytes=60 * 2**20),
         name="assemble",
@@ -1890,6 +1977,7 @@
         kept,
         picks,
         first_half,
+        first_far,
         part,
         kept_units,
         expert_grads,
@@ -1924,6 +2012,7 @@
         outers,
         segments,
         first_half,
+        first_far,
         expert_grads,
         part,
         picks,
@@ -1969,9 +2058,17 @@
         7,
         "owners",
     )
-    query_sum, key_sum, value_sum, output_sum, small_sum, inner_sum, outer_sum = assemble(
-        attn_in, small_in, [near_first, near_next, near_last], outers
-    )
+    (
+        query_sum,
+        key_sum,
+        value_sum,
+        output_sum,
+        router_sum,
+        gain_one_sum,
+        gain_two_sum,
+        inner_sum,
+        outer_sum,
+    ) = assemble(attn_in, small_in, [near_first, near_next, near_last], outers)
     return (
         output.reshape(tokens.shape),
         token_grad.reshape(tokens.shape),
@@ -1979,11 +2076,11 @@
         key_sum,
         value_sum,
         output_sum,
-        small_sum[:, EXPERTS],
-        small_sum[:, :EXPERTS],
+        gain_one_sum[0],
+        router_sum.T,
         inner_sum,
         outer_sum,
-        small_sum[:, EXPERTS + 1],
+        gain_two_sum[0],
     )
 
 

time: 300 us -> 283 us (0.943); the launches traced: 294 us -> 283 us
  Pallas kernels: 285 us -> 276 us
    pallas_call x1, Pallas kernels: 54.1 us -> 50.8 us  [turning(): comm_call(functools.partial(turning_kernel, outers), [shape((count, D), F...]
where the time goes in v5:
time: 283 us
  Pallas kernels  276 us (98%)
  local copies, waits for them, and re-layouts  3.04 us (1%)
    pallas_call x1, Pallas kernels, opening(): comm_call(functools.partial(opening_kernel, outers), [shape((D, wide), BF...  117 us
    pallas_call x1, Pallas kernels, finish(): comm_call(functools.partial(finish_kernel, outers), [shape((count, D), BF...  74.2 us
    pallas_call x1, Pallas kernels, turning(): comm_call(functools.partial(turning_kernel, outers), [shape((count, D), F...  50.8 us
    pallas_call x1, Pallas kernels, owners(): comm_call(functools.partial(owners_kernel, devices, count, near_count), s...  30.3 us

profile of v5, /device:TPU:0, one launch (start us, length us, event | category | flops | bytes accessed | tf_op | source)
XLA Modules:
  0.0 282.6 jit_solution(3835468305188212633)
XLA Ops:
  0.6 0.1 add_multiply_fusion
  0.7 0.1 add_convert_fusion
  0.8 0.1 convert_element_type.11
  0.9 0.1 pad.13.clone
  1.0 0.7 broadcast_in_dim.6
  1.7 0.7 broadcast_in_dim.14
  2.3 1.4 maximum_maximum_fusion.small
  3.8 0.3 fusion
  4.1 0.8 pad_maximum_fusion
  4.9 116.6 %opening.1 = (bf16[1024,2048]{1,0:T(8,128)(2,1)}, bf16[1024,1024]{1,0:T(8,128)(2,1)}, bf16[32,1024]{1,0:T(8,128)(2,1)}, bf16[128,1024]{1,0:T(8,128)(2,1)}, bf16[...) custom-call(s32[1,2048]{1,0:T(1,128)} %seg_ref.3, ...), custom_call_target="tpu_custom_call" | custom-call | flops 99999997952 | bytes 314572800 | tf_op jit(solution)/shard_map/opening/pallas_call | solution.py:1390
  121.5 50.8 %turning.1 = (f32[128,1024]{1,0:T(8,128)}, bf16[128,1024]{1,0:T(8,128)(2,1)}, bf16[128,1024]{1,0:T(8,128)(2,1)}, f32[32,1024]{1,0:T(8,128)}, bf16[8,128,1024]{2,...) custom-call(s32[1,2048]{1,0:T(1,128)} %seg_ref.3, ...), custom_call_target="tpu_custom_call" | custom-call | flops 35000000512 | bytes 110100480 | tf_op jit(solution)/shard_map/turning/pallas_call | solution.py:1763
  172.3 74.2 %finish.1 = (bf16[128,1024]{1,0:T(8,128)(2,1)}, f32[128,1024]{1,0:T(8,128)}, bf16[1024,384]{1,0:T(8,128)(2,1)}, bf16[1024,128]{1,0:T(8,128)(2,1)}, bf16[8,2,32,7...) custom-call(bf16[32,64,1024]{2,1,0:T(8,128)(2,1)} %get-tuple-element.70.part, ...), custom_call_target="tpu_custom_call" | custom-call | flops 60000002048 | bytes 188743680 | tf_op jit(solution)/shard_map/finish/pallas_call | solution.py:771
  246.5 0.0 copy-start.1
  246.5 30.3 %owners.1 = (bf16[32,32,384]{2,1,0:T(8,128)(2,1)}, bf16[32,32,128]{2,1,0:T(8,128)(2,1)}, bf16[8,1,32,768]{3,2,1,0:T(8,128)(2,1)}) custom-call(bf16[1024,384]{1,0:T(8,128)(2,1)} %get-tuple-element.82.refs_0_, bf16[1024,128]{1,0:T(8,128)(2,1)} %get-tuple-element.83.refs_1_, bf16[1,8,32,768]{3,2,1,0:T(8,128)(2,1)} %bitcast.35), custom_call_target="tpu_custom_call" | custom-call | flops 20000000000 | bytes 62914560 | tf_op jit(solution)/shard_map/owners/pallas_call | solution.py:312
  276.8 0.0 copy-start
  276.8 4.3 %assemble.1 = (f32[32,1024]{1,0:T(8,128)}, f32[32,512]{1,0:T(8,128)}, f32[32,512]{1,0:T(8,128)}, f32[32,1024]{1,0:T(8,128)}, f32[16,32]{1,0:T(8,128)}, /*index=5...) custom-call(bf16[32,32,384]{2,1,0:T(8,128)(2,1)} %get-tuple-element.85.refs_0_, ...), custom_call_target="tpu_custom_call" | custom-call | tf_op jit(solution)/shard_map/assemble/pallas_call | solution.py:1909
  281.1 0.0 copy-done.1
  281.1 0.7 copy.28
  281.8 0.0 copy-done
  281.8 0.8 copy.29
  (2 shorter events, 0.0 us)
Async XLA Ops:
  246.5 34.6 %copy-start.1 = (bf16[128,1024]{1,0:T(8,128)(2,1)S(1)}, bf16[128,1024]{1,0:T(8,128)(2,1)}, u32[]{:S(2)}) copy-start(bf16[128,1024]{1,0:T(8,128)(2,1)} %get-tuple-element.80) | copy-start | bytes 786436
  276.8 5.0 %copy-start = (f32[128,1024]{1,0:T(8,128)S(1)}, f32[128,1024]{1,0:T(8,128)}, u32[]{:S(2)}) copy-start(f32[128,1024]{1,0:T(8,128)} %get-tuple-element.81) | copy-start | bytes 1572868

commit v6 on v5

--- a/solution.py
+++ b/solution.py
@@ -1589,8 +1589,7 @@
     for copy in z_loads:
         copy.wait()
     if outers > 2:
-        for halving in rest:
-            halving.start(0)
+        rest[0].start(0)
     if far_first(outers):
         za_send = remote(za_ref.at[:, 1 - at.y], za_in, zas, zar, at.beside)
         za_send.start()
@@ -1641,6 +1640,9 @@
     for slot in range(3):
         second[slot].wait_recv()
         hidden_sum = hidden_sum + far_in[slot].astype(F32)
+    if outers > 2:
+        for halving in rest[1:]:
+            halving.start(0)
     for copy in [first] + second:
         copy.wait_send()
     small = small_ref[...]

time: 283 us -> 277 us (0.979)
  Pallas kernels: 276 us -> 271 us
    pallas_call x1, Pallas kernels: 50.8 us -> 46.2 us  [turning(): comm_call(functools.partial(turning_kernel, outers), [shape((count, D), F...]
where the time goes in v6:
time: 277 us
  Pallas kernels  271 us (98%)
  local copies, waits for them, and re-layouts  3.04 us (1%)
    pallas_call x1, Pallas kernels, opening(): comm_call(functools.partial(opening_kernel, outers), [shape((D, wide), BF...  117 us
    pallas_call x1, Pallas kernels, finish(): comm_call(functools.partial(finish_kernel, outers), [shape((count, D), BF...  72.6 us
    pallas_call x1, Pallas kernels, turning(): comm_call(functools.partial(turning_kernel, outers), [shape((count, D), F...  46.2 us
    pallas_call x1, Pallas kernels, owners(): comm_call(functools.partial(owners_kernel, devices, count, near_count), s...  31 us

profile of v6, /device:TPU:0, one launch (start us, length us, event | category | flops | bytes accessed | tf_op | source)
XLA Modules:
  0.0 277.1 jit_solution(5741499777163568021)
XLA Ops:
  0.6 0.1 add_multiply_fusion
  0.7 0.1 add_convert_fusion
  0.8 0.1 convert_element_type.11
  0.9 0.1 pad.13.clone
  1.0 0.7 broadcast_in_dim.6
  1.7 0.7 broadcast_in_dim.14
  2.3 1.4 maximum_maximum_fusion.small
  3.8 0.3 fusion
  4.1 0.8 pad_maximum_fusion
  4.9 116.6 %opening.1 = (bf16[1024,2048]{1,0:T(8,128)(2,1)}, bf16[1024,1024]{1,0:T(8,128)(2,1)}, bf16[32,1024]{1,0:T(8,128)(2,1)}, bf16[128,1024]{1,0:T(8,128)(2,1)}, bf16[...) custom-call(s32[1,2048]{1,0:T(1,128)} %seg_ref.3, ...), custom_call_target="tpu_custom_call" | custom-call | flops 99999997952 | bytes 314572800 | tf_op jit(solution)/shard_map/opening/pallas_call | solution.py:1390
  121.5 46.2 %turning.1 = (f32[128,1024]{1,0:T(8,128)}, bf16[128,1024]{1,0:T(8,128)(2,1)}, bf16[128,1024]{1,0:T(8,128)(2,1)}, f32[32,1024]{1,0:T(8,128)}, bf16[8,128,1024]{2,...) custom-call(s32[1,2048]{1,0:T(1,128)} %seg_ref.3, ...), custom_call_target="tpu_custom_call" | custom-call | flops 35000000512 | bytes 110100480 | tf_op jit(solution)/shard_map/turning/pallas_call | solution.py:1765
  167.7 72.6 %finish.1 = (bf16[128,1024]{1,0:T(8,128)(2,1)}, f32[128,1024]{1,0:T(8,128)}, bf16[1024,384]{1,0:T(8,128)(2,1)}, bf16[1024,128]{1,0:T(8,128)(2,1)}, bf16[8,2,32,7...) custom-call(bf16[32,64,1024]{2,1,0:T(8,128)(2,1)} %get-tuple-element.70.part, ...), custom_call_target="tpu_custom_call" | custom-call | flops 60000002048 | bytes 188743680 | tf_op jit(solution)/shard_map/finish/pallas_call | solution.py:771
  240.2 0.0 copy-start.1
  240.2 31.0 %owners.1 = (bf16[32,32,384]{2,1,0:T(8,128)(2,1)}, bf16[32,32,128]{2,1,0:T(8,128)(2,1)}, bf16[8,1,32,768]{3,2,1,0:T(8,128)(2,1)}) custom-call(bf16[1024,384]{1,0:T(8,128)(2,1)} %get-tuple-element.82.refs_0_, bf16[1024,128]{1,0:T(8,128)(2,1)} %get-tuple-element.83.refs_1_, bf16[1,8,32,768]{3,2,1,0:T(8,128)(2,1)} %bitcast.35), custom_call_target="tpu_custom_call" | custom-call | flops 20000000000 | bytes 62914560 | tf_op jit(solution)/shard_map/owners/pallas_call | solution.py:312
  271.3 0.0 copy-start
  271.3 4.3 %assemble.1 = (f32[32,1024]{1,0:T(8,128)}, f32[32,512]{1,0:T(8,128)}, f32[32,512]{1,0:T(8,128)}, f32[32,1024]{1,0:T(8,128)}, f32[16,32]{1,0:T(8,128)}, /*index=5...) custom-call(bf16[32,32,384]{2,1,0:T(8,128)(2,1)} %get-tuple-element.85.refs_0_, ...), custom_call_target="tpu_custom_call" | custom-call | tf_op jit(solution)/shard_map/assemble/pallas_call | solution.py:1911
  275.6 0.0 copy-done.1
  275.6 0.7 copy.28
  276.3 0.0 copy-done
  276.3 0.8 copy.29
  (2 shorter events, 0.0 us)
Async XLA Ops:
  240.2 35.4 %copy-start.1 = (bf16[128,1024]{1,0:T(8,128)(2,1)S(1)}, bf16[128,1024]{1,0:T(8,128)(2,1)}, u32[]{:S(2)}) copy-start(bf16[128,1024]{1,0:T(8,128)(2,1)} %get-tuple-element.80) | copy-start | bytes 786436
  271.3 5.0 %copy-start = (f32[128,1024]{1,0:T(8,128)S(1)}, f32[128,1024]{1,0:T(8,128)}, u32[]{:S(2)}) copy-start(f32[128,1024]{1,0:T(8,128)} %get-tuple-element.81) | copy-start | bytes 1572868

commit v7 on v6

--- a/solution.py
+++ b/solution.py
@@ -268,8 +268,6 @@
             copy_of(k, r).start()
         return carry
 
-    lax.fori_loop(1, devices, start, 0)
-
     near_copies = []
     for k in range(near_count):
         for slot, bits in enumerate(OTHERS):
@@ -279,6 +277,8 @@
             )
             copy.start()
             near_copies.append(copy)
+    lax.fori_loop(1, devices, start, 0)
+
     keeps = []
     for k in range(count):
         keep = pltpu.make_async_copy(rows_of(parts[k], me), outs[k].at[me], local.at[k])

time: 277 us -> 276 us (level)
  Pallas kernels: 271 us -> 268 us
where the time goes in v7:
time: 276 us; the launch traced here: 275 us
  Pallas kernels  268 us (97%)
  local copies, waits for them, and re-layouts  3.04 us (1%)
    pallas_call x1, Pallas kernels, opening(): comm_call(functools.partial(opening_kernel, outers), [shape((D, wide), BF...  117 us
    pallas_call x1, Pallas kernels, finish(): comm_call(functools.partial(finish_kernel, outers), [shape((count, D), BF...  72.6 us
    pallas_call x1, Pallas kernels, turning(): comm_call(functools.partial(turning_kernel, outers), [shape((count, D), F...  46.2 us
    pallas_call x1, Pallas kernels, owners(): comm_call(functools.partial(owners_kernel, devices, count, near_count), s...  28.8 us

profile of v7, /device:TPU:0, one launch (start us, length us, event | category | flops | bytes accessed | tf_op | source)
XLA Modules:
  0.0 274.8 jit_solution(11852839448859003206)
XLA Ops:
  0.6 0.1 add_multiply_fusion
  0.7 0.1 add_convert_fusion
  0.8 0.1 convert_element_type.11
  0.9 0.1 pad.13.clone
  1.0 0.7 broadcast_in_dim.6
  1.7 0.7 broadcast_in_dim.14
  2.3 1.4 maximum_maximum_fusion.small
  3.8 0.3 fusion
  4.1 0.8 pad_maximum_fusion
  4.9 116.6 %opening.1 = (bf16[1024,2048]{1,0:T(8,128)(2,1)}, bf16[1024,1024]{1,0:T(8,128)(2,1)}, bf16[32,1024]{1,0:T(8,128)(2,1)}, bf16[128,1024]{1,0:T(8,128)(2,1)}, bf16[...) custom-call(s32[1,2048]{1,0:T(1,128)} %seg_ref.3, ...), custom_call_target="tpu_custom_call" | custom-call | flops 99999997952 | bytes 314572800 | tf_op jit(solution)/shard_map/opening/pallas_call | solution.py:1390
  121.5 46.2 %turning.1 = (f32[128,1024]{1,0:T(8,128)}, bf16[128,1024]{1,0:T(8,128)(2,1)}, bf16[128,1024]{1,0:T(8,128)(2,1)}, f32[32,1024]{1,0:T(8,128)}, bf16[8,128,1024]{2,...) custom-call(s32[1,2048]{1,0:T(1,128)} %seg_ref.3, ...), custom_call_target="tpu_custom_call" | custom-call | flops 35000000512 | bytes 110100480 | tf_op jit(solution)/shard_map/turning/pallas_call | solution.py:1765
  167.7 72.6 %finish.1 = (bf16[128,1024]{1,0:T(8,128)(2,1)}, f32[128,1024]{1,0:T(8,128)}, bf16[1024,384]{1,0:T(8,128)(2,1)}, bf16[1024,128]{1,0:T(8,128)(2,1)}, bf16[8,2,32,7...) custom-call(bf16[32,64,1024]{2,1,0:T(8,128)(2,1)} %get-tuple-element.70.part, ...), custom_call_target="tpu_custom_call" | custom-call | flops 60000002048 | bytes 188743680 | tf_op jit(solution)/shard_map/finish/pallas_call | solution.py:771
  240.2 0.0 copy-start.1
  240.2 28.8 %owners.1 = (bf16[32,32,384]{2,1,0:T(8,128)(2,1)}, bf16[32,32,128]{2,1,0:T(8,128)(2,1)}, bf16[8,1,32,768]{3,2,1,0:T(8,128)(2,1)}) custom-call(bf16[1024,384]{1,0:T(8,128)(2,1)} %get-tuple-element.82.refs_0_, bf16[1024,128]{1,0:T(8,128)(2,1)} %get-tuple-element.83.refs_1_, bf16[1,8,32,768]{3,2,1,0:T(8,128)(2,1)} %bitcast.35), custom_call_target="tpu_custom_call" | custom-call | flops 20000000000 | bytes 62914560 | tf_op jit(solution)/shard_map/owners/pallas_call | solution.py:312
  269.0 0.0 copy-start
  269.0 4.3 %assemble.1 = (f32[32,1024]{1,0:T(8,128)}, f32[32,512]{1,0:T(8,128)}, f32[32,512]{1,0:T(8,128)}, f32[32,1024]{1,0:T(8,128)}, f32[16,32]{1,0:T(8,128)}, /*index=5...) custom-call(bf16[32,32,384]{2,1,0:T(8,128)(2,1)} %get-tuple-element.85.refs_0_, ...), custom_call_target="tpu_custom_call" | custom-call | tf_op jit(solution)/shard_map/assemble/pallas_call | solution.py:1911
  273.3 0.0 copy-done.1
  273.3 0.7 copy.28
  274.0 0.0 copy-done
  274.0 0.8 copy.29
  (2 shorter events, 0.0 us)
Async XLA Ops:
  240.2 33.1 %copy-start.1 = (bf16[128,1024]{1,0:T(8,128)(2,1)S(1)}, bf16[128,1024]{1,0:T(8,128)(2,1)}, u32[]{:S(2)}) copy-start(bf16[128,1024]{1,0:T(8,128)(2,1)} %get-tuple-element.80) | copy-start | bytes 786436
  269.0 5.0 %copy-start = (f32[128,1024]{1,0:T(8,128)S(1)}, f32[128,1024]{1,0:T(8,128)}, u32[]{:S(2)}) copy-start(f32[128,1024]{1,0:T(8,128)} %get-tuple-element.81) | copy-start | bytes 1572868
